TPU v7x, 256 devices: a whole 4x4x8 slice. The times are simulated.
256 devices in a mesh: ctx: 64 (over z, y, x_hi), head: 4 (over x_lo, core).
Axes of the slice: x: 4 (x_hi: 2, x_lo: 2; x = x_hi * 2 + x_lo), y: 4, z: 8, core: 2. Of those that a mesh axis runs over, the one named last changes fastest.
Arguments:
- prompt_keys: bfloat16 [16384, 8, 128], P('ctx', 'head'), may hold values from -12 to 12
- prompt_values: bfloat16 [16384, 8, 128], P('ctx', 'head'), may hold values from -6 to 6
- prompt_mask: int32 [16384], P('ctx'), may hold values from 0 to 1
- response_queries: bfloat16 [512, 2, 40, 128], P(('ctx', 'head')), may hold values from -16 to 16
- response_keys: bfloat16 [512, 2, 8, 128], P(('ctx', 'head')), may hold values from -8 to 8
- response_values: bfloat16 [512, 2, 8, 128], P(('ctx', 'head')), may hold values from -6 to 6
- resp_lengths: int32 [2], replicated, may hold values from 256 to 512
- prompt_reach: int32 [2], replicated, may hold values from 8192 to 16384
Outputs:
- attended: bfloat16 [512, 2, 40, 128], P(('ctx', 'head'))
All inputs are finite; a program needn't handle non-finite values.
Results may differ from a plain program's by a relative error of at most 0.0031.
Values may be sent and summed in bfloat16 or wider, within the bound.
No kernel may reach another device: no remote copies, remote signals or barrier semaphores. Data moves between devices by JAX's collectives and lax.ppermute only.
A program may use at most 64 MiB of HBM per device.

v0:
```python
import math

import jax
import jax.numpy as jnp
from jax import lax
from jax.sharding import PartitionSpec as P

lowest = -1e30


def grouped(query_rows, group_count):
    return query_rows.reshape(
        query_rows.shape[0],
        query_rows.shape[1],
        group_count,
        query_rows.shape[2] // group_count,
        query_rows.shape[3],
    )


def score_block(query_rows, key_rows, mask_rows, first_place, prompt_reach, score_scale):
    scores = (
        jnp.einsum("trgjd,pgd->trgjp", query_rows, key_rows, preferred_element_type=jnp.float32)
        * score_scale
    )
    key_places = first_place + jnp.arange(key_rows.shape[0], dtype=jnp.int32)
    visible = (mask_rows[None, :] == 1) & (key_places[None, :] < prompt_reach[:, None])
    return jnp.where(visible[None, :, None, None, :], scores, lowest)


def prompt_top(query_rows, key_rows, mask_rows, first_place, prompt_reach, score_scale):
    key_count = key_rows.shape[0]
    key_block = math.gcd(key_count, 512)
    block_count = key_count // key_block

    def visit_block(highest, block_item):
        block_index, key_part, mask_part = block_item
        scores = score_block(
            query_rows,
            key_part,
            mask_part,
            first_place + block_index * key_block,
            prompt_reach,
            score_scale,
        )
        return (jnp.maximum(highest, jnp.max(scores, axis=-1)), None)

    initial = jnp.full(query_rows.shape[:4], lowest, jnp.float32)
    items = (
        jnp.arange(block_count, dtype=jnp.int32),
        key_rows.reshape((block_count, key_block) + key_rows.shape[1:]),
        mask_rows.reshape(block_count, key_block),
    )
    highest, unused = lax.scan(visit_block, initial, items)
    return highest


def prompt_sums(
    query_rows, key_rows, value_rows, mask_rows, first_place, prompt_reach, score_scale, top_rows
):
    key_count = key_rows.shape[0]
    key_block = math.gcd(key_count, 512)
    block_count = key_count // key_block

    def visit_block(running, block_item):
        block_index, key_part, value_part, mask_part = block_item
        scores = score_block(
            query_rows,
            key_part,
            mask_part,
            first_place + block_index * key_block,
            prompt_reach,
            score_scale,
        )
        weights = jnp.exp(scores - top_rows[..., None])
        rounded = weights.astype(jnp.bfloat16)
        more_sums = jnp.einsum(
            "trgjp,pgd->trgjd", rounded, value_part, preferred_element_type=jnp.float32
        )
        return ((running[0] + jnp.sum(weights, axis=-1), running[1] + more_sums), None)

    initial = (jnp.zeros(top_rows.shape, jnp.float32), jnp.zeros(query_rows.shape, jnp.float32))
    items = (
        jnp.arange(block_count, dtype=jnp.int32),
        key_rows.reshape((block_count, key_block) + key_rows.shape[1:]),
        value_rows.reshape((block_count, key_block) + value_rows.shape[1:]),
        mask_rows.reshape(block_count, key_block),
    )
    running, unused = lax.scan(visit_block, initial, items)
    return running


def rows_top(query_rows, key_rows, mask_rows, first_place, prompt_reach, score_scale):
    row_count = query_rows.shape[0]
    row_block = math.gcd(row_count, 32)
    stacked = query_rows.reshape((row_count // row_block, row_block) + query_rows.shape[1:])
    block_tops = lax.map(
        lambda block_rows: prompt_top(
            block_rows, key_rows, mask_rows, first_place, prompt_reach, score_scale
        ),
        stacked,
    )
    return block_tops.reshape((row_count,) + block_tops.shape[2:])


def rows_sums(
    query_rows, key_rows, value_rows, mask_rows, first_place, prompt_reach, score_scale, top_rows
):
    row_count = query_rows.shape[0]
    row_block = math.gcd(row_count, 32)
    stacked = query_rows.reshape((row_count // row_block, row_block) + query_rows.shape[1:])
    stacked_tops = top_rows.reshape((row_count // row_block, row_block) + top_rows.shape[1:])

    def one_block(block_item):
        return prompt_sums(
            block_item[0],
            key_rows,
            value_rows,
            mask_rows,
            first_place,
            prompt_reach,
            score_scale,
            block_item[1],
        )

    totals, summed = lax.map(one_block, (stacked, stacked_tops))
    return (totals.reshape(top_rows.shape), summed.reshape(query_rows.shape))


def own_scores(query_rows, key_rows, first_row, score_scale):
    scores = (
        jnp.einsum("trgjd,srgd->trgjs", query_rows, key_rows, preferred_element_type=jnp.float32)
        * score_scale
    )
    row_places = first_row + jnp.arange(query_rows.shape[0], dtype=jnp.int32)
    key_places = jnp.arange(key_rows.shape[0], dtype=jnp.int32)
    visible = key_places[None, :] <= row_places[:, None]
    return jnp.where(visible[:, None, None, None, :], scores, lowest)


def per_device(
    prompt_keys,
    prompt_values,
    prompt_mask,
    response_queries,
    response_keys,
    response_values,
    resp_lengths,
    prompt_reach,
):
    queries, own_keys, own_values = (
        lax.all_to_all(response_queries, "head", split_axis=2, concat_axis=0, tiled=True),
        lax.all_to_all(response_keys, "head", split_axis=2, concat_axis=0, tiled=True),
        lax.all_to_all(response_values, "head", split_axis=2, concat_axis=0, tiled=True),
    )
    group_count = own_keys.shape[2]
    score_scale = 1.0 / math.sqrt(queries.shape[3])
    local_rows = grouped(queries, group_count)
    row_count = local_rows.shape[0]
    first_row = lax.axis_index("ctx") * row_count
    all_keys, all_values = (
        lax.all_gather(own_keys, "ctx", axis=0, tiled=True),
        lax.all_gather(own_values, "ctx", axis=0, tiled=True),
    )
    self_scores = own_scores(local_rows, all_keys, first_row, score_scale)
    self_top = jnp.max(self_scores, axis=-1)
    prompt_first = lax.axis_index("ctx") * prompt_keys.shape[0]
    shard_piece = lax.all_gather(local_rows, "ctx", axis=0, tiled=True)
    gathered_tops = rows_top(
        shard_piece, prompt_keys, prompt_mask, prompt_first, prompt_reach, score_scale
    )
    own_part = lax.dynamic_slice_in_dim(gathered_tops, first_row, row_count, 0)
    gathered_tops = lax.dynamic_update_slice_in_dim(
        gathered_tops, jnp.maximum(own_part, self_top), first_row, 0
    )
    global_tops = lax.pmax(gathered_tops, "ctx")
    row_tops = lax.dynamic_slice_in_dim(global_tops, first_row, row_count, 0)
    partial_totals, partial_sums = rows_sums(
        shard_piece,
        prompt_keys,
        prompt_values,
        prompt_mask,
        prompt_first,
        prompt_reach,
        score_scale,
        global_tops,
    )
    whole_totals, whole_sums = lax.psum((partial_totals, partial_sums), "ctx")
    prompt_totals = lax.dynamic_slice_in_dim(whole_totals, first_row, row_count, 0)
    prompt_summed = lax.dynamic_slice_in_dim(whole_sums, first_row, row_count, 0)
    own_weights = jnp.exp(self_scores - row_tops[..., None])
    own_summed = jnp.einsum(
        "trgjs,srgd->trgjd",
        own_weights.astype(jnp.bfloat16),
        all_values,
        preferred_element_type=jnp.float32,
    )
    totals = prompt_totals + jnp.sum(own_weights, axis=-1)
    summed = prompt_summed + own_summed
    live_rows = (first_row + jnp.arange(row_count, dtype=jnp.int32))[:, None] < resp_lengths[
        None, :
    ]
    attended = jnp.where(live_rows[:, :, None, None, None], summed / totals[..., None], 0.0)
    attended = attended.reshape(queries.shape).astype(jnp.bfloat16)
    return lax.all_to_all(attended, "head", split_axis=0, concat_axis=2, tiled=True)


def solution(mesh):
    return jax.shard_map(
        per_device,
        mesh=mesh,
        in_specs=(
            P("ctx", "head", None),
            P("ctx", "head", None),
            P("ctx"),
            P(("ctx", "head"), None, None, None),
            P(("ctx", "head"), None, None, None),
            P(("ctx", "head"), None, None, None),
            P(),
            P(),
        ),
        out_specs=P(("ctx", "head"), None, None, None),
        check_vma=False,
    )
```

profile of v0, /device:TPU:1, one launch (start us, length us, event | category | flops | bytes accessed | tf_op | source)
XLA Modules:
  0.0 1364.2 jit_solution(6537605826266422419)
XLA Ops:
  7.4 8.8 all_to_all.69
  16.8 1.3 copy.83
  18.1 4.0 all-to-all-start.1
  25.2 158.2 %all_gather.10 = bf16[512,2,2,128]{3,0,2,1:T(8,128)(2,1)S(1)} all-gather(bf16[8,2,2,128]{3,0,2,1:T(8,128)(2,1)S(1)} %bitcast.130), channel_id=1, replica_groups=mesh['ctx'=64,'head'=4] {'ctx'}, dimensions={0}, use_global_device_ids=true | all-gather | bytes 532480 | tf_op jit(solution)/shard_map/all_gather | solution.py:162
  183.5 1.7 fusion.29
  185.2 2.5 copy.86
  187.8 19.5 %while.37 = (s32[]{:T(128)}, f32[16,32,2,2,5]{1,0,3,4,2:T(8,128)S(1)}, s32[256]{0:T(256)}, s32[]{:T(128)}, s32[2]{0:T(128)S(1)}, /*index=5*/bf16[16,32,2,2,5,128...) while((s32[]{:T(128)}, f32[16,32,2,2,5]{1,0,3,4,2:T(8,128)S(1)}, ...), condition=%wide.region_2.3_spmd, body=%wide.region_0.0_spmd.sunk | while | flops 42436096 | bytes 318065 | solution.py:97
  209.2 296.8 %pmax.7 = f32[512,2,2,5]{0,2,3,1:T(2,128)S(1)} all-reduce(f32[512,2,2,5]{0,2,3,1:T(2,128)S(1)} %dynamic_update_slice.23), channel_id=1, replica_groups=mesh['ctx'=64,'head'=4] {'ctx'}, use_global_device_ids=true, to_apply=%region_4.5 | all-reduce | flops 10240 | bytes 81920 | tf_op jit(solution)/shard_map/pmax | solution.py:176
  506.1 51.7 %while.38 = (s32[]{:T(128)}, f32[16,32,2,2,5]{1,0,4,3,2:T(8,128)S(1)}, f32[16,32,2,2,5,128]{5,1,0,4,3,2:T(8,128)}, s32[256]{0:T(256)}, s32[]{:T(128)}, /*index=5...) while((s32[]{:T(128)}, ...), condition=%wide.region_7.8_spmd, body=%wide.region_5.7_spmd.sunk | while | flops 84706176 | bytes 2109581 | solution.py:126
  507.0 1.3 fusion.43
  510.2 1.3 fusion.43
  523.1 1.3 fusion.43
  529.5 1.3 fusion.43
  532.8 1.3 fusion.43
  539.2 1.3 fusion.43
  542.5 1.3 fusion.43
  548.9 1.3 fusion.43
  552.1 1.3 fusion.43
  559.1 86.8 %all-to-all-start.2 = ((bf16[2,2,8,128]{3,1,0,2:T(2,128)(2,1)}), bf16[2,2,8,128]{3,1,0,2:T(2,128)(2,1)S(1)}, u32[]{:S(2)}, u32[]{:S(2)}) async-start(bf16[2,2,8,128]{3,1,0,2:T(2,128)(2,1)} %copy.92), calls=%async_computation.2 | async-start | bytes 16384 | tf_op jit(solution)/shard_map/all_to_all | solution.py:154
  646.0 3.4 all-to-all-done.2
  649.4 153.0 %all_gather.11 = bf16[512,2,2,128]{3,0,2,1:T(8,128)(2,1)S(1)} all-gather(bf16[8,2,2,128]{3,0,2,1:T(8,128)(2,1)S(1)} %bitcast.131), channel_id=1, replica_groups=mesh['ctx'=64,'head'=4] {'ctx'}, dimensions={0}, use_global_device_ids=true | all-gather | bytes 532480 | tf_op jit(solution)/shard_map/all_gather | solution.py:163
  802.6 304.5 %psum.15 = f32[512,2,2,5]{0,3,2,1:T(8,128)S(1)} all-reduce(f32[512,2,2,5]{0,3,2,1:T(8,128)S(1)} %reshape.203), channel_id=1, replica_groups=mesh['ctx'=64,'head'=4] {'ctx'}, use_global_device_ids=true, to_apply=%region_9.10 | all-reduce | flops 10240 | bytes 81920 | tf_op jit(solution)/shard_map/psum | solution.py:188
  1107.4 199.6 %all-reduce.2.cloned.1.call-done = f32[512,2,2,5,128]{4,0,3,2,1:T(8,128)} async-done(((f32[512,2,2,5,128]{4,0,3,2,1:T(8,128)}), f32[512,2,2,5,128]{4,0,3,2,1:T(8,128)}) %all-reduce.2.cloned.1.call-update) | async-done | bytes 5242896 | tf_op jit(solution)/shard_map/psum | solution.py:188
  1308.2 48.5 %all_to_all.70 = bf16[8,2,10,128]{3,1,2,0:T(2,128)(2,1)S(1)} all-to-all(bf16[8,2,10,128]{3,1,2,0:T(2,128)(2,1)S(1)} %copy.96), channel_id=1, replica_groups=mesh['ctx'=64,'head'=4] {'head'}, dimensions={0} | all-to-all | bytes 81920 | tf_op jit(solution)/shard_map/all_to_all | solution.py:205
  (310 shorter events, 68.0 us)
Async XLA Ops:
  6.5 181.2 %copy-start.1 = (s32[2]{0:T(128)S(1)}, s32[2]{0:T(128)}, u32[]{:S(2)}) copy-start(s32[2]{0:T(128)} %param.19) | copy-start | bytes 28
  6.5 178.7 %all-gather.2.cloned.1.call-start = ((), (), s32[]{:S(2)}) async-start(), calls=%async_computation.4 | async-start | bytes 2662400 | tf_op jit(solution)/shard_map/all_gather | solution.py:168
  18.1 7.1 all-to-all-start.1
  22.1 1284.9 %all-reduce.2.cloned.1.call-start = ((), (), s32[]{:S(2)}) async-start(), calls=%async_computation.5 | async-start | bytes 10485760 | tf_op jit(solution)/shard_map/psum | solution.py:188
  22.1 3.1 copy-start.3
  207.3 0.6 copy-start
  557.8 0.7 copy-start.2
  557.8 88.1 %copy-start.4 = (s32[8]{0:T(128)S(1)}, s32[8]{0:T(128)}, u32[]{:S(2)}) copy-start(s32[8]{0:T(128)} %copy-done.3) | copy-start | bytes 100
  557.8 88.1 %copy-start.5 = (s32[2]{0:T(128)S(1)}, s32[2]{0:T(128)}, u32[]{:S(2)}) copy-start(s32[2]{0:T(128)} %param.18) | copy-start | bytes 28
  559.1 90.3 %all-to-all-start.2 = ((bf16[2,2,8,128]{3,1,0,2:T(2,128)(2,1)}), bf16[2,2,8,128]{3,1,0,2:T(2,128)(2,1)S(1)}, u32[]{:S(2)}, u32[]{:S(2)}) async-start(bf16[2,2,8,128]{3,1,0,2:T(2,128)(2,1)} %copy.92), calls=%async_computation.2 | async-start | bytes 16384 | tf_op jit(solution)/shard_map/all_to_all | solution.py:154
Sparse Core Ops, SparseCore 0:
  16.9 113.1 all-gather.1
  558.0 748.9 all-reduce.1
where the time goes:
time: 1370 us; the launch traced here: 1360 us
  blocking collectives  970 us (71%)
  waiting for transfers between devices  204 us (15%)
  starting transfers between devices  90.8 us (7%)
  matrix products  32.6 us (2%)
  local copies, waits for them, and re-layouts  25.7 us (2%)
  other arithmetic  25.7 us (2%)
    psum x1, blocking collectives, per_device(): whole_totals, whole_sums = lax.psum((partial_totals, partial_sums), 'ctx')  305 us
    pmax x1, blocking collectives, per_device(): global_tops = lax.pmax(gathered_tops, 'ctx')  297 us
    psum x1, waiting for transfers between devices, per_device(): whole_totals, whole_sums = lax.psum((partial_totals, partial_sums), 'ctx')  200 us
    all_gather x1, blocking collectives, per_device(): lax.all_gather(own_keys, 'ctx', axis=0, tiled=True)  158 us
    all_gather x1, blocking collectives, per_device(): lax.all_gather(own_values, 'ctx', axis=0, tiled=True)  153 us
    all_to_all x1, starting transfers between devices, per_device(): lax.all_to_all(response_values, 'head', split_axis=2, concat_axis=0, tile...  86.8 us
    all_to_all x1, blocking collectives, per_device(): lax.all_to_all(attended, 'head', split_axis=0, concat_axis=2, tiled=True)  48.5 us
  transfers between devices with their start and end apart: 4, of which 3 were waited for; matrix products, arithmetic and copies ran while one was open for 0% of the time, Pallas kernels for 0%

commit v1 on v0

v1 whole, which is shorter than its diff:
```python
import functools
import math

import jax
import jax.numpy as jnp
from jax import lax
from jax.experimental import pallas as pl
from jax.experimental.pallas import tpu as pltpu
from jax.sharding import Mesh, PartitionSpec as P

Z, Y, XH, XL, C = 8, 4, 2, 2, 2
PLANE = Y * XH * XL * C
HOLD = Y * XH
T, R, G, J, D = 2, 2, 2, 5, 128
LIVE = R * T * J
ROWS = 24
OWN = Z * PLANE
PROMPT_DEV = 256
LOWEST = -1e30
LOG2E = math.log2(math.e)
F32 = jnp.float32
BF16 = jnp.bfloat16


def three_parts(x):
    hi = x.astype(BF16).astype(F32)
    mid = (x - hi).astype(BF16).astype(F32)
    lo = (x - hi - mid).astype(BF16).astype(F32)
    return hi, mid, lo


def attend_kernel(info_ref, q_ref, kv_ref, own_ref, out_ref, bias_ref):
    z = info_ref[0]
    hold = info_ref[1]
    own_g = info_ref[2]
    own_r = info_ref[3]
    own_t = info_ref[4]
    scale = LOG2E / math.sqrt(D)
    lane = lax.broadcasted_iota(jnp.int32, (1, D), 1)
    for zz in range(Z):
        for i in range(PROMPT_DEV // D):
            place = (zz * HOLD + hold) * PROMPT_DEV + i * D + lane
            mask = kv_ref[zz, 1024:1040, :].astype(F32)[i : i + 1, :]
            at = zz * PROMPT_DEV + i * D
            for r in range(R):
                seen = (mask > 0.5) & (place < info_ref[5 + r])
                bias_ref[r : r + 1, at : at + D] = jnp.where(seen, 0.0, LOWEST)
    own_keys = own_ref[:, :PLANE, :].reshape(OWN, D)
    own_values = own_ref[:, PLANE:, :].reshape(OWN, D)
    sources = 16
    rows = sources * ROWS
    within = lax.broadcasted_iota(jnp.int32, (sources, ROWS, 1), 1).reshape(rows, 1)
    source = lax.broadcasted_iota(jnp.int32, (sources, ROWS, 1), 0).reshape(rows, 1)
    is_r1 = within >= T * J
    in_r = jnp.where(is_r1, within - T * J, within)
    token = jnp.where(in_r >= J, 1, 0)
    row_r = jnp.where(is_r1, 1, 0)
    own_place = 2 * lax.broadcasted_iota(jnp.int32, (1, OWN), 1) + own_t
    lanes = lax.broadcasted_iota(jnp.int32, (rows, D), 1)
    for tile in range(PLANE // sources):
        row_token = 2 * (z * PLANE + tile * sources + source) + token
        stats = jnp.zeros((rows, D), F32)
        for g in range(G):
            q = q_ref[tile * sources : (tile + 1) * sources, g].astype(F32)
            q = q.reshape(rows, D).astype(BF16)
            keys = kv_ref[:, g * 512 : g * 512 + 256, :].reshape(Z * PROMPT_DEV, D)
            values = kv_ref[:, g * 512 + 256 : g * 512 + 512, :].reshape(Z * PROMPT_DEV, D)
            dims = (((1,), (1,)), ((), ()))
            s = lax.dot_general(q, keys, dims, preferred_element_type=F32) * scale
            s = s + jnp.where(is_r1, bias_ref[1:2, :], bias_ref[0:1, :])
            so = lax.dot_general(q, own_keys, dims, preferred_element_type=F32) * scale
            own_row = jnp.where((row_r == own_r) & (own_g == g), row_token, -1)
            so = jnp.where(own_place <= own_row, so, LOWEST)
            top = jnp.maximum(
                jnp.max(s, axis=1, keepdims=True), jnp.max(so, axis=1, keepdims=True)
            )
            p = jnp.exp2(s - top)
            po = jnp.exp2(so - top)
            total = jnp.sum(p, axis=1, keepdims=True) + jnp.sum(po, axis=1, keepdims=True)
            o = jnp.dot(p.astype(BF16), values, preferred_element_type=F32)
            o = o + jnp.dot(po.astype(BF16), own_values, preferred_element_type=F32)
            o = o / total
            out_ref[tile * sources : (tile + 1) * sources, g * ROWS : (g + 1) * ROWS, :] = (
                o.astype(BF16).reshape(sources, ROWS, D)
            )
            for k, part in enumerate(three_parts(top + jnp.log2(total))):
                stats = jnp.where(lanes == g * 3 + k, part, stats)
        out_ref[tile * sources : (tile + 1) * sources, G * ROWS :, :] = stats.astype(BF16).reshape(
            sources, ROWS, D
        )


def combine_kernel(in_ref, out_ref):
    for h in range(XL * C):
        part = in_ref[:, h].astype(F32)
        for g in range(G):
            stats = part[:, G * ROWS :, :]
            lse = stats[:, :, 3 * g : 3 * g + 1] + stats[:, :, 3 * g + 1 : 3 * g + 2]
            lse = lse + stats[:, :, 3 * g + 2 : 3 * g + 3]
            top = jnp.max(lse, axis=0, keepdims=True)
            w = jnp.exp2(lse - top)
            o = jnp.sum(part[:, g * ROWS : (g + 1) * ROWS, :] * w, axis=0)
            out_ref[h, g] = o / jnp.sum(w, axis=0)


def per_device(
    prompt_keys,
    prompt_values,
    prompt_mask,
    response_queries,
    response_keys,
    response_values,
    resp_lengths,
    prompt_reach,
):
    plane = ("y", "xh", "xl", "c")
    z = lax.axis_index("z")
    y = lax.axis_index("y")
    xh = lax.axis_index("xh")
    hold = y * XH + xh
    kv = jnp.stack([prompt_keys, prompt_values]).transpose(2, 0, 1, 3).reshape(1024, D)
    mask_rows = jnp.pad(prompt_mask.astype(BF16).reshape(2, D), ((0, 14), (0, 0)))
    kv = jnp.concatenate([kv, mask_rows], axis=0)
    kv = lax.all_gather(kv, "z", axis=0, tiled=False)
    heads = XL * C
    q = response_queries.reshape(T, R, heads, G, J, D).transpose(2, 3, 1, 0, 4, 5)
    q = q.reshape(heads, G, LIVE, D)
    own = jnp.stack([response_keys, response_values]).reshape(2, T, R, heads, G, D)
    own = own.transpose(1, 2, 4, 3, 0, 5).reshape(HOLD, heads, 2, D)
    zeros = jnp.zeros((HOLD, heads, 2, D), BF16)
    first = jnp.concatenate(
        [jnp.broadcast_to(q[None, :, 0], (HOLD, heads, LIVE, D)), own, zeros], axis=2
    )
    second = jnp.concatenate(
        [jnp.broadcast_to(q[None, :, 1], (HOLD, heads, LIVE, D)), zeros, zeros], axis=2
    )
    message = jnp.stack([first, second], axis=2).reshape(PLANE, G * ROWS, D)
    rows = lax.all_to_all(message, plane, 0, 0, tiled=True)
    own_rows = jnp.concatenate([rows[:, LIVE], rows[:, LIVE + 1]], axis=0)
    own_rows = jnp.broadcast_to(own_rows[None], (Z, 2 * PLANE, D))
    own_rows = lax.all_to_all(own_rows, "z", 0, 0, tiled=True)
    info = jnp.stack(
        [z, hold, hold % 2, (hold // 2) % 2, hold // 4, prompt_reach[0], prompt_reach[1]]
    ).astype(jnp.int32)
    vmem = pl.BlockSpec(memory_space=pltpu.VMEM)
    partial = pl.pallas_call(
        attend_kernel,
        out_shape=jax.ShapeDtypeStruct((PLANE, (G + 1) * ROWS, D), BF16),
        in_specs=[pl.BlockSpec(memory_space=pltpu.SMEM), vmem, vmem, vmem],
        out_specs=vmem,
        scratch_shapes=[pltpu.VMEM((8, Z * PROMPT_DEV), F32)],
        compiler_params=pltpu.CompilerParams(vmem_limit_bytes=40 << 20),
        name="attend",
    )(info, rows.reshape(PLANE, G, ROWS, D), kv, own_rows)
    partial = lax.all_to_all(partial, plane, 0, 0, tiled=True)
    attended = pl.pallas_call(
        combine_kernel,
        out_shape=jax.ShapeDtypeStruct((heads, G, ROWS, D), F32),
        in_specs=[vmem],
        out_specs=vmem,
        name="combine",
    )(partial.reshape(HOLD, heads, (G + 1) * ROWS, D))
    attended = attended[:, :, :LIVE].reshape(heads, G, R, T, J, D).transpose(3, 2, 0, 1, 4, 5)
    first_row = 2 * ((z * HOLD + hold) * heads + lax.axis_index(("xl", "c")))
    live = (first_row + jnp.arange(T, dtype=jnp.int32))[:, None] < resp_lengths[None, :]
    attended = jnp.where(live[:, :, None, None], attended.reshape(T, R, heads * G * J, D), 0.0)
    return attended.astype(BF16)


def solution(mesh):
    fine = Mesh(mesh.devices.reshape(Z, Y, XH, XL, C), ("z", "y", "xh", "xl", "c"))
    ctx, head = ("z", "y", "xh"), ("xl", "c")
    return jax.shard_map(
        per_device,
        mesh=fine,
        in_specs=(
            P(ctx, head, None),
            P(ctx, head, None),
            P(ctx),
            P(ctx + head, None, None, None),
            P(ctx + head, None, None, None),
            P(ctx + head, None, None, None),
            P(),
            P(),
        ),
        out_specs=P(ctx + head, None, None, None),
        check_vma=False,
    )
```

time: 1370 us -> 97.6 us (0.07)
  blocking collectives: 970 us -> 18.6 us
  waiting for transfers between devices: 204 us -> 26.2 us
  starting transfers between devices: 90.8 us -> 19.2 us
  matrix products: 32.6 us -> 0 us
  other arithmetic: 25.7 us -> 2.51 us
  local copies, waits for them, and re-layouts: 25.7 us -> 6.94 us
    all_gather x2 -> x0, blocking collectives: 311 us -> none  [the longest x1 158 us: per_device(): lax.all_gather(own_keys, 'ctx', axis=0, tiled=True)]
    psum x1 -> x0, blocking collectives: 305 us -> none  [per_device(): whole_totals, whole_sums = lax.psum((partial_totals, partial_sums), 'ctx')]
    pmax x1 -> x0, blocking collectives: 297 us -> none  [per_device(): global_tops = lax.pmax(gathered_tops, 'ctx')]
    psum x1 -> x0, waiting for transfers between devices: 200 us -> none  [per_device(): whole_totals, whole_sums = lax.psum((partial_totals, partial_sums), 'ctx')]
    all_to_all x2, starting transfers between devices: 90.8 us -> 19.2 us  [the longest x1 11.1 us: per_device(): partial = lax.all_to_all(partial, plane, 0, 0, tiled=True)]
    all_to_all x2 -> x1, blocking collectives: 57.3 us -> 18.6 us  [per_device(): rows = lax.all_to_all(message, plane, 0, 0, tiled=True)]
    dot_general x50 -> x0, matrix products: 32.6 us -> none  [the longest x32 25.9 us: score_block(): jnp.einsum('trgjd,pgd->trgjp', query_rows, key_rows, preferred_element_ty...]
    eq x32 -> x0, other arithmetic: 21.9 us -> none  [score_block(): mask_rows[None, :] == 1]
  transfers between devices with their start and end apart: 4 -> 3, of which waited for: 3 -> 3; matrix products, arithmetic and copies ran while one was open for 0% -> 3% of each run, Pallas kernels for 0% -> 0%
where the time goes in v1:
time: 97.6 us; the launch traced here: 97.1 us
  waiting for transfers between devices  26.2 us (27%)
  starting transfers between devices  19.2 us (20%)
  blocking collectives  18.6 us (19%)
  between operations  13.6 us (14%)
  Pallas kernels  9.98 us (10%)
  local copies, waits for them, and re-layouts  6.94 us (7%)
  other arithmetic  2.51 us (3%)
    all_to_all x1, blocking collectives, per_device(): rows = lax.all_to_all(message, plane, 0, 0, tiled=True)  18.6 us
    all_to_all x1, waiting for transfers between devices, per_device(): partial = lax.all_to_all(partial, plane, 0, 0, tiled=True)  12.1 us
    all_to_all x1, starting transfers between devices, per_device(): partial = lax.all_to_all(partial, plane, 0, 0, tiled=True)  11.1 us
    all_to_all x1, waiting for transfers between devices, per_device(): own_rows = lax.all_to_all(own_rows, 'z', 0, 0, tiled=True)  10.5 us
    all_to_all x1, starting transfers between devices, per_device(): own_rows = lax.all_to_all(own_rows, 'z', 0, 0, tiled=True)  8.19 us
    pallas_call x1, Pallas kernels, per_device(): pl.pallas_call(attend_kernel, out_shape=jax.ShapeDtypeStruct((PLANE, (G +...  7.49 us
    all_gather x1, waiting for transfers between devices, per_device(): kv = lax.all_gather(kv, 'z', axis=0, tiled=False)  3.57 us
    unnamed x11, local copies, waits for them, and re-layouts  3.25 us
  transfers between devices with their start and end apart: 3, of which 3 were waited for; matrix products, arithmetic and copies ran while one was open for 3% of the time, Pallas kernels for 0%

profile of v1, /device:TPU:1, one launch (start us, length us, event | category | flops | bytes accessed | tf_op | source)
XLA Modules:
  0.0 97.1 jit_solution(16325458149525512234)
XLA Ops:
  6.5 0.7 convert_bitcast_fusion
  7.2 1.0 %copy_bitcast_fusion = (bf16[1,256,2,128]{3,1,0,2:T(8,128)(2,1)S(1)}, bf16[1,256,2,128]{3,1,0,2:T(8,128)(2,1)S(1)}) fusion(bf16[256,2,128]{2,1,0:T(2,128)(2,1)} %param.9, bf16[256,2,128]{2,1,0:T(2,128)(2,1)} %param.8), kind=kLoop, calls=%fused_computation.7 | loop fusion | bytes 524288 | tf_op jit(solution)/shard_map/stack | solution.py:121
  8.3 0.7 fusion.1
  9.0 0.7 pad_maximum_fusion.2
  9.8 0.8 copy.52
  10.7 0.1 fusion.3
  10.8 0.1 pad.16.clone
  11.0 0.1 maximum_bitcast_fusion
  11.1 18.6 %all_to_all.15 = bf16[32,48,128]{2,1,0:T(8,128)(2,1)S(1)} all-to-all(bf16[32,48,128]{2,1,0:T(8,128)(2,1)S(1)} %bitcast.48), channel_id=1, replica_groups=mesh['z'=8,'y'=4,'xh'=2,'xl'=2,'c'=2] {'y','xh','xl','c'}, dimensions={0} | all-to-all | bytes 786432 | tf_op jit(solution)/shard_map/all_to_all | solution.py:138
  29.8 0.7 broadcast_in_dim.44
  30.4 8.2 %all-to-all-start.1 = ((bf16[8,64,128]{2,1,0:T(8,128)(2,1)}), bf16[8,64,128]{2,1,0:T(8,128)(2,1)S(1)}, u32[]{:S(2)}, u32[]{:S(2)}) async-start(bf16[8,64,128]{2,1,0:T(8,128)(2,1)} %broadcast_in_dim.44), calls=%async_computation.1 | async-start | bytes 262144 | tf_op jit(solution)/shard_map/all_to_all | solution.py:141
  38.6 0.1 stack.50.info_ref
  38.7 10.5 %all-to-all-done.1.own_ref = bf16[8,64,128]{2,1,0:T(8,128)(2,1)S(1)} async-done(((bf16[8,64,128]{2,1,0:T(8,128)(2,1)}), bf16[8,64,128]{2,1,0:T(8,128)(2,1)S(1)}, u32[]{:S(2)}, u32[]{:S(2)}) %all-to-all-start.1) | async-done | bytes 131104 | tf_op jit(solution)/shard_map/all_to_all | solution.py:141
  49.2 3.6 %all-gather.3.cloned.1.call-done = bf16[8320,128]{1,0:T(8,128)(2,1)} async-done(((bf16[1040,128]{1,0:T(8,128)(2,1)}), bf16[8320,128]{1,0:T(8,128)(2,1)}) %all-gather.3.cloned.1.call-update) | async-done | bytes 2129936 | tf_op jit(solution)/shard_map/all_gather | solution.py:124
  52.8 1.6 %copy-done = bf16[8320,128]{1,0:T(8,128)(2,1)S(1)} copy-done((bf16[8320,128]{1,0:T(8,128)(2,1)S(1)}, bf16[8320,128]{1,0:T(8,128)(2,1)}, u32[]{:S(2)}) %copy-start) | copy-done | bytes 2129944
  54.4 7.5 %attend.1 = bf16[32,72,128]{2,1,0:T(8,128)(2,1)} custom-call(s32[7]{0:T(128)S(1)} %stack.50.info_ref, bf16[32,2,24,128]{3,2,1,0:T(8,128)(2,1)S(1)} %bitcast.46, bf16[8,1040,128]{2,1,0:T(8,128)(2,1)S(1)} %bitcast.45, bf16[8,64,128]{2,1,0:T(8,128)(2,1)S(1)} %all-to-all-done.1.own_ref), custom_call_target="tpu_custom_call" | custom-call | tf_op jit(solution)/shard_map/attend/pallas_call | solution.py:146
  61.9 11.1 %all-to-all-start.2 = ((bf16[32,72,128]{2,1,0:T(8,128)(2,1)}), bf16[32,72,128]{2,1,0:T(8,128)(2,1)S(1)}, u32[]{:S(2)}, u32[]{:S(2)}) async-start(bf16[32,72,128]{2,1,0:T(8,128)(2,1)} %attend.1), calls=%async_computation.2 | async-start | bytes 1179648 | tf_op jit(solution)/shard_map/all_to_all | solution.py:155
  73.0 0.1 broadcast_compare_fusion
  73.1 12.1 %all-to-all-done.2 = bf16[32,72,128]{2,1,0:T(8,128)(2,1)S(1)} async-done(((bf16[32,72,128]{2,1,0:T(8,128)(2,1)}), bf16[32,72,128]{2,1,0:T(8,128)(2,1)S(1)}, u32[]{:S(2)}, u32[]{:S(2)}) %all-to-all-start.2) | async-done | bytes 589856 | tf_op jit(solution)/shard_map/all_to_all | solution.py:155
  85.2 0.8 copy-done.1
  86.0 2.5 %combine.1 = f32[4,2,24,128]{3,2,1,0:T(8,128)} custom-call(bf16[8,4,72,128]{3,2,1,0:T(8,128)(2,1)} %bitcast.47), custom_call_target="tpu_custom_call" | custom-call | tf_op jit(solution)/shard_map/combine/pallas_call | solution.py:156
  88.5 0.9 slice.27
  89.5 0.1 select_convert_fusion
  89.6 0.6 copy.67
  (27 shorter events, 0.4 us)
Async XLA Ops:
  6.5 46.3 %all-gather.3.cloned.1.call-start = ((), (), s32[]{:S(2)}) async-start(), calls=%async_computation.3 | async-start | bytes 2396160 | tf_op jit(solution)/shard_map/all_gather | solution.py:124
  9.0 29.6 %copy-start.2 = (s32[2]{0:T(128)S(1)}, s32[2]{0:T(128)}, u32[]{:S(2)}) copy-start(s32[2]{0:T(128)} %param.15) | copy-start | bytes 28
  30.4 18.8 %all-to-all-start.1 = ((bf16[8,64,128]{2,1,0:T(8,128)(2,1)}), bf16[8,64,128]{2,1,0:T(8,128)(2,1)S(1)}, u32[]{:S(2)}, u32[]{:S(2)}) async-start(bf16[8,64,128]{2,1,0:T(8,128)(2,1)} %broadcast_in_dim.44), calls=%async_computation.1 | async-start | bytes 262144 | tf_op jit(solution)/shard_map/all_to_all | solution.py:141
  52.8 1.6 %copy-start = (bf16[8320,128]{1,0:T(8,128)(2,1)S(1)}, bf16[8320,128]{1,0:T(8,128)(2,1)}, u32[]{:S(2)}) copy-start(bf16[8320,128]{1,0:T(8,128)(2,1)} %all-gather.3.cloned.1.call-done) | copy-start | bytes 6389764
  54.4 18.6 %copy-start.3 = (s32[2]{0:T(128)S(1)}, s32[2]{0:T(128)}, u32[]{:S(2)}) copy-start(s32[2]{0:T(128)} %param.14) | copy-start | bytes 28
  61.9 23.3 %all-to-all-start.2 = ((bf16[32,72,128]{2,1,0:T(8,128)(2,1)}), bf16[32,72,128]{2,1,0:T(8,128)(2,1)S(1)}, u32[]{:S(2)}, u32[]{:S(2)}) async-start(bf16[32,72,128]{2,1,0:T(8,128)(2,1)} %attend.1), calls=%async_computation.2 | async-start | bytes 1179648 | tf_op jit(solution)/shard_map/all_to_all | solution.py:155
  85.2 0.8 copy-start.1
Sparse Core Ops, SparseCore 0:
  9.1 43.6 all-gather.2

commit v2 on v1

v2 whole, which is shorter than its diff:
```python
import functools
import math

import jax
import jax.numpy as jnp
from jax import lax
from jax.experimental import pallas as pl
from jax.experimental.pallas import tpu as pltpu
from jax.sharding import Mesh, PartitionSpec as P

Z, Y, XH, XL, C = 8, 4, 2, 2, 2
HEADS = XL * C
PLANE = Z * HEADS
HOLD = Y * XH
T, R, G, J, D = 2, 2, 2, 5, 128
LIVE = R * T * J
ROWS = 24
OWN = HOLD * PLANE
BLOCK = 256
SOURCES = 16
TILE = SOURCES * ROWS
TILES = PLANE // SOURCES
LOWEST = -1e30
LOG2E = math.log2(math.e)
F32 = jnp.float32
BF16 = jnp.bfloat16
FIRST = ((0, 0), (3, 0), (1, 0), (2, 0), (0, 1))
SECOND = ((3, 1), (1, 1), (2, 1))
CONTRACT_LAST = (((1,), (1,)), ((), ()))


def three_parts(x):
    hi = x.astype(BF16).astype(F32)
    mid = (x - hi).astype(BF16).astype(F32)
    lo = (x - hi - mid).astype(BF16).astype(F32)
    return hi, mid, lo


def fill_bias(info_ref, kv_refs, offsets, bias_ref):
    z, y, xh = info_ref[0], info_ref[1], info_ref[2]
    lane = lax.broadcasted_iota(jnp.int32, (1, D), 1)
    for b, (kv_ref, (dy, dx)) in enumerate(zip(kv_refs, offsets)):
        ctx = z * HOLD + lax.rem(y + dy, Y) * XH + lax.rem(xh + dx, XH)
        mask = kv_ref[1024:1040, :].astype(F32)
        for i in range(BLOCK // D):
            place = ctx * BLOCK + i * D + lane
            at = b * BLOCK + i * D
            for r in range(R):
                seen = (mask[i : i + 1, :] > 0.5) & (place < info_ref[3 + r])
                bias_ref[r : r + 1, at : at + D] = jnp.where(seen, 0.0, LOWEST)


def row_parts():
    within = lax.broadcasted_iota(jnp.int32, (SOURCES, ROWS, 1), 1).reshape(TILE, 1)
    source = lax.broadcasted_iota(jnp.int32, (SOURCES, ROWS, 1), 0).reshape(TILE, 1)
    return within, source


def tile_queries(q_ref, tile, g):
    q = q_ref[tile * SOURCES : (tile + 1) * SOURCES, g].astype(F32)
    return q.reshape(TILE, D).astype(BF16)


def block_scores(q, kv_refs, g, bias_ref, is_r1):
    scale = LOG2E / math.sqrt(D)
    scores = []
    for b, kv_ref in enumerate(kv_refs):
        keys = kv_ref[g * 2 * BLOCK : g * 2 * BLOCK + BLOCK, :]
        s = lax.dot_general(q, keys, CONTRACT_LAST, preferred_element_type=F32) * scale
        at = slice(b * BLOCK, (b + 1) * BLOCK)
        scores.append(s + jnp.where(is_r1, bias_ref[1:2, at], bias_ref[0:1, at]))
    return scores


def block_values(kv_refs, g):
    return [kv_ref[g * 2 * BLOCK + BLOCK : (g + 1) * 2 * BLOCK, :] for kv_ref in kv_refs]


def weigh(scores, values, top):
    total, summed = 0.0, 0.0
    for s, v in zip(scores, values):
        p = jnp.exp2(s - top)
        total = total + jnp.sum(p, axis=1, keepdims=True)
        summed = summed + jnp.dot(p.astype(BF16), v, preferred_element_type=F32)
    return total, summed


def top_of(scores):
    wide = functools.reduce(jnp.maximum, scores)
    return jnp.max(wide, axis=1, keepdims=True)


def first_kernel(info_ref, q_ref, *refs):
    kv_refs, (acc_ref, stat_ref, bias_ref) = refs[: len(FIRST)], refs[len(FIRST) :]
    fill_bias(info_ref, kv_refs, FIRST, bias_ref)
    within, _ = row_parts()
    lanes = lax.broadcasted_iota(jnp.int32, (TILE, D), 1)
    for tile in range(TILES):
        for g in range(G):
            q = tile_queries(q_ref, tile, g)
            scores = block_scores(q, kv_refs, g, bias_ref, within >= T * J)
            top = top_of(scores)
            total, summed = weigh(scores, block_values(kv_refs, g), top)
            acc_ref[tile, g] = summed
            stat_ref[tile, g] = jnp.where(lanes == 0, top, total)


def second_kernel(info_ref, q_ref, *refs):
    kv_refs, (own_ref, acc_ref, stat_ref, out_ref, bias_ref) = refs[: len(SECOND)], refs[len(SECOND) :]
    z, y, xh = info_ref[0], info_ref[1], info_ref[2]
    fill_bias(info_ref, kv_refs, SECOND, bias_ref)
    own_keys = own_ref[:, :PLANE, :].reshape(OWN, D)
    own_values = own_ref[:, PLANE:, :].reshape(OWN, D)
    within, source = row_parts()
    is_r1 = within >= T * J
    in_r = jnp.where(is_r1, within - T * J, within)
    row_r = jnp.where(is_r1, 1, 0)
    row_t = jnp.where(in_r >= J, 1, 0)
    k = lax.broadcasted_iota(jnp.int32, (1, OWN), 1)
    own_device = ((k >> 2) & (Z - 1)) * HOLD * HEADS + (k >> 5) * HEADS + (k & (HEADS - 1))
    own_place = 2 * own_device + (z >> 2)
    lanes = lax.broadcasted_iota(jnp.int32, (TILE, D), 1)
    for tile in range(TILES):
        from_source = tile * SOURCES + source
        row_device = (from_source >> 2) * HOLD * HEADS + (y * XH + xh) * HEADS + (from_source & (HEADS - 1))
        row_place = 2 * row_device + row_t
        stats = jnp.zeros((TILE, D), F32)
        outs = []
        for g in range(G):
            q = tile_queries(q_ref, tile, g)
            scores = block_scores(q, kv_refs, g, bias_ref, is_r1)
            so = lax.dot_general(q, own_keys, CONTRACT_LAST, preferred_element_type=F32)
            so = so * (LOG2E / math.sqrt(D))
            own_row = jnp.where((row_r == ((z >> 1) & 1)) & ((z & 1) == g), row_place, -1)
            scores.append(jnp.where(own_place <= own_row, so, LOWEST))
            before = stat_ref[tile, g]
            top_before, total_before = before[:, 0:1], before[:, 1:2]
            top = jnp.maximum(top_of(scores), top_before)
            total, summed = weigh(scores, block_values(kv_refs, g) + [own_values], top)
            shrink = jnp.exp2(top_before - top)
            total = total + total_before * shrink
            summed = (summed + acc_ref[tile, g] * shrink) / total
            outs.append(summed.reshape(SOURCES, ROWS, D))
            for i, part in enumerate(three_parts(top + jnp.log2(total))):
                stats = jnp.where(lanes == (g * 3 + i) * LIVE + within, part, stats)
        stats = jnp.where(within < LIVE, stats, 0.0).reshape(SOURCES, ROWS, D)
        stats = jnp.sum(stats, axis=1, keepdims=True)
        spare = lax.broadcasted_iota(jnp.int32, (SOURCES, ROWS, D), 1) == LIVE
        at = slice(tile * SOURCES, (tile + 1) * SOURCES)
        out_ref[at, 0] = jnp.where(spare, stats, outs[0]).astype(BF16)
        out_ref[at, 1] = outs[1].astype(BF16)


def combine_kernel(in_ref, out_ref):
    lane = lax.broadcasted_iota(jnp.int32, (1, ROWS, D), 2)
    row = lax.broadcasted_iota(jnp.int32, (1, ROWS, D), 1)
    for h in range(HEADS):
        parts = [in_ref[:, h, g].astype(F32) for g in range(G)]
        stats = parts[0][:, LIVE : LIVE + 1, :]
        for g in range(G):
            mine = False
            for i in range(3):
                mine = mine | (lane == (g * 3 + i) * LIVE + row)
            mine = mine & (row < LIVE)
            lse = jnp.sum(jnp.where(mine, stats, 0.0), axis=2, keepdims=True)
            top = jnp.max(lse, axis=0, keepdims=True)
            w = jnp.exp2(lse - top)
            out_ref[h, g] = jnp.sum(parts[g] * w, axis=0) / jnp.sum(w, axis=0)


def permute(x, axis, size, shift):
    return lax.ppermute(x, axis, [(i, (i + shift) % size) for i in range(size)])


def per_device(
    prompt_keys,
    prompt_values,
    prompt_mask,
    response_queries,
    response_keys,
    response_values,
    resp_lengths,
    prompt_reach,
):
    plane = ("z", "xl", "c")
    z = lax.axis_index("z")
    y = lax.axis_index("y")
    xh = lax.axis_index("xh")
    q = response_queries.reshape(T, R, HEADS, G, J, D).transpose(2, 3, 1, 0, 4, 5)
    q = q.reshape(HEADS, G, LIVE, D)
    own = jnp.stack([response_keys, response_values]).reshape(2, T, R, HEADS, G, D)
    own = own.transpose(1, 2, 4, 3, 0, 5).reshape(Z, HEADS, 2, D)
    zeros = jnp.zeros((Z, HEADS, 2, D), BF16)
    first = jnp.concatenate(
        [jnp.broadcast_to(q[None, :, 0], (Z, HEADS, LIVE, D)), own, zeros], axis=2
    )
    second = jnp.concatenate(
        [jnp.broadcast_to(q[None, :, 1], (Z, HEADS, LIVE, D)), zeros, zeros], axis=2
    )
    message = jnp.stack([first, second], axis=2).reshape(PLANE, G * ROWS, D)
    rows = lax.all_to_all(message, plane, 0, 0, tiled=True)
    kv = jnp.stack([prompt_keys, prompt_values]).transpose(2, 0, 1, 3).reshape(4 * BLOCK, D)
    mask_rows = jnp.pad(prompt_mask.astype(BF16).reshape(2, D), ((0, 14), (0, 0)))
    kv = jnp.concatenate([kv, mask_rows], axis=0)
    before = permute(kv, "y", Y, 1)
    after = permute(kv, "y", Y, 3)
    far = permute(kv, "y", Y, 2)
    across = permute(kv, "xh", XH, 1)
    rows, before, after, far, across = lax.optimization_barrier((rows, before, after, far, across))
    across_before = permute(across, "y", Y, 1)
    across_after = permute(across, "y", Y, 3)
    across_far = permute(far, "xh", XH, 1)
    own_rows = jnp.concatenate([rows[:, LIVE], rows[:, LIVE + 1]], axis=0)
    own_rows = jnp.broadcast_to(own_rows[None], (HOLD, 2 * PLANE, D))
    own_rows = lax.all_to_all(own_rows, ("y", "xh"), 0, 0, tiled=True)
    info = jnp.stack([z, y, xh, prompt_reach[0], prompt_reach[1]]).astype(jnp.int32)
    smem = pl.BlockSpec(memory_space=pltpu.SMEM)
    vmem = pl.BlockSpec(memory_space=pltpu.VMEM)
    rows = rows.reshape(PLANE, G, ROWS, D)
    pair_flops = 4 * PLANE * G * ROWS * BLOCK * D
    acc, stat = pl.pallas_call(
        first_kernel,
        out_shape=[jax.ShapeDtypeStruct((TILES, G, TILE, D), F32)] * 2,
        in_specs=[smem] + [vmem] * (1 + len(FIRST)),
        out_specs=[vmem] * 2,
        scratch_shapes=[pltpu.VMEM((8, len(FIRST) * BLOCK), F32)],
        compiler_params=pltpu.CompilerParams(vmem_limit_bytes=40 << 20),
        cost_estimate=pl.CostEstimate(
            flops=len(FIRST) * pair_flops, bytes_accessed=3 << 20, transcendentals=len(FIRST) * pair_flops // 512
        ),
        name="attend_first",
    )(info, rows, kv, before, after, far, across)
    partial = pl.pallas_call(
        second_kernel,
        out_shape=jax.ShapeDtypeStruct((PLANE, G, ROWS, D), BF16),
        in_specs=[smem] + [vmem] * (4 + len(SECOND)),
        out_specs=vmem,
        scratch_shapes=[pltpu.VMEM((8, len(SECOND) * BLOCK), F32)],
        compiler_params=pltpu.CompilerParams(vmem_limit_bytes=40 << 20),
        cost_estimate=pl.CostEstimate(
            flops=4 * pair_flops, bytes_accessed=3 << 20, transcendentals=4 * pair_flops // 512
        ),
        name="attend_second",
    )(info, rows, across_before, across_after, across_far, own_rows, acc, stat)
    partial = lax.all_to_all(partial.reshape(PLANE, G * ROWS, D), plane, 0, 0, tiled=True)
    attended = pl.pallas_call(
        combine_kernel,
        out_shape=jax.ShapeDtypeStruct((HEADS, G, ROWS, D), F32),
        in_specs=[vmem],
        out_specs=vmem,
        name="combine",
    )(partial.reshape(Z, HEADS, G, ROWS, D))
    attended = attended[:, :, :LIVE].reshape(HEADS, G, R, T, J, D).transpose(3, 2, 0, 1, 4, 5)
    first_row = T * (((z * Y + y) * XH + xh) * HEADS + lax.axis_index(("xl", "c")))
    live = (first_row + jnp.arange(T, dtype=jnp.int32))[:, None] < resp_lengths[None, :]
    attended = jnp.where(live[:, :, None, None], attended.reshape(T, R, HEADS * G * J, D), 0.0)
    return attended.astype(BF16)


def solution(mesh):
    fine = Mesh(mesh.devices.reshape(Z, Y, XH, XL, C), ("z", "y", "xh", "xl", "c"))
    ctx, head = ("z", "y", "xh"), ("xl", "c")
    return jax.shard_map(
        per_device,
        mesh=fine,
        in_specs=(
            P(ctx, head, None),
            P(ctx, head, None),
            P(ctx),
            P(ctx + head, None, None, None),
            P(ctx + head, None, None, None),
            P(ctx + head, None, None, None),
            P(),
            P(),
        ),
        out_specs=P(ctx + head, None, None, None),
        check_vma=False,
    )
```

time: 97.6 us -> 84 us (0.86)
  blocking collectives: 18.6 us -> 0 us
  starting transfers between devices: 19.2 us -> 37 us
  between operations: 13.6 us -> 0.3 us
  waiting for transfers between devices: 26.2 us -> 20.8 us
  local copies, waits for them, and re-layouts: 6.94 us -> 10.2 us
  Pallas kernels: 9.98 us -> 13 us
    all_to_all x1 -> x0, blocking collectives: 18.6 us -> none  [per_device(): rows = lax.all_to_all(message, plane, 0, 0, tiled=True)]
    ppermute x0 -> x7, starting transfers between devices: none -> 12 us  [permute(): return lax.ppermute(x, axis, [(i, (i + shift) % size) for i in range(size)])]
    all_to_all x2 -> x3, waiting for transfers between devices: 22.6 us -> 13 us  [the longest x1 13 us: per_device(): lax.all_to_all(partial.reshape(PLANE, G * ROWS, D), plane, 0, 0, tiled=True)]
    ppermute x0 -> x7, waiting for transfers between devices: none -> 7.8 us  [permute(): return lax.ppermute(x, axis, [(i, (i + shift) % size) for i in range(size)])]
    all_to_all x2 -> x3, starting transfers between devices: 19.2 us -> 25 us  [the longest x1 11.2 us: per_device(): rows = lax.all_to_all(message, plane, 0, 0, tiled=True)]
    unnamed x11 -> x25, local copies, waits for them, and re-layouts: 3.25 us -> 7.49 us
    all_gather x1 -> x0, waiting for transfers between devices: 3.57 us -> none  [per_device(): kv = lax.all_gather(kv, 'z', axis=0, tiled=False)]
    pallas_call x2 -> x3, Pallas kernels: 9.98 us -> 13 us  [the longest x1 6.6 us: per_device(): pl.pallas_call(second_kernel, out_shape=jax.ShapeDtypeStruct((PLANE, G, R...]
  transfers between devices with their start and end apart: 3 -> 10, of which waited for: 3 -> 3; matrix products, arithmetic and copies ran while one was open for 3% -> 2% of each run, Pallas kernels for 0% -> 5%
where the time goes in v2:
time: 84 us; the launch traced here: 82.9 us
  starting transfers between devices  37 us (44%)
  waiting for transfers between devices  20.8 us (25%)
  Pallas kernels  13 us (15%)
  local copies, waits for them, and re-layouts  10.2 us (12%)
  other arithmetic  1.58 us (2%)
    all_to_all x1, waiting for transfers between devices, per_device(): lax.all_to_all(partial.reshape(PLANE, G * ROWS, D), plane, 0, 0, tiled=True)  13 us
    ppermute x7, starting transfers between devices, permute(): return lax.ppermute(x, axis, [(i, (i + shift) % size) for i in range(size)])  12 us
    all_to_all x1, starting transfers between devices, per_device(): rows = lax.all_to_all(message, plane, 0, 0, tiled=True)  11.2 us
    all_to_all x1, starting transfers between devices, per_device(): lax.all_to_all(partial.reshape(PLANE, G * ROWS, D), plane, 0, 0, tiled=True)  10.3 us
    ppermute x7, waiting for transfers between devices, permute(): return lax.ppermute(x, axis, [(i, (i + shift) % size) for i in range(size)])  7.8 us
    unnamed x25, local copies, waits for them, and re-layouts  7.49 us
    pallas_call x1, Pallas kernels, per_device(): pl.pallas_call(second_kernel, out_shape=jax.ShapeDtypeStruct((PLANE, G, R...  6.6 us
    pallas_call x1, Pallas kernels, per_device(): pl.pallas_call(first_kernel, out_shape=[jax.ShapeDtypeStruct((TILES, G, T...  4.41 us
  transfers between devices with their start and end apart: 10, of which 3 were waited for; matrix products, arithmetic and copies ran while one was open for 2% of the time, Pallas kernels for 5%

profile of v2, /device:TPU:1, one launch (start us, length us, event | category | flops | bytes accessed | tf_op | source)
XLA Modules:
  0.0 82.9 jit_solution(4593107595274114798)
XLA Ops:
  0.0 0.8 copy.50
  2.1 0.8 pad_maximum_fusion
  2.9 11.2 %all-to-all-start = ((bf16[32,48,128]{2,1,0:T(8,128)(2,1)}), bf16[32,48,128]{2,1,0:T(8,128)(2,1)S(1)}, u32[]{:S(2)}, u32[]{:S(2)}) async-start(bf16[32,48,128]{2,1,0:T(8,128)(2,1)} %bitcast.14), calls=%async_computation | async-start | bytes 786432 | tf_op jit(solution)/shard_map/all_to_all | solution.py:201
  15.2 1.4 %collective-permute-start = (bf16[1040,128]{1,0:T(8,128)(2,1)S(1)}, bf16[1040,128]{1,0:T(8,128)(2,1)S(1)}, u32[]{:S(2)}, u32[]{:S(2)}) collective-permute-start(bf16[1040,128]{1,0:T(8,128)(2,1)S(1)} %fusion.1.refs_0_), channel_id=1, source_target_pairs={{0,8},{8,16},{16,24},{24,0},{1,9},{9,17},{17,25},{25,1},{2,10},{10... | collective-permute-start | bytes 798728 | tf_op jit(solution)/shard_map/ppermute | solution.py:172
  16.5 1.5 %collective-permute-start.1 = (bf16[1040,128]{1,0:T(8,128)(2,1)S(1)}, bf16[1040,128]{1,0:T(8,128)(2,1)S(1)}, u32[]{:S(2)}, u32[]{:S(2)}) collective-permute-start(bf16[1040,128]{1,0:T(8,128)(2,1)S(1)} %fusion.1.refs_0_), channel_id=1, source_target_pairs={{0,24},{8,0},{16,8},{24,16},{1,25},{9,1},{17,9},{25,17},{2,26},{10... | collective-permute-start | bytes 798728 | tf_op jit(solution)/shard_map/ppermute | solution.py:172
  18.1 1.6 %collective-permute-start.2 = (bf16[1040,128]{1,0:T(8,128)(2,1)S(1)}, bf16[1040,128]{1,0:T(8,128)(2,1)S(1)}, u32[]{:S(2)}, u32[]{:S(2)}) collective-permute-start(bf16[1040,128]{1,0:T(8,128)(2,1)S(1)} %fusion.1.refs_0_), channel_id=1, source_target_pairs={{0,16},{8,24},{16,0},{24,8},{1,17},{9,25},{17,1},{25,9},{2,18},{10... | collective-permute-start | bytes 798728 | tf_op jit(solution)/shard_map/ppermute | solution.py:172
  19.6 2.5 %collective-permute-start.3 = (bf16[1040,128]{1,0:T(8,128)(2,1)S(1)}, bf16[1040,128]{1,0:T(8,128)(2,1)}, u32[]{:S(2)}, u32[]{:S(2)}) collective-permute-start(bf16[1040,128]{1,0:T(8,128)(2,1)S(1)} %fusion.1.refs_0_), channel_id=1, source_target_pairs={{0,4},{4,0},{1,5},{5,1},{2,6},{6,2},{3,7},{7,3},{8,12},{12,8},{9,1... | collective-permute-start | bytes 798728 | tf_op jit(solution)/shard_map/ppermute | solution.py:172
  22.1 2.3 %collective-permute-done.refs_1_ = bf16[1040,128]{1,0:T(8,128)(2,1)S(1)} collective-permute-done((bf16[1040,128]{1,0:T(8,128)(2,1)S(1)}, bf16[1040,128]{1,0:T(8,128)(2,1)S(1)}, u32[]{:S(2)}, u32[]{:S(2)}) %collective-permute-start) | collective-permute-done | bytes 266272 | tf_op jit(solution)/shard_map/ppermute | solution.py:172
  24.3 0.7 copy-done
  25.0 0.7 copy-done.2
  25.7 5.5 %collective-permute-done.2.refs_3_ = bf16[1040,128]{1,0:T(8,128)(2,1)S(1)} collective-permute-done((bf16[1040,128]{1,0:T(8,128)(2,1)S(1)}, bf16[1040,128]{1,0:T(8,128)(2,1)S(1)}, u32[]{:S(2)}, u32[]{:S(2)}) %collective-permute-start.2) | collective-permute-done | bytes 266272 | tf_op jit(solution)/shard_map/ppermute | solution.py:172
  31.8 2.1 %collective-permute-start.5 = (bf16[1040,128]{1,0:T(8,128)(2,1)}, bf16[1040,128]{1,0:T(8,128)(2,1)S(1)}, u32[]{:S(2)}, u32[]{:S(2)}) collective-permute-start(bf16[1040,128]{1,0:T(8,128)(2,1)} %collective-permute-done.3.refs_4_), channel_id=1, source_target_pairs={{0,24},{8,0},{16,8},{24,16},{1,25},{9,1},{17,9},{25,17},{2,26},{10... | collective-permute-start | bytes 798728 | tf_op jit(solution)/shard_map/ppermute | solution.py:172
  34.1 2.4 %collective-permute-start.6 = (bf16[1040,128]{1,0:T(8,128)(2,1)S(1)}, bf16[1040,128]{1,0:T(8,128)(2,1)S(1)}, u32[]{:S(2)}, u32[]{:S(2)}) collective-permute-start(bf16[1040,128]{1,0:T(8,128)(2,1)S(1)} %collective-permute-done.2.refs_3_), channel_id=1, source_target_pairs={{0,4},{4,0},{1,5},{5,1},{2,6},{6,2},{3,7},{7,3},{8,12},{12,8},{9,1... | collective-permute-start | bytes 798728 | tf_op jit(solution)/shard_map/ppermute | solution.py:172
  36.5 0.7 broadcast_in_dim.44
  37.2 3.5 %all-to-all-start.1 = ((bf16[8,64,128]{2,1,0:T(8,128)(2,1)}), bf16[8,64,128]{2,1,0:T(8,128)(2,1)S(1)}, u32[]{:S(2)}, u32[]{:S(2)}) async-start(bf16[8,64,128]{2,1,0:T(8,128)(2,1)} %broadcast_in_dim.44), calls=%async_computation.1 | async-start | bytes 262144 | tf_op jit(solution)/shard_map/all_to_all | solution.py:215
  41.5 1.0 %copy-done.1 = bf16[1040,128]{1,0:T(8,128)(2,1)S(1)} copy-done((bf16[1040,128]{1,0:T(8,128)(2,1)S(1)}, bf16[1040,128]{1,0:T(8,128)(2,1)}, u32[]{:S(2)}) %copy-start.1) | copy-done | bytes 266264
  42.4 0.9 %copy-done.3 = bf16[1040,128]{1,0:T(8,128)(2,1)S(1)} copy-done((bf16[1040,128]{1,0:T(8,128)(2,1)S(1)}, bf16[1040,128]{1,0:T(8,128)(2,1)}, u32[]{:S(2)}) %copy-start.3) | copy-done | bytes 266264
  43.4 4.4 %attend_first.1 = (f32[2,2,384,128]{3,2,1,0:T(8,128)S(1)}, f32[2,2,384,128]{3,2,1,0:T(8,128)S(1)}) custom-call(s32[5]{0:T(128)S(1)} %pad_add_fusion.info_ref, bf16[32,2,24,128]{3,2,1,0:T(8,128)(2,1)S(1)} %bitcast.39, bf16[1040,128]{1,0:T(8,128)(2,1)S(1)} %fusion.1.refs_0_, bf16[1040,128]{1,0:T(8,128)(2,1)S(1)} %copy-done.1, bf16[1040,128]{1,0:T(8,128)(2,1)S(1)} %copy-done.3, ...), custom_call_target="tpu_custom_call" | custom-call | flops 1006632960 | bytes 3145728 | tf_op jit(solution)/shard_map/attend_first/pallas_call | solution.py:221
  47.8 6.6 %attend_second.1 = bf16[32,2,24,128]{3,2,1,0:T(8,128)(2,1)} custom-call(s32[5]{0:T(128)S(1)} %pad_add_fusion.info_ref, bf16[32,2,24,128]{3,2,1,0:T(8,128)(2,1)S(1)} %bitcast.40, bf16[1040,128]{1,0:T(8,128)(2,1)S(1)} %collective-permute-done.4.refs_0_, bf16[1040,128]{1,0:T(8,128)(2,1)S(1)} %collective-permute-done.5.refs_1_, ...), custom_call_target="tpu_custom_call" | custom-call | flops 805306368 | bytes 3145728 | tf_op jit(solution)/shard_map/attend_second/pallas_call | solution.py:233
  54.4 10.3 %all-to-all-start.2 = ((bf16[32,48,128]{2,1,0:T(8,128)(2,1)}), bf16[32,48,128]{2,1,0:T(8,128)(2,1)S(1)}, u32[]{:S(2)}, u32[]{:S(2)}) async-start(bf16[32,48,128]{2,1,0:T(8,128)(2,1)} %bitcast.23), calls=%async_computation.2 | async-start | bytes 786432 | tf_op jit(solution)/shard_map/all_to_all | solution.py:245
  65.5 13.0 %all-to-all-done.2 = bf16[32,48,128]{2,1,0:T(8,128)(2,1)S(1)} async-done(((bf16[32,48,128]{2,1,0:T(8,128)(2,1)}), bf16[32,48,128]{2,1,0:T(8,128)(2,1)S(1)}, u32[]{:S(2)}, u32[]{:S(2)}) %all-to-all-start.2) | async-done | bytes 393248 | tf_op jit(solution)/shard_map/all_to_all | solution.py:245
  78.5 0.8 copy-done.4
  79.3 1.9 %combine.1 = f32[4,2,24,128]{3,2,1,0:T(8,128)} custom-call(bf16[8,4,2,24,128]{4,3,2,1,0:T(8,128)(2,1)} %bitcast.41), custom_call_target="tpu_custom_call" | custom-call | tf_op jit(solution)/shard_map/combine/pallas_call | solution.py:246
  81.2 0.9 %slice.27 = bf16[4,2,20,128]{3,2,1,0:T(8,128)(2,1)S(1)} slice(f32[4,2,24,128]{3,2,1,0:T(8,128)} %combine.1), slice={[0:4], [0:2], [0:20], [0:128]} | slice | bytes 81920 | tf_op jit(solution)/shard_map/slice | solution.py:253
  (55 shorter events, 5.1 us)
Async XLA Ops:
  1.0 0.7 copy-start.7
  1.0 0.7 copy-start.8
  2.8 11.2 %copy-start.5 = (bf16[256,2,128]{2,1,0:T(2,128)(2,1)S(1)}, bf16[256,2,128]{2,1,0:T(2,128)(2,1)}, u32[]{:S(2)}) copy-start(bf16[256,2,128]{2,1,0:T(2,128)(2,1)} %param.9) | copy-start | bytes 393220
  2.8 11.2 %copy-start.6 = (bf16[256,2,128]{2,1,0:T(2,128)(2,1)S(1)}, bf16[256,2,128]{2,1,0:T(2,128)(2,1)}, u32[]{:S(2)}) copy-start(bf16[256,2,128]{2,1,0:T(2,128)(2,1)} %param.8) | copy-start | bytes 393220
  2.9 28.4 %all-to-all-start = ((bf16[32,48,128]{2,1,0:T(8,128)(2,1)}), bf16[32,48,128]{2,1,0:T(8,128)(2,1)S(1)}, u32[]{:S(2)}, u32[]{:S(2)}) async-start(bf16[32,48,128]{2,1,0:T(8,128)(2,1)} %bitcast.14), calls=%async_computation | async-start | bytes 786432 | tf_op jit(solution)/shard_map/all_to_all | solution.py:201
  14.4 0.7 copy-start.10
  15.2 9.2 %collective-permute-start = (bf16[1040,128]{1,0:T(8,128)(2,1)S(1)}, bf16[1040,128]{1,0:T(8,128)(2,1)S(1)}, u32[]{:S(2)}, u32[]{:S(2)}) collective-permute-start(bf16[1040,128]{1,0:T(8,128)(2,1)S(1)} %fusion.1.refs_0_), channel_id=1, source_target_pairs={{0,8},{8,16},{16,24},{24,0},{1,9},{9,17},{17,25},{25,1},{2,10},{10... | collective-permute-start | bytes 798728 | tf_op jit(solution)/shard_map/ppermute | solution.py:172
  16.5 8.5 %collective-permute-start.1 = (bf16[1040,128]{1,0:T(8,128)(2,1)S(1)}, bf16[1040,128]{1,0:T(8,128)(2,1)S(1)}, u32[]{:S(2)}, u32[]{:S(2)}) collective-permute-start(bf16[1040,128]{1,0:T(8,128)(2,1)S(1)} %fusion.1.refs_0_), channel_id=1, source_target_pairs={{0,24},{8,0},{16,8},{24,16},{1,25},{9,1},{17,9},{25,17},{2,26},{10... | collective-permute-start | bytes 798728 | tf_op jit(solution)/shard_map/ppermute | solution.py:172
  18.1 13.2 %collective-permute-start.2 = (bf16[1040,128]{1,0:T(8,128)(2,1)S(1)}, bf16[1040,128]{1,0:T(8,128)(2,1)S(1)}, u32[]{:S(2)}, u32[]{:S(2)}) collective-permute-start(bf16[1040,128]{1,0:T(8,128)(2,1)S(1)} %fusion.1.refs_0_), channel_id=1, source_target_pairs={{0,16},{8,24},{16,0},{24,8},{1,17},{9,25},{17,1},{25,9},{2,18},{10... | collective-permute-start | bytes 798728 | tf_op jit(solution)/shard_map/ppermute | solution.py:172
  19.6 11.6 %collective-permute-start.3 = (bf16[1040,128]{1,0:T(8,128)(2,1)S(1)}, bf16[1040,128]{1,0:T(8,128)(2,1)}, u32[]{:S(2)}, u32[]{:S(2)}) collective-permute-start(bf16[1040,128]{1,0:T(8,128)(2,1)S(1)} %fusion.1.refs_0_), channel_id=1, source_target_pairs={{0,4},{4,0},{1,5},{5,1},{2,6},{6,2},{3,7},{7,3},{8,12},{12,8},{9,1... | collective-permute-start | bytes 798728 | tf_op jit(solution)/shard_map/ppermute | solution.py:172
  24.3 0.7 copy-start
  25.0 0.7 copy-start.2
  31.3 16.5 %collective-permute-start.4 = (bf16[1040,128]{1,0:T(8,128)(2,1)}, bf16[1040,128]{1,0:T(8,128)(2,1)S(1)}, u32[]{:S(2)}, u32[]{:S(2)}) collective-permute-start(bf16[1040,128]{1,0:T(8,128)(2,1)} %collective-permute-done.3.refs_4_), channel_id=1, source_target_pairs={{0,8},{8,16},{16,24},{24,0},{1,9},{9,17},{17,25},{25,1},{2,10},{10... | collective-permute-start | bytes 798728 | tf_op jit(solution)/shard_map/ppermute | solution.py:172
  31.8 16.0 %collective-permute-start.5 = (bf16[1040,128]{1,0:T(8,128)(2,1)}, bf16[1040,128]{1,0:T(8,128)(2,1)S(1)}, u32[]{:S(2)}, u32[]{:S(2)}) collective-permute-start(bf16[1040,128]{1,0:T(8,128)(2,1)} %collective-permute-done.3.refs_4_), channel_id=1, source_target_pairs={{0,24},{8,0},{16,8},{24,16},{1,25},{9,1},{17,9},{25,17},{2,26},{10... | collective-permute-start | bytes 798728 | tf_op jit(solution)/shard_map/ppermute | solution.py:172
  34.1 13.8 %collective-permute-start.6 = (bf16[1040,128]{1,0:T(8,128)(2,1)S(1)}, bf16[1040,128]{1,0:T(8,128)(2,1)S(1)}, u32[]{:S(2)}, u32[]{:S(2)}) collective-permute-start(bf16[1040,128]{1,0:T(8,128)(2,1)S(1)} %collective-permute-done.2.refs_3_), channel_id=1, source_target_pairs={{0,4},{4,0},{1,5},{5,1},{2,6},{6,2},{3,7},{7,3},{8,12},{12,8},{9,1... | collective-permute-start | bytes 798728 | tf_op jit(solution)/shard_map/ppermute | solution.py:172
  37.2 10.6 %all-to-all-start.1 = ((bf16[8,64,128]{2,1,0:T(8,128)(2,1)}), bf16[8,64,128]{2,1,0:T(8,128)(2,1)S(1)}, u32[]{:S(2)}, u32[]{:S(2)}) async-start(bf16[8,64,128]{2,1,0:T(8,128)(2,1)} %broadcast_in_dim.44), calls=%async_computation.1 | async-start | bytes 262144 | tf_op jit(solution)/shard_map/all_to_all | solution.py:215
  40.7 0.7 copy-start.9
  41.5 1.0 %copy-start.1 = (bf16[1040,128]{1,0:T(8,128)(2,1)S(1)}, bf16[1040,128]{1,0:T(8,128)(2,1)}, u32[]{:S(2)}) copy-start(bf16[1040,128]{1,0:T(8,128)(2,1)} %copy-done) | copy-start | bytes 798724
  42.4 1.0 %copy-start.3 = (bf16[1040,128]{1,0:T(8,128)(2,1)S(1)}, bf16[1040,128]{1,0:T(8,128)(2,1)}, u32[]{:S(2)}) copy-start(bf16[1040,128]{1,0:T(8,128)(2,1)} %copy-done.2) | copy-start | bytes 798724
  54.4 24.1 %all-to-all-start.2 = ((bf16[32,48,128]{2,1,0:T(8,128)(2,1)}), bf16[32,48,128]{2,1,0:T(8,128)(2,1)S(1)}, u32[]{:S(2)}, u32[]{:S(2)}) async-start(bf16[32,48,128]{2,1,0:T(8,128)(2,1)} %bitcast.23), calls=%async_computation.2 | async-start | bytes 786432 | tf_op jit(solution)/shard_map/all_to_all | solution.py:245
  64.8 0.7 copy-start.11
  78.5 0.8 copy-start.4

commit v3 on v2

v3 whole, which is shorter than its diff:
```python
import functools
import math

import jax
import jax.numpy as jnp
import numpy as np
from jax import lax
from jax.experimental import pallas as pl
from jax.experimental.pallas import tpu as pltpu
from jax.sharding import Mesh, PartitionSpec as P

Z, Y, XH, XL, C = 8, 4, 2, 2, 2
HEADS = XL * C
PLANE = Z * HEADS
HOLD = Y * XH
T, R, G, J, D = 2, 2, 2, 5, 128
LIVE = R * T * J
ROWS = 24
BLOCK = 256
QUERIES = T * R * HEADS * G * J
MESSAGE = HEADS * G * ROWS
MASK = 4 * BLOCK
OWN = MASK + 16
OWN_ROWS = 16
PACK = OWN + 2 * G * OWN_ROWS
SOURCES = 16
TILE = SOURCES * ROWS
TILES = PLANE // SOURCES
LOWEST = -1e30
LOG2E = math.log2(math.e)
F32 = jnp.float32
BF16 = jnp.bfloat16
FIRST = ((0, 0), (3, 0), (1, 0), (2, 0), (0, 1))
SECOND = ((3, 1), (1, 1), (2, 1))
CONTRACT_LAST = (((1,), (1,)), ((), ()))


def three_parts(x):
    hi = x.astype(BF16).astype(F32)
    mid = (x - hi).astype(BF16).astype(F32)
    lo = (x - hi - mid).astype(BF16).astype(F32)
    return hi, mid, lo


def ctx_of(offset):
    dy, dx = offset
    y = lax.rem(lax.axis_index("y") + dy, Y)
    xh = lax.rem(lax.axis_index("xh") + dx, XH)
    return (lax.axis_index("z") * Y + y) * XH + xh


def fill_bias(reach_ref, kv_refs, offsets, bias_ref):
    lane = lax.broadcasted_iota(jnp.int32, (1, D), 1)
    for b, (kv_ref, offset) in enumerate(zip(kv_refs, offsets)):
        ctx = ctx_of(offset)
        mask = kv_ref[MASK:OWN, :].astype(F32)
        for i in range(BLOCK // D):
            place = ctx * BLOCK + i * D + lane
            at = b * BLOCK + i * D
            for r in range(R):
                seen = (mask[i : i + 1, :] > 0.5) & (place < reach_ref[r])
                bias_ref[r : r + 1, at : at + D] = jnp.where(seen, 0.0, LOWEST)


def row_parts():
    within = lax.broadcasted_iota(jnp.int32, (SOURCES, ROWS, 1), 1).reshape(TILE, 1)
    source = lax.broadcasted_iota(jnp.int32, (SOURCES, ROWS, 1), 0).reshape(TILE, 1)
    return within, source


def tile_queries(q_ref, tile, g):
    q = q_ref[tile * SOURCES : (tile + 1) * SOURCES, g].astype(F32)
    return q.reshape(TILE, D).astype(BF16)


def block_scores(q, kv_refs, g, bias_ref, is_r1):
    scale = LOG2E / math.sqrt(D)
    scores = []
    for b, kv_ref in enumerate(kv_refs):
        keys = kv_ref[g * 2 * BLOCK : g * 2 * BLOCK + BLOCK, :]
        s = lax.dot_general(q, keys, CONTRACT_LAST, preferred_element_type=F32) * scale
        at = slice(b * BLOCK, (b + 1) * BLOCK)
        scores.append(s + jnp.where(is_r1, bias_ref[1:2, at], bias_ref[0:1, at]))
    return scores


def block_values(kv_refs, g):
    return [kv_ref[g * 2 * BLOCK + BLOCK : (g + 1) * 2 * BLOCK, :] for kv_ref in kv_refs]


def weigh(scores, values, top):
    total, summed = 0.0, 0.0
    for s, v in zip(scores, values):
        p = jnp.exp2(s - top)
        total = total + jnp.sum(p, axis=1, keepdims=True)
        summed = summed + jnp.dot(p.astype(BF16), v, preferred_element_type=F32)
    return total, summed


def top_of(scores):
    wide = functools.reduce(jnp.maximum, scores)
    return jnp.max(wide, axis=1, keepdims=True)


def first_kernel(reach_ref, q_ref, *refs):
    kv_refs, (acc_ref, stat_ref, bias_ref) = refs[: len(FIRST)], refs[len(FIRST) :]
    fill_bias(reach_ref, kv_refs, FIRST, bias_ref)
    within, _ = row_parts()
    lanes = lax.broadcasted_iota(jnp.int32, (TILE, D), 1)
    for tile in range(TILES):
        for g in range(G):
            q = tile_queries(q_ref, tile, g)
            scores = block_scores(q, kv_refs, g, bias_ref, within >= T * J)
            top = top_of(scores)
            total, summed = weigh(scores, block_values(kv_refs, g), top)
            acc_ref[tile, g] = summed
            stat_ref[tile, g] = jnp.where(lanes == 0, top, total)


def second_kernel(reach_ref, q_ref, *refs):
    all_refs, (acc_ref, stat_ref, out_ref, bias_ref) = refs[:HOLD], refs[HOLD:]
    kv_refs = all_refs[len(FIRST) :]
    fill_bias(reach_ref, kv_refs, SECOND, bias_ref)
    within, source = row_parts()
    is_r1 = within >= T * J
    in_r = jnp.where(is_r1, within - T * J, within)
    row_r = jnp.where(is_r1, 1, 0)
    row_t = jnp.where(in_r >= J, 1, 0)
    k = lax.broadcasted_iota(jnp.int32, (1, HOLD * OWN_ROWS), 1)
    own_ctx = jnp.zeros((1, HOLD * OWN_ROWS), jnp.int32)
    for b, offset in enumerate(FIRST + SECOND):
        own_ctx = jnp.where((k >> 4) == b, ctx_of(offset), own_ctx)
    own_place = T * (own_ctx * HEADS + ((k >> 2) & 3)) + (k & 1)
    own_r = (k >> 1) & 1
    lanes = lax.broadcasted_iota(jnp.int32, (TILE, D), 1)
    here = lax.axis_index("y") * XH + lax.axis_index("xh")
    for tile in range(TILES):
        from_source = tile * SOURCES + source
        row_device = ((from_source >> 2) * HOLD + here) * HEADS + (from_source & 3)
        row_place = T * row_device + row_t
        seen = (own_r == row_r) & (own_place <= row_place)
        stats = jnp.zeros((TILE, D), F32)
        outs = []
        for g in range(G):
            q = tile_queries(q_ref, tile, g)
            scores = block_scores(q, kv_refs, g, bias_ref, is_r1)
            at = OWN + g * OWN_ROWS
            own_keys = jnp.concatenate([ref[at : at + OWN_ROWS, :] for ref in all_refs], axis=0)
            at = at + G * OWN_ROWS
            own_values = jnp.concatenate([ref[at : at + OWN_ROWS, :] for ref in all_refs], axis=0)
            so = lax.dot_general(q, own_keys, CONTRACT_LAST, preferred_element_type=F32)
            so = jnp.where(seen, so * (LOG2E / math.sqrt(D)), LOWEST)
            before = stat_ref[tile, g]
            top_before, total_before = before[:, 0:1], before[:, 1:2]
            top = jnp.maximum(top_of(scores), jnp.max(so, axis=1, keepdims=True))
            top = jnp.maximum(top, top_before)
            values = block_values(kv_refs, g) + [own_values]
            total, summed = weigh(scores + [so], values, top)
            shrink = jnp.exp2(top_before - top)
            total = total + total_before * shrink
            summed = (summed + acc_ref[tile, g] * shrink) * (1.0 / total)
            outs.append(summed.reshape(SOURCES, ROWS, D))
            for i, part in enumerate(three_parts(top + jnp.log2(total))):
                stats = jnp.where(lanes == (g * 3 + i) * LIVE + within, part, stats)
        stats = jnp.where(within < LIVE, stats, 0.0).reshape(SOURCES, ROWS, D)
        stats = jnp.sum(stats, axis=1, keepdims=True)
        spare = lax.broadcasted_iota(jnp.int32, (SOURCES, ROWS, D), 1) == LIVE
        at = slice(tile * SOURCES, (tile + 1) * SOURCES)
        out_ref[at, 0] = jnp.where(spare, stats, outs[0]).astype(BF16)
        out_ref[at, 1] = outs[1].astype(BF16)


def combine_kernel(lengths_ref, order_ref, in_ref, out_ref, rows_ref):
    lane = lax.broadcasted_iota(jnp.int32, (1, ROWS, D), 2)
    row = lax.broadcasted_iota(jnp.int32, (1, ROWS, D), 1)
    for h in range(HEADS):
        parts = [in_ref[:, h, g].astype(F32) for g in range(G)]
        stats = parts[0][:, LIVE : LIVE + 1, :]
        for g in range(G):
            mine = False
            for i in range(3):
                mine = mine | (lane == (g * 3 + i) * LIVE + row)
            mine = mine & (row < LIVE)
            lse = jnp.sum(jnp.where(mine, stats, 0.0), axis=2, keepdims=True)
            top = jnp.max(lse, axis=0, keepdims=True)
            w = jnp.exp2(lse - top)
            o = jnp.sum(parts[g] * w, axis=0) / jnp.sum(w, axis=0)
            at = (h * G + g) * ROWS
            rows_ref[at : at + ROWS, :] = jnp.where(row[0] < LIVE, o, 0.0)
    rows = jnp.dot(order_ref[...], rows_ref[...].astype(BF16), preferred_element_type=F32)
    heads = HEADS * G * J
    first = T * (ctx_of((0, 0)) * HEADS + lax.axis_index("xl") * C + lax.axis_index("c"))
    for t in range(T):
        for r in range(R):
            at = (t * R + r) * heads
            live = first + t < lengths_ref[r]
            out_ref[t, r] = jnp.where(live, rows[at : at + heads, :], 0.0).astype(BF16)


def message_order():
    order = np.zeros((MESSAGE, QUERIES), np.float32)
    for h in range(HEADS):
        for g in range(G):
            for r in range(R):
                for t in range(T):
                    for j in range(J):
                        to = (h * G + g) * ROWS + (r * T + t) * J + j
                        order[to, (t * R + r) * HEADS * G * J + (h * G + g) * J + j] = 1
    return order


def own_order():
    kv_heads = HEADS * G
    order = np.zeros((2 * T * R * kv_heads, 2 * T * R * kv_heads), np.float32)
    for h in range(HEADS):
        for kv in range(2):
            for g in range(G):
                for r in range(R):
                    for t in range(T):
                        to = ((h * 2 + kv) * G + g) * R * T + r * T + t
                        order[to, (kv * T * R + t * R + r) * kv_heads + h * G + g] = 1
    return order


def message_kernel(order_ref, own_order_ref, q_ref, k_ref, v_ref, message_ref, *refs):
    own_refs, own_rows = refs[:HEADS], refs[HEADS]
    q = q_ref[...].astype(F32).reshape(QUERIES, D).astype(BF16)
    rows = jnp.dot(order_ref[...], q, preferred_element_type=F32).astype(BF16)
    for z in range(Z):
        message_ref[z] = rows
    own = [ref[...].astype(F32).reshape(T * R * HEADS * G, D) for ref in (k_ref, v_ref)]
    own = jnp.concatenate(own, axis=0).astype(BF16)
    own = jnp.dot(own_order_ref[...], own, preferred_element_type=F32)
    own_rows[...] = own.reshape(HEADS, own.shape[0] // HEADS, D)
    head = lax.axis_index("xl") * C + lax.axis_index("c")
    for step, own_ref in enumerate(own_refs):
        own_ref[...] = own_rows[lax.rem(head + step, HEADS)].astype(BF16)


def pack_kernel(mask_ref, k_ref, v_ref, *refs):
    own_refs, (pack_ref, wide, by_head, sorted_rows) = refs[:HEADS], refs[HEADS:]
    for kv, ref in enumerate((k_ref, v_ref)):
        wide[kv] = ref[...].astype(F32)
        for g in range(G):
            at = (g * 2 + kv) * BLOCK
            pack_ref[at : at + BLOCK, :] = wide[kv, pl.ds(g, BLOCK, stride=G), :].astype(BF16)
    head = lax.axis_index("xl") * C + lax.axis_index("c")
    for step, own_ref in enumerate(own_refs):
        by_head[lax.rem(head + HEADS - step, HEADS)] = own_ref[...].astype(F32)
    part = T * R
    for h in range(HEADS):
        for kind in range(2 * G):
            at = kind * OWN_ROWS + h * part
            sorted_rows[at : at + part, :] = by_head[h, kind * part : (kind + 1) * part, :]
    pack_ref[OWN:PACK, :] = sorted_rows[...].astype(BF16)
    by_head[0] = jnp.zeros((16, D), F32)
    by_head[0, 0 : BLOCK // D, :] = mask_ref[...].astype(F32)
    pack_ref[MASK:OWN, :] = by_head[0].astype(BF16)


def permute(x, axis, size, shift):
    return lax.ppermute(x, axis, [(i, (i + shift) % size) for i in range(size)])


def per_device(
    prompt_keys,
    prompt_values,
    prompt_mask,
    response_queries,
    response_keys,
    response_values,
    resp_lengths,
    prompt_reach,
):
    plane = ("z", "xl", "c")
    head = ("xl", "c")
    smem = pl.BlockSpec(memory_space=pltpu.SMEM)
    vmem = pl.BlockSpec(memory_space=pltpu.VMEM)
    order = message_order()
    own_part = 2 * G * T * R
    message, *own = pl.pallas_call(
        message_kernel,
        out_shape=[jax.ShapeDtypeStruct((Z, MESSAGE, D), BF16)]
        + [jax.ShapeDtypeStruct((own_part, D), BF16)] * HEADS,
        in_specs=[vmem] * 5,
        out_specs=[vmem] * (1 + HEADS),
        scratch_shapes=[pltpu.VMEM((HEADS, own_part, D), F32)],
        name="message",
    )(
        jnp.asarray(order, BF16),
        jnp.asarray(own_order(), BF16),
        response_queries,
        response_keys,
        response_values,
    )
    own = [own[0]] + [permute(own[step], head, HEADS, step) for step in range(1, HEADS)]
    rows = lax.all_to_all(message.reshape(PLANE, G * ROWS, D), plane, 0, 0, tiled=True)
    kv = pl.pallas_call(
        pack_kernel,
        out_shape=jax.ShapeDtypeStruct((PACK, D), BF16),
        in_specs=[vmem] * (3 + HEADS),
        out_specs=vmem,
        scratch_shapes=[
            pltpu.VMEM((2, G * BLOCK, D), F32),
            pltpu.VMEM((HEADS, own_part, D), F32),
            pltpu.VMEM((HEADS * own_part, D), F32),
        ],
        name="pack",
    )(
        prompt_mask.reshape(BLOCK // D, D),
        prompt_keys.reshape(BLOCK * G, D),
        prompt_values.reshape(BLOCK * G, D),
        *own,
    )
    across = permute(kv, "xh", XH, 1)
    far = permute(kv, "y", Y, 2)
    before = permute(kv, "y", Y, 1)
    after = permute(kv, "y", Y, 3)
    across_before = permute(across, "y", Y, 1)
    across_after = permute(across, "y", Y, 3)
    across_far = permute(far, "xh", XH, 1)
    rows = rows.reshape(PLANE, G, ROWS, D)
    first_blocks = (kv, before, after, far, across)
    second_blocks = (across_before, across_after, across_far)
    pair_flops = 4 * PLANE * G * ROWS * BLOCK * D
    acc, stat = pl.pallas_call(
        first_kernel,
        out_shape=[jax.ShapeDtypeStruct((TILES, G, TILE, D), F32)] * 2,
        in_specs=[smem] + [vmem] * (1 + len(FIRST)),
        out_specs=[vmem] * 2,
        scratch_shapes=[pltpu.VMEM((8, len(FIRST) * BLOCK), F32)],
        compiler_params=pltpu.CompilerParams(vmem_limit_bytes=24 << 20),
        cost_estimate=pl.CostEstimate(
            flops=len(FIRST) * pair_flops,
            bytes_accessed=3 << 20,
            transcendentals=len(FIRST) * pair_flops // 512,
        ),
        name="attend_first",
    )(prompt_reach, rows, *first_blocks)
    partial = pl.pallas_call(
        second_kernel,
        out_shape=jax.ShapeDtypeStruct((PLANE, G, ROWS, D), BF16),
        in_specs=[smem] + [vmem] * (3 + HOLD),
        out_specs=vmem,
        scratch_shapes=[pltpu.VMEM((8, len(SECOND) * BLOCK), F32)],
        compiler_params=pltpu.CompilerParams(vmem_limit_bytes=24 << 20),
        cost_estimate=pl.CostEstimate(
            flops=4 * pair_flops, bytes_accessed=3 << 20, transcendentals=4 * pair_flops // 512
        ),
        name="attend_second",
    )(prompt_reach, rows, *first_blocks, *second_blocks, acc, stat)
    partial = lax.all_to_all(partial.reshape(PLANE, G * ROWS, D), plane, 0, 0, tiled=True)
    return pl.pallas_call(
        combine_kernel,
        out_shape=jax.ShapeDtypeStruct((T, R, HEADS * G * J, D), BF16),
        in_specs=[smem, vmem, vmem],
        out_specs=vmem,
        scratch_shapes=[pltpu.VMEM((MESSAGE, D), F32)],
        name="combine",
    )(resp_lengths, jnp.asarray(order.T, BF16), partial.reshape(Z, HEADS, G, ROWS, D))


def solution(mesh):
    fine = Mesh(mesh.devices.reshape(Z, Y, XH, XL, C), ("z", "y", "xh", "xl", "c"))
    ctx, head = ("z", "y", "xh"), ("xl", "c")
    return jax.shard_map(
        per_device,
        mesh=fine,
        in_specs=(
            P(ctx, head, None),
            P(ctx, head, None),
            P(ctx),
            P(ctx + head, None, None, None),
            P(ctx + head, None, None, None),
            P(ctx + head, None, None, None),
            P(),
            P(),
        ),
        out_specs=P(ctx + head, None, None, None),
        check_vma=False,
    )
```

time: 84 us -> 75.8 us (0.902)
  blocking collectives: 0 us -> 21.6 us
  starting transfers between devices: 37 us -> 24.8 us
  waiting for transfers between devices: 20.8 us -> 11.3 us
  local copies, waits for them, and re-layouts: 10.2 us -> 1.56 us
  Pallas kernels: 13 us -> 15.9 us
  other arithmetic: 1.58 us -> 0 us
    all_to_all x0 -> x1, blocking collectives: none -> 21.6 us  [per_device(): lax.all_to_all(partial.reshape(PLANE, G * ROWS, D), plane, 0, 0, tiled=True)]
    all_to_all x3 -> x1, starting transfers between devices: 25 us -> 11.1 us  [per_device(): lax.all_to_all(message.reshape(PLANE, G * ROWS, D), plane, 0, 0, tiled=True)]
    all_to_all x3 -> x1, waiting for transfers between devices: 13 us -> 0.01 us  [per_device(): lax.all_to_all(message.reshape(PLANE, G * ROWS, D), plane, 0, 0, tiled=True)]
    unnamed x25 -> x18, local copies, waits for them, and re-layouts: 7.49 us -> 1.56 us
    pallas_call x1 -> x3, Pallas kernels: 1.94 us -> 5.81 us  [the longest x1 2.13 us: per_device(): pl.pallas_call(combine_kernel, out_shape=jax.ShapeDtypeStruct((T, R, HEAD...]
    ppermute x7 -> x10, waiting for transfers between devices: 7.8 us -> 11.3 us  [permute(): return lax.ppermute(x, axis, [(i, (i + shift) % size) for i in range(size)])]
    ppermute x7 -> x10, starting transfers between devices: 12 us -> 13.8 us  [permute(): return lax.ppermute(x, axis, [(i, (i + shift) % size) for i in range(size)])]
    another operation x4 -> x0, other arithmetic: 1 us -> none  [the longest x2 0.9 us: per_device(): message = jnp.stack([first, second], axis=2).reshape(PLANE, G * ROWS, D)]
  transfers between devices with their start and end apart: 10 -> 11, of which waited for: 3 -> 6; matrix products, arithmetic and copies ran while one was open for 2% -> 0% of each run, Pallas kernels for 5% -> 8%
where the time goes in v3:
time: 75.8 us; the launch traced here: 75.3 us
  starting transfers between devices  24.8 us (33%)
  blocking collectives  21.6 us (28%)
  Pallas kernels  15.9 us (21%)
  waiting for transfers between devices  11.3 us (15%)
  local copies, waits for them, and re-layouts  1.56 us (2%)
    all_to_all x1, blocking collectives, per_device(): lax.all_to_all(partial.reshape(PLANE, G * ROWS, D), plane, 0, 0, tiled=True)  21.6 us
    ppermute x10, starting transfers between devices, permute(): return lax.ppermute(x, axis, [(i, (i + shift) % size) for i in range(size)])  13.8 us
    ppermute x10, waiting for transfers between devices, permute(): return lax.ppermute(x, axis, [(i, (i + shift) % size) for i in range(size)])  11.3 us
    all_to_all x1, starting transfers between devices, per_device(): lax.all_to_all(message.reshape(PLANE, G * ROWS, D), plane, 0, 0, tiled=True)  11.1 us
    pallas_call x1, Pallas kernels, per_device(): pl.pallas_call(second_kernel, out_shape=jax.ShapeDtypeStruct((PLANE, G, R...  6.06 us
    pallas_call x1, Pallas kernels, per_device(): pl.pallas_call(first_kernel, out_shape=[jax.ShapeDtypeStruct((TILES, G, T...  4.01 us
    pallas_call x1, Pallas kernels, per_device(): pl.pallas_call(combine_kernel, out_shape=jax.ShapeDtypeStruct((T, R, HEAD...  2.13 us
    pallas_call x1, Pallas kernels, per_device(): pl.pallas_call(message_kernel, out_shape=[jax.ShapeDtypeStruct((Z, MESSAG...  1.87 us
  transfers between devices with their start and end apart: 11, of which 6 were waited for; matrix products, arithmetic and copies ran while one was open for 0% of the time, Pallas kernels for 8%

profile of v3, /device:TPU:1, one launch (start us, length us, event | category | flops | bytes accessed | tf_op | source)
XLA Modules:
  0.0 75.3 jit_solution(17979391359159849333)
XLA Ops:
  0.0 1.9 %message.1 = (bf16[8,192,128]{2,1,0:T(8,128)(2,1)}, bf16[16,128]{1,0:T(8,128)(2,1)}, bf16[16,128]{1,0:T(8,128)(2,1)}, bf16[16,128]{1,0:T(8,128)(2,1)}, bf16[16,128]{1,0:T(8,128)(2,1)}) custom-call(bf16[192,160]{1,0:T(8,128)(2,1)} %constant.6.clone.order_ref, bf16[64,64]{1,0:T(8,128)(2,1)} %constant.7.clone.own_order_ref, bf16[2,2,40,128]{3,2,1,0:T(8,128)(2,1)} %q_ref.1, ...), custom_call_target="tpu_custom_call" | custom-call | tf_op jit(solution)/shard_map/message/pallas_call | solution.py:281
  1.9 11.1 %all-to-all-start = ((bf16[32,48,128]{2,1,0:T(8,128)(2,1)}), bf16[32,48,128]{2,1,0:T(8,128)(2,1)S(1)}, u32[]{:S(2)}, u32[]{:S(2)}) async-start(bf16[32,48,128]{2,1,0:T(8,128)(2,1)} %bitcast.11), calls=%async_computation | async-start | bytes 786432 | tf_op jit(solution)/shard_map/all_to_all | solution.py:297
  13.0 1.7 %collective-permute-start = (bf16[16,128]{1,0:T(8,128)(2,1)S(1)}, bf16[16,128]{1,0:T(8,128)(2,1)S(1)}, u32[]{:S(2)}, u32[]{:S(2)}) collective-permute-start(bf16[16,128]{1,0:T(8,128)(2,1)S(1)} %copy-done.8), channel_id=1, source_target_pairs={{0,1},{1,2},{2,3},{3,0},{4,5},{5,6},{6,7},{7,4},{8,9},{9,10},{10,1... | collective-permute-start | bytes 12296 | tf_op jit(solution)/shard_map/ppermute | solution.py:262
  14.7 0.0 collective-permute-start.1
  14.7 0.5 collective-permute-start.2
  15.2 0.2 collective-permute-done.refs_1_
  15.4 2.0 %collective-permute-done.1.refs_2_ = bf16[16,128]{1,0:T(8,128)(2,1)S(1)} collective-permute-done((bf16[16,128]{1,0:T(8,128)(2,1)S(1)}, bf16[16,128]{1,0:T(8,128)(2,1)S(1)}, u32[]{:S(2)}, u32[]{:S(2)}) %collective-permute-start.1) | collective-permute-done | bytes 4128 | tf_op jit(solution)/shard_map/ppermute | solution.py:262
  17.4 0.7 collective-permute-done.2.refs_3_
  18.1 0.6 copy-done.5
  18.7 1.8 %pack.1.refs_0_ = bf16[1104,128]{1,0:T(8,128)(2,1)} custom-call(s32[2,128]{1,0:T(2,128)} %bitcast.14, bf16[512,128]{1,0:T(8,128)(2,1)} %bitcast.12, bf16[512,128]{1,0:T(8,128)(2,1)} %bitcast.13, bf16[16,128]{1,0:T(8,128)(2,1)} %get-tuple-element.13.refs_0_, bf16[16,128]{1,0:T(8,128)(2,1)} %copy-done.3, bf16[16,128]{1,0:T(8,128)(2,1)} %copy-done.4, ...), custom_call_target="tpu_custom_call" | custom-call | tf_op jit(solution)/shard_map/pack/pallas_call | solution.py:298
  20.5 2.5 %collective-permute-start.6 = (bf16[1104,128]{1,0:T(8,128)(2,1)}, bf16[1104,128]{1,0:T(8,128)(2,1)S(1)}, u32[]{:S(2)}, u32[]{:S(2)}) collective-permute-start(bf16[1104,128]{1,0:T(8,128)(2,1)} %pack.1.refs_0_), channel_id=1, source_target_pairs={{0,4},{4,0},{1,5},{5,1},{2,6},{6,2},{3,7},{7,3},{8,12},{12,8},{9,1... | collective-permute-start | bytes 847880 | tf_op jit(solution)/shard_map/ppermute | solution.py:262
  22.9 2.9 %collective-permute-start.5 = (bf16[1104,128]{1,0:T(8,128)(2,1)}, bf16[1104,128]{1,0:T(8,128)(2,1)S(1)}, u32[]{:S(2)}, u32[]{:S(2)}) collective-permute-start(bf16[1104,128]{1,0:T(8,128)(2,1)} %pack.1.refs_0_), channel_id=1, source_target_pairs={{0,16},{8,24},{16,0},{24,8},{1,17},{9,25},{17,1},{25,9},{2,18},{10... | collective-permute-start | bytes 847880 | tf_op jit(solution)/shard_map/ppermute | solution.py:262
  25.9 0.8 %collective-permute-start.4 = (bf16[1104,128]{1,0:T(8,128)(2,1)}, bf16[1104,128]{1,0:T(8,128)(2,1)S(1)}, u32[]{:S(2)}, u32[]{:S(2)}) collective-permute-start(bf16[1104,128]{1,0:T(8,128)(2,1)} %pack.1.refs_0_), channel_id=1, source_target_pairs={{0,24},{8,0},{16,8},{24,16},{1,25},{9,1},{17,9},{25,17},{2,26},{10... | collective-permute-start | bytes 847880 | tf_op jit(solution)/shard_map/ppermute | solution.py:262
  26.6 0.7 collective-permute-start.3
  27.3 4.3 %collective-permute-done.6.refs_4_ = bf16[1104,128]{1,0:T(8,128)(2,1)S(1)} collective-permute-done((bf16[1104,128]{1,0:T(8,128)(2,1)}, bf16[1104,128]{1,0:T(8,128)(2,1)S(1)}, u32[]{:S(2)}, u32[]{:S(2)}) %collective-permute-start.6) | collective-permute-done | bytes 282656 | tf_op jit(solution)/shard_map/ppermute | solution.py:262
  31.6 2.7 %collective-permute-start.8 = (bf16[1104,128]{1,0:T(8,128)(2,1)S(1)}, bf16[1104,128]{1,0:T(8,128)(2,1)S(1)}, u32[]{:S(2)}, u32[]{:S(2)}) collective-permute-start(bf16[1104,128]{1,0:T(8,128)(2,1)S(1)} %collective-permute-done.6.refs_4_), channel_id=1, source_target_pairs={{0,24},{8,0},{16,8},{24,16},{1,25},{9,1},{17,9},{25,17},{2,26},{10... | collective-permute-start | bytes 847880 | tf_op jit(solution)/shard_map/ppermute | solution.py:262
  34.3 1.9 %collective-permute-start.9 = (bf16[1104,128]{1,0:T(8,128)(2,1)S(1)}, bf16[1104,128]{1,0:T(8,128)(2,1)S(1)}, u32[]{:S(2)}, u32[]{:S(2)}) collective-permute-start(bf16[1104,128]{1,0:T(8,128)(2,1)S(1)} %collective-permute-done.5.refs_3_), channel_id=1, source_target_pairs={{0,4},{4,0},{1,5},{5,1},{2,6},{6,2},{3,7},{7,3},{8,12},{12,8},{9,1... | collective-permute-start | bytes 847880 | tf_op jit(solution)/shard_map/ppermute | solution.py:262
  36.3 3.1 %collective-permute-done.4.refs_2_ = bf16[1104,128]{1,0:T(8,128)(2,1)S(1)} collective-permute-done((bf16[1104,128]{1,0:T(8,128)(2,1)}, bf16[1104,128]{1,0:T(8,128)(2,1)S(1)}, u32[]{:S(2)}, u32[]{:S(2)}) %collective-permute-start.4) | collective-permute-done | bytes 282656 | tf_op jit(solution)/shard_map/ppermute | solution.py:262
  39.4 0.9 %copy-done = bf16[1104,128]{1,0:T(8,128)(2,1)S(1)} copy-done((bf16[1104,128]{1,0:T(8,128)(2,1)S(1)}, bf16[1104,128]{1,0:T(8,128)(2,1)}, u32[]{:S(2)}) %copy-start) | copy-done | bytes 282648
  40.4 4.0 %attend_first.1 = (f32[2,2,384,128]{3,2,1,0:T(8,128)S(1)}, f32[2,2,384,128]{3,2,1,0:T(8,128)S(1)}) custom-call(s32[2]{0:T(128)S(1)} %copy-done.2, bf16[32,2,24,128]{3,2,1,0:T(8,128)(2,1)S(1)} %bitcast.7, bf16[1104,128]{1,0:T(8,128)(2,1)S(1)} %copy-done, bf16[1104,128]{1,0:T(8,128)(2,1)S(1)} %collective-permute-done.3.refs_1_, ...), custom_call_target="tpu_custom_call" | custom-call | flops 1006632960 | bytes 3145728 | tf_op jit(solution)/shard_map/attend_first/pallas_call | solution.py:326
  44.4 1.1 %collective-permute-done.8.refs_6_ = bf16[1104,128]{1,0:T(8,128)(2,1)S(1)} collective-permute-done((bf16[1104,128]{1,0:T(8,128)(2,1)S(1)}, bf16[1104,128]{1,0:T(8,128)(2,1)S(1)}, u32[]{:S(2)}, u32[]{:S(2)}) %collective-permute-start.8) | collective-permute-done | bytes 282656 | tf_op jit(solution)/shard_map/ppermute | solution.py:262
  45.5 6.1 %attend_second.1 = bf16[32,2,24,128]{3,2,1,0:T(8,128)(2,1)S(1)} custom-call(s32[2]{0:T(128)S(1)} %copy-done.2, bf16[32,2,24,128]{3,2,1,0:T(8,128)(2,1)S(1)} %bitcast.8, bf16[1104,128]{1,0:T(8,128)(2,1)S(1)} %copy-done.1, bf16[1104,128]{1,0:T(8,128)(2,1)S(1)} %collective-permute-done.3.refs_1_, bf16[1104,128]{1,0:T(8,128)(2,1)S(1)} %collective-permute-done.4.refs_2_, ...), custom_call_target="tpu_custom_call" | custom-call | flops 805306368 | bytes 3145728 | tf_op jit(solution)/shard_map/attend_second/pallas_call | solution.py:340
  51.6 21.6 %all_to_all.10 = bf16[32,48,128]{2,1,0:T(8,128)(2,1)} all-to-all(bf16[32,48,128]{2,1,0:T(8,128)(2,1)S(1)} %bitcast.9), channel_id=1, replica_groups=mesh['z'=8,'y'=4,'xh'=2,'xl'=2,'c'=2] {'z','xl','c'}, dimensions={0} | all-to-all | bytes 786432 | tf_op jit(solution)/shard_map/all_to_all | solution.py:352
  73.1 2.1 %combine.1 = bf16[2,2,40,128]{3,2,1,0:T(8,128)(2,1)} custom-call(s32[2]{0:T(128)} %lengths_ref.1, bf16[160,192]{1,0:T(8,128)(2,1)} %constant.8.clone.order_ref, bf16[8,4,2,24,128]{4,3,2,1,0:T(8,128)(2,1)} %bitcast.10), custom_call_target="tpu_custom_call" | custom-call | tf_op jit(solution)/shard_map/combine/pallas_call | solution.py:353
  (22 shorter events, 0.0 us)
Async XLA Ops:
  1.9 11.1 %copy-start.8 = (bf16[16,128]{1,0:T(8,128)(2,1)S(1)}, bf16[16,128]{1,0:T(8,128)(2,1)}, u32[]{:S(2)}) copy-start(bf16[16,128]{1,0:T(8,128)(2,1)} %get-tuple-element.14) | copy-start | bytes 12292
  1.9 12.8 %copy-start.7 = (bf16[16,128]{1,0:T(8,128)(2,1)S(1)}, bf16[16,128]{1,0:T(8,128)(2,1)}, u32[]{:S(2)}) copy-start(bf16[16,128]{1,0:T(8,128)(2,1)} %get-tuple-element.15) | copy-start | bytes 12292
  1.9 37.6 %all-to-all-start = ((bf16[32,48,128]{2,1,0:T(8,128)(2,1)}), bf16[32,48,128]{2,1,0:T(8,128)(2,1)S(1)}, u32[]{:S(2)}, u32[]{:S(2)}) async-start(bf16[32,48,128]{2,1,0:T(8,128)(2,1)} %bitcast.11), calls=%async_computation | async-start | bytes 786432 | tf_op jit(solution)/shard_map/all_to_all | solution.py:297
  12.9 1.7 %copy-start.6 = (bf16[16,128]{1,0:T(8,128)(2,1)S(1)}, bf16[16,128]{1,0:T(8,128)(2,1)}, u32[]{:S(2)}) copy-start(bf16[16,128]{1,0:T(8,128)(2,1)} %get-tuple-element.16) | copy-start | bytes 12292
  13.0 2.5 %collective-permute-start = (bf16[16,128]{1,0:T(8,128)(2,1)S(1)}, bf16[16,128]{1,0:T(8,128)(2,1)S(1)}, u32[]{:S(2)}, u32[]{:S(2)}) collective-permute-start(bf16[16,128]{1,0:T(8,128)(2,1)S(1)} %copy-done.8), channel_id=1, source_target_pairs={{0,1},{1,2},{2,3},{3,0},{4,5},{5,6},{6,7},{7,4},{8,9},{9,10},{10,1... | collective-permute-start | bytes 12296 | tf_op jit(solution)/shard_map/ppermute | solution.py:262
  14.7 2.8 %collective-permute-start.1 = (bf16[16,128]{1,0:T(8,128)(2,1)S(1)}, bf16[16,128]{1,0:T(8,128)(2,1)S(1)}, u32[]{:S(2)}, u32[]{:S(2)}) collective-permute-start(bf16[16,128]{1,0:T(8,128)(2,1)S(1)} %copy-done.7), channel_id=1, source_target_pairs={{0,2},{1,3},{2,0},{3,1},{4,6},{5,7},{6,4},{7,5},{8,10},{9,11},{10,... | collective-permute-start | bytes 12296 | tf_op jit(solution)/shard_map/ppermute | solution.py:262
  14.7 3.4 %collective-permute-start.2 = (bf16[16,128]{1,0:T(8,128)(2,1)S(1)}, bf16[16,128]{1,0:T(8,128)(2,1)S(1)}, u32[]{:S(2)}, u32[]{:S(2)}) collective-permute-start(bf16[16,128]{1,0:T(8,128)(2,1)S(1)} %copy-done.6), channel_id=1, source_target_pairs={{0,3},{1,0},{2,1},{3,2},{4,7},{5,4},{6,5},{7,6},{8,11},{9,8},{10,9... | collective-permute-start | bytes 12296 | tf_op jit(solution)/shard_map/ppermute | solution.py:262
  15.4 2.7 %copy-start.3 = (bf16[16,128]{1,0:T(8,128)(2,1)}, bf16[16,128]{1,0:T(8,128)(2,1)S(1)}, u32[]{:S(2)}) copy-start(bf16[16,128]{1,0:T(8,128)(2,1)S(1)} %collective-permute-done.refs_1_) | copy-start | bytes 12292
  17.4 0.7 copy-start.4
  18.1 0.6 copy-start.5
  20.5 18.9 %copy-start.2 = (s32[2]{0:T(128)S(1)}, s32[2]{0:T(128)}, u32[]{:S(2)}) copy-start(s32[2]{0:T(128)} %reach_ref.3) | copy-start | bytes 28
  20.5 11.1 %collective-permute-start.6 = (bf16[1104,128]{1,0:T(8,128)(2,1)}, bf16[1104,128]{1,0:T(8,128)(2,1)S(1)}, u32[]{:S(2)}, u32[]{:S(2)}) collective-permute-start(bf16[1104,128]{1,0:T(8,128)(2,1)} %pack.1.refs_0_), channel_id=1, source_target_pairs={{0,4},{4,0},{1,5},{5,1},{2,6},{6,2},{3,7},{7,3},{8,12},{12,8},{9,1... | collective-permute-start | bytes 847880 | tf_op jit(solution)/shard_map/ppermute | solution.py:262
  22.9 11.4 %collective-permute-start.5 = (bf16[1104,128]{1,0:T(8,128)(2,1)}, bf16[1104,128]{1,0:T(8,128)(2,1)S(1)}, u32[]{:S(2)}, u32[]{:S(2)}) collective-permute-start(bf16[1104,128]{1,0:T(8,128)(2,1)} %pack.1.refs_0_), channel_id=1, source_target_pairs={{0,16},{8,24},{16,0},{24,8},{1,17},{9,25},{17,1},{25,9},{2,18},{10... | collective-permute-start | bytes 847880 | tf_op jit(solution)/shard_map/ppermute | solution.py:262
  25.9 13.6 %collective-permute-start.4 = (bf16[1104,128]{1,0:T(8,128)(2,1)}, bf16[1104,128]{1,0:T(8,128)(2,1)S(1)}, u32[]{:S(2)}, u32[]{:S(2)}) collective-permute-start(bf16[1104,128]{1,0:T(8,128)(2,1)} %pack.1.refs_0_), channel_id=1, source_target_pairs={{0,24},{8,0},{16,8},{24,16},{1,25},{9,1},{17,9},{25,17},{2,26},{10... | collective-permute-start | bytes 847880 | tf_op jit(solution)/shard_map/ppermute | solution.py:262
  26.6 12.8 %collective-permute-start.3 = (bf16[1104,128]{1,0:T(8,128)(2,1)}, bf16[1104,128]{1,0:T(8,128)(2,1)S(1)}, u32[]{:S(2)}, u32[]{:S(2)}) collective-permute-start(bf16[1104,128]{1,0:T(8,128)(2,1)} %pack.1.refs_0_), channel_id=1, source_target_pairs={{0,8},{8,16},{16,24},{24,0},{1,9},{9,17},{17,25},{25,1},{2,10},{10... | collective-permute-start | bytes 847880 | tf_op jit(solution)/shard_map/ppermute | solution.py:262
  31.6 13.9 %collective-permute-start.8 = (bf16[1104,128]{1,0:T(8,128)(2,1)S(1)}, bf16[1104,128]{1,0:T(8,128)(2,1)S(1)}, u32[]{:S(2)}, u32[]{:S(2)}) collective-permute-start(bf16[1104,128]{1,0:T(8,128)(2,1)S(1)} %collective-permute-done.6.refs_4_), channel_id=1, source_target_pairs={{0,24},{8,0},{16,8},{24,16},{1,25},{9,1},{17,9},{25,17},{2,26},{10... | collective-permute-start | bytes 847880 | tf_op jit(solution)/shard_map/ppermute | solution.py:262
  34.3 11.1 %collective-permute-start.7 = (bf16[1104,128]{1,0:T(8,128)(2,1)S(1)}, bf16[1104,128]{1,0:T(8,128)(2,1)S(1)}, u32[]{:S(2)}, u32[]{:S(2)}) collective-permute-start(bf16[1104,128]{1,0:T(8,128)(2,1)S(1)} %collective-permute-done.6.refs_4_), channel_id=1, source_target_pairs={{0,8},{8,16},{16,24},{24,0},{1,9},{9,17},{17,25},{25,1},{2,10},{10... | collective-permute-start | bytes 847880 | tf_op jit(solution)/shard_map/ppermute | solution.py:262
  34.3 11.1 %collective-permute-start.9 = (bf16[1104,128]{1,0:T(8,128)(2,1)S(1)}, bf16[1104,128]{1,0:T(8,128)(2,1)S(1)}, u32[]{:S(2)}, u32[]{:S(2)}) collective-permute-start(bf16[1104,128]{1,0:T(8,128)(2,1)S(1)} %collective-permute-done.5.refs_3_), channel_id=1, source_target_pairs={{0,4},{4,0},{1,5},{5,1},{2,6},{6,2},{3,7},{7,3},{8,12},{12,8},{9,1... | collective-permute-start | bytes 847880 | tf_op jit(solution)/shard_map/ppermute | solution.py:262
  39.4 1.0 %copy-start = (bf16[1104,128]{1,0:T(8,128)(2,1)S(1)}, bf16[1104,128]{1,0:T(8,128)(2,1)}, u32[]{:S(2)}) copy-start(bf16[1104,128]{1,0:T(8,128)(2,1)} %pack.1.refs_0_) | copy-start | bytes 847876
  40.4 5.1 %copy-start.1 = (bf16[1104,128]{1,0:T(8,128)(2,1)S(1)}, bf16[1104,128]{1,0:T(8,128)(2,1)}, u32[]{:S(2)}) copy-start(bf16[1104,128]{1,0:T(8,128)(2,1)} %pack.1.refs_0_) | copy-start | bytes 847876

commit v4 on v3

v4 whole, which is shorter than its diff:
```python
import functools
import math

import jax
import jax.numpy as jnp
import numpy as np
from jax import lax
from jax.experimental import pallas as pl
from jax.experimental.pallas import tpu as pltpu
from jax.sharding import Mesh, PartitionSpec as P

Z, Y, XH, XL, C = 8, 4, 2, 2, 2
HEADS = XL * C
PLANE = Z * HEADS
HOLD = Y * XH
T, R, G, J, D = 2, 2, 2, 5, 128
LIVE = R * T * J
ROWS = 24
BLOCK = 256
QUERIES = T * R * HEADS * G * J
MESSAGE = HEADS * G * ROWS
MASK = 4 * BLOCK
PACK = MASK + 16
OWN_PART = 2 * G * R * T
NEAR = HOLD * HEADS
BLOCKS = ((0, 0), (3, 0), (1, 0), (2, 0), (0, 1), (3, 1), (1, 1), (2, 1))
SOURCES = 16
TILE = SOURCES * ROWS
TILES = PLANE // SOURCES
LOWEST = -1e30
LOG2E = math.log2(math.e)
F32 = jnp.float32
BF16 = jnp.bfloat16
CONTRACT_LAST = (((1,), (1,)), ((), ()))


def three_parts(x):
    hi = x.astype(BF16).astype(F32)
    mid = (x - hi).astype(BF16).astype(F32)
    lo = (x - hi - mid).astype(BF16).astype(F32)
    return hi, mid, lo


def ctx_of(offset):
    dy, dx = offset
    y = lax.rem(lax.axis_index("y") + dy, Y)
    xh = lax.rem(lax.axis_index("xh") + dx, XH)
    return (lax.axis_index("z") * Y + y) * XH + xh


def row_parts():
    lane = lax.broadcasted_iota(jnp.int32, (1, TILE), 1)
    source = (lane * 2731) >> 16
    return source, lane - source * ROWS


def fill_bias(reach_ref, kv_refs, bias_ref):
    lane = lax.broadcasted_iota(jnp.int32, (1, D), 1)
    sub = lax.broadcasted_iota(jnp.int32, (8, D), 0)
    _, within = row_parts()
    row_r = jnp.where(within >= T * J, 1, 0)
    pick = (lax.broadcasted_iota(jnp.int32, (8, TILE), 0) == row_r).astype(F32).astype(BF16)
    for b, (kv_ref, offset) in enumerate(zip(kv_refs, BLOCKS)):
        ctx = ctx_of(offset)
        mask = kv_ref[MASK:PACK, :].astype(F32)
        for i in range(BLOCK // D):
            place = ctx * BLOCK + i * D + lane
            reach = jnp.where(sub == 0, reach_ref[0], reach_ref[1])
            seen = (mask[i : i + 1, :] > 0.5) & (place < reach)
            hide = jnp.where(seen, 0.0, LOWEST).astype(BF16)
            bias_ref[b, i * D : (i + 1) * D, :] = lax.dot_general(
                hide, pick, (((0,), (0,)), ((), ())), preferred_element_type=F32
            )


def tile_queries(q_ref, tile, g):
    q = q_ref[tile * SOURCES : (tile + 1) * SOURCES, g].astype(F32)
    return q.reshape(TILE, D).astype(BF16)


def block_scores(q, kv_refs, g, bias_ref):
    scores = []
    for b, kv_ref in enumerate(kv_refs):
        keys = kv_ref[g * 2 * BLOCK : g * 2 * BLOCK + BLOCK, :]
        s = lax.dot_general(keys, q, CONTRACT_LAST, preferred_element_type=F32)
        scores.append(s + bias_ref[b])
    return scores


def block_values(kv_refs, g):
    return [kv_ref[g * 2 * BLOCK + BLOCK : (g + 1) * 2 * BLOCK, :] for kv_ref in kv_refs]


def weigh(scores, values, top):
    scale = LOG2E / math.sqrt(D)
    total, summed = 0.0, 0.0
    top = top * scale
    for s, v in zip(scores, values):
        p = jnp.exp2(s * scale - top)
        total = total + jnp.sum(p, axis=0, keepdims=True)
        summed = summed + lax.dot_general(
            v, p.astype(BF16), (((0,), (0,)), ((), ())), preferred_element_type=F32
        )
    return total, summed


def top_of(scores):
    wide = functools.reduce(jnp.maximum, scores)
    return jnp.max(wide, axis=0, keepdims=True)


def finish(outs, lse, tile, out_ref):
    source, within = row_parts()
    mine = lax.broadcasted_iota(jnp.int32, (SOURCES, TILE), 0) == source
    row = lax.broadcasted_iota(jnp.int32, (SOURCES, ROWS, D), 1).reshape(TILE, D)
    lane = lax.broadcasted_iota(jnp.int32, (TILE, D), 1)
    spread = ((row == lane) & (row < LIVE)).astype(F32).astype(BF16)
    stats = 0.0
    for g in range(G):
        for i, part in enumerate(three_parts(lse[g])):
            rows = jnp.where(mine, part, 0.0).astype(BF16)
            rows = jnp.dot(rows, spread, preferred_element_type=F32)
            at = (g * 3 + i) * LIVE
            stats = stats + (pltpu.roll(rows, at, 1) if at else rows)
    at = slice(tile * SOURCES, (tile + 1) * SOURCES)
    spare = lax.broadcasted_iota(jnp.int32, (SOURCES, ROWS, D), 1) == LIVE
    out_ref[at, 0] = jnp.where(spare, stats[:, None, :], outs[0]).astype(BF16)
    out_ref[at, 1] = outs[1].astype(BF16)


def own_seen(tile):
    source, within = row_parts()
    is_r1 = within >= T * J
    in_r = jnp.where(is_r1, within - T * J, within)
    row_r = jnp.where(is_r1, 1, 0)
    row_t = jnp.where(in_r >= J, 1, 0)
    k = lax.broadcasted_iota(jnp.int32, (R * T * NEAR, 1), 0)
    own_place = T * (lax.axis_index("z") * NEAR + (k & (NEAR - 1))) + ((k >> 5) & 1)
    own_r = k >> 6
    here = lax.axis_index("y") * XH + lax.axis_index("xh")
    from_source = tile * SOURCES + source
    row_device = ((from_source >> 2) * HOLD + here) * HEADS + (from_source & 3)
    row_place = T * row_device + row_t
    return (own_r == row_r) & (own_place <= row_place)


def own_part(own_rows, kind):
    at = kind * R * T
    parts = [own_rows[pl.ds(at + e, NEAR, stride=OWN_PART), :] for e in range(R * T)]
    return jnp.concatenate(parts, axis=0).astype(BF16)


def attend_kernel(reach_ref, q_ref, own_ref, *refs):
    kv_refs, (out_ref, bias_ref, own_rows) = refs[:HOLD], refs[HOLD:]
    fill_bias(reach_ref, kv_refs, bias_ref)
    own_rows[...] = own_ref[...].astype(F32)
    own_keys = [own_part(own_rows, g) for g in range(G)]
    own_values = [own_part(own_rows, G + g) for g in range(G)]
    scale = LOG2E / math.sqrt(D)
    for tile in range(TILES):
        seen = own_seen(tile)
        outs, lse = [], []
        for g in range(G):
            q = tile_queries(q_ref, tile, g)
            scores = block_scores(q, kv_refs, g, bias_ref)
            so = lax.dot_general(own_keys[g], q, CONTRACT_LAST, preferred_element_type=F32)
            so = jnp.where(seen, so, LOWEST)
            top = jnp.maximum(top_of(scores), jnp.max(so, axis=0, keepdims=True))
            values = block_values(kv_refs, g) + [own_values[g]]
            total, summed = weigh(scores + [so], values, top)
            summed = summed * (1.0 / total)
            outs.append(jnp.transpose(summed).reshape(SOURCES, ROWS, D))
            lse.append(top * scale + jnp.log2(total))
        finish(outs, lse, tile, out_ref)


def combine_kernel(lengths_ref, order_ref, in_ref, out_ref, rows_ref):
    lane = lax.broadcasted_iota(jnp.int32, (1, ROWS, D), 2)
    row = lax.broadcasted_iota(jnp.int32, (1, ROWS, D), 1)
    for h in range(HEADS):
        parts = [in_ref[:, h, g].astype(F32) for g in range(G)]
        stats = parts[0][:, LIVE : LIVE + 1, :]
        for g in range(G):
            mine = False
            for i in range(3):
                mine = mine | (lane == (g * 3 + i) * LIVE + row)
            mine = mine & (row < LIVE)
            lse = jnp.sum(jnp.where(mine, stats, 0.0), axis=2, keepdims=True)
            top = jnp.max(lse, axis=0, keepdims=True)
            w = jnp.exp2(lse - top)
            o = jnp.sum(parts[g] * w, axis=0) / jnp.sum(w, axis=0)
            at = (h * G + g) * ROWS
            rows_ref[at : at + ROWS, :] = jnp.where(row[0] < LIVE, o, 0.0)
    rows = jnp.dot(order_ref[...], rows_ref[...].astype(BF16), preferred_element_type=F32)
    heads = HEADS * G * J
    first = T * (ctx_of((0, 0)) * HEADS + lax.axis_index("xl") * C + lax.axis_index("c"))
    for t in range(T):
        for r in range(R):
            at = (t * R + r) * heads
            live = first + t < lengths_ref[r]
            out_ref[t, r] = jnp.where(live, rows[at : at + heads, :], 0.0).astype(BF16)


def message_order():
    order = np.zeros((MESSAGE, QUERIES), np.float32)
    for h in range(HEADS):
        for g in range(G):
            for r in range(R):
                for t in range(T):
                    for j in range(J):
                        to = (h * G + g) * ROWS + (r * T + t) * J + j
                        order[to, (t * R + r) * HEADS * G * J + (h * G + g) * J + j] = 1
    return order


def own_order():
    kv_heads = HEADS * G
    order = np.zeros((2 * T * R * kv_heads, 2 * T * R * kv_heads), np.float32)
    for h in range(HEADS):
        for kv in range(2):
            for g in range(G):
                for r in range(R):
                    for t in range(T):
                        to = ((h * 2 + kv) * G + g) * R * T + r * T + t
                        order[to, (kv * T * R + t * R + r) * kv_heads + h * G + g] = 1
    return order


def message_kernel(order_ref, own_order_ref, q_ref, k_ref, v_ref, message_ref, own_ref):
    q = q_ref[...].astype(F32).reshape(QUERIES, D).astype(BF16)
    rows = jnp.dot(order_ref[...], q, preferred_element_type=F32).astype(BF16)
    for z in range(Z):
        message_ref[z] = rows
    own = [ref[...].astype(F32).reshape(T * R * HEADS * G, D) for ref in (k_ref, v_ref)]
    own = jnp.concatenate(own, axis=0).astype(BF16)
    own = jnp.dot(own_order_ref[...], own, preferred_element_type=F32).astype(BF16)
    for hold in range(HOLD):
        own_ref[hold] = own


def pack_kernel(mask_ref, k_ref, v_ref, pack_ref, wide, mask_rows):
    for kv, ref in enumerate((k_ref, v_ref)):
        wide[kv] = ref[...].astype(F32)
        for g in range(G):
            at = (g * 2 + kv) * BLOCK
            pack_ref[at : at + BLOCK, :] = wide[kv, pl.ds(g, BLOCK, stride=G), :].astype(BF16)
    mask_rows[...] = jnp.zeros_like(mask_rows)
    mask_rows[0 : BLOCK // D, :] = mask_ref[...].astype(F32)
    pack_ref[MASK:PACK, :] = mask_rows[...].astype(BF16)


def permute(x, axis, size, shift):
    return lax.ppermute(x, axis, [(i, (i + shift) % size) for i in range(size)])


def per_device(
    prompt_keys,
    prompt_values,
    prompt_mask,
    response_queries,
    response_keys,
    response_values,
    resp_lengths,
    prompt_reach,
):
    plane = ("z", "xl", "c")
    near = ("y", "xh", "xl", "c")
    smem = pl.BlockSpec(memory_space=pltpu.SMEM)
    vmem = pl.BlockSpec(memory_space=pltpu.VMEM)
    order = message_order()
    kv = pl.pallas_call(
        pack_kernel,
        out_shape=jax.ShapeDtypeStruct((PACK, D), BF16),
        in_specs=[vmem] * 3,
        out_specs=vmem,
        scratch_shapes=[pltpu.VMEM((2, G * BLOCK, D), F32), pltpu.VMEM((16, D), F32)],
        name="pack",
    )(
        prompt_mask.reshape(BLOCK // D, D),
        prompt_keys.reshape(BLOCK * G, D),
        prompt_values.reshape(BLOCK * G, D),
    )
    across = permute(kv, "xh", XH, 1)
    far = permute(kv, "y", Y, 2)
    before = permute(kv, "y", Y, 1)
    after = permute(kv, "y", Y, 3)
    message, own = pl.pallas_call(
        message_kernel,
        out_shape=[
            jax.ShapeDtypeStruct((Z, MESSAGE, D), BF16),
            jax.ShapeDtypeStruct((HOLD, HEADS * OWN_PART, D), BF16),
        ],
        in_specs=[vmem] * 5,
        out_specs=[vmem] * 2,
        name="message",
    )(
        jnp.asarray(order, BF16),
        jnp.asarray(own_order(), BF16),
        response_queries,
        response_keys,
        response_values,
    )
    rows = lax.all_to_all(message.reshape(PLANE, G * ROWS, D), plane, 0, 0, tiled=True)
    rows, own = lax.optimization_barrier((rows, own))
    own = lax.all_to_all(own.reshape(NEAR, OWN_PART, D), near, 0, 0, tiled=True)
    across_before = permute(across, "y", Y, 1)
    across_after = permute(across, "y", Y, 3)
    across_far = permute(far, "xh", XH, 1)
    blocks = (kv, before, after, far, across, across_before, across_after, across_far)
    pair_flops = 4 * PLANE * G * ROWS * BLOCK * D
    partial = pl.pallas_call(
        attend_kernel,
        out_shape=jax.ShapeDtypeStruct((PLANE, G, ROWS, D), BF16),
        in_specs=[smem] + [vmem] * (2 + HOLD),
        out_specs=vmem,
        scratch_shapes=[
            pltpu.VMEM((HOLD, BLOCK, TILE), F32),
            pltpu.VMEM((NEAR * OWN_PART, D), F32),
        ],
        compiler_params=pltpu.CompilerParams(vmem_limit_bytes=32 << 20),
        cost_estimate=pl.CostEstimate(
            flops=9 * pair_flops, bytes_accessed=4 << 20, transcendentals=9 * pair_flops // 512
        ),
        name="attend",
    )(prompt_reach, rows.reshape(PLANE, G, ROWS, D), own.reshape(NEAR * OWN_PART, D), *blocks)
    partial = lax.all_to_all(partial.reshape(PLANE, G * ROWS, D), plane, 0, 0, tiled=True)
    return pl.pallas_call(
        combine_kernel,
        out_shape=jax.ShapeDtypeStruct((T, R, HEADS * G * J, D), BF16),
        in_specs=[smem, vmem, vmem],
        out_specs=vmem,
        scratch_shapes=[pltpu.VMEM((MESSAGE, D), F32)],
        name="combine",
    )(resp_lengths, jnp.asarray(order.T, BF16), partial.reshape(Z, HEADS, G, ROWS, D))


def solution(mesh):
    fine = Mesh(mesh.devices.reshape(Z, Y, XH, XL, C), ("z", "y", "xh", "xl", "c"))
    ctx, head = ("z", "y", "xh"), ("xl", "c")
    return jax.shard_map(
        per_device,
        mesh=fine,
        in_specs=(
            P(ctx, head, None),
            P(ctx, head, None),
            P(ctx),
            P(ctx + head, None, None, None),
            P(ctx + head, None, None, None),
            P(ctx + head, None, None, None),
            P(),
            P(),
        ),
        out_specs=P(ctx + head, None, None, None),
        check_vma=False,
    )
```

time: 75.8 us -> 76.1 us (level)
  starting transfers between devices: 24.8 us -> 30.2 us
  Pallas kernels: 15.9 us -> 12.1 us
  blocking collectives: 21.6 us -> 19.9 us
  waiting for transfers between devices: 11.3 us -> 12.7 us
  local copies, waits for them, and re-layouts: 1.56 us -> 0.66 us
    all_to_all x0 -> x1, waiting for transfers between devices: none -> 7.57 us  [per_device(): own = lax.all_to_all(own.reshape(NEAR, OWN_PART, D), near, 0, 0, tiled=True)]
    all_to_all x0 -> x1, starting transfers between devices: none -> 6.81 us  [per_device(): own = lax.all_to_all(own.reshape(NEAR, OWN_PART, D), near, 0, 0, tiled=True)]
    ppermute x10 -> x7, waiting for transfers between devices: 11.3 us -> 5.14 us  [permute(): return lax.ppermute(x, axis, [(i, (i + shift) % size) for i in range(size)])]
    pallas_call x2 -> x1, Pallas kernels: 10.1 us -> 6.28 us  [per_device(): pl.pallas_call(attend_kernel, out_shape=jax.ShapeDtypeStruct((PLANE, G, R...]
    all_to_all x1, blocking collectives: 21.6 us -> 19.9 us  [per_device(): lax.all_to_all(partial.reshape(PLANE, G * ROWS, D), plane, 0, 0, tiled=True)]
    ppermute x10 -> x7, starting transfers between devices: 13.8 us -> 12.3 us  [permute(): return lax.ppermute(x, axis, [(i, (i + shift) % size) for i in range(size)])]
    unnamed x18 -> x4, local copies, waits for them, and re-layouts: 1.56 us -> 0.66 us
  transfers between devices with their start and end apart: 11 -> 9, of which waited for: 6 -> 2; matrix products, arithmetic and copies ran while one was open for 0% -> 0% of each run, Pallas kernels for 8% -> 2%
where the time goes in v4:
time: 76.1 us; the launch traced here: 75.6 us
  starting transfers between devices  30.2 us (40%)
  blocking collectives  19.9 us (26%)
  waiting for transfers between devices  12.7 us (17%)
  Pallas kernels  12.1 us (16%)
    all_to_all x1, blocking collectives, per_device(): lax.all_to_all(partial.reshape(PLANE, G * ROWS, D), plane, 0, 0, tiled=True)  19.9 us
    ppermute x7, starting transfers between devices, permute(): return lax.ppermute(x, axis, [(i, (i + shift) % size) for i in range(size)])  12.3 us
    all_to_all x1, starting transfers between devices, per_device(): lax.all_to_all(message.reshape(PLANE, G * ROWS, D), plane, 0, 0, tiled=True)  11.1 us
    all_to_all x1, waiting for transfers between devices, per_device(): own = lax.all_to_all(own.reshape(NEAR, OWN_PART, D), near, 0, 0, tiled=True)  7.57 us
    all_to_all x1, starting transfers between devices, per_device(): own = lax.all_to_all(own.reshape(NEAR, OWN_PART, D), near, 0, 0, tiled=True)  6.81 us
    pallas_call x1, Pallas kernels, per_device(): pl.pallas_call(attend_kernel, out_shape=jax.ShapeDtypeStruct((PLANE, G, R...  6.28 us
    ppermute x7, waiting for transfers between devices, permute(): return lax.ppermute(x, axis, [(i, (i + shift) % size) for i in range(size)])  5.14 us
    pallas_call x1, Pallas kernels, per_device(): pl.pallas_call(combine_kernel, out_shape=jax.ShapeDtypeStruct((T, R, HEAD...  2.13 us
  transfers between devices with their start and end apart: 9, of which 2 were waited for; matrix products, arithmetic and copies ran while one was open for 0% of the time, Pallas kernels for 2%

profile of v4, /device:TPU:1, one launch (start us, length us, event | category | flops | bytes accessed | tf_op | source)
XLA Modules:
  0.0 75.6 jit_solution(3945207808703993169)
XLA Ops:
  0.0 1.9 %message.1 = (bf16[8,192,128]{2,1,0:T(8,128)(2,1)}, bf16[8,64,128]{2,1,0:T(8,128)(2,1)}) custom-call(bf16[192,160]{1,0:T(8,128)(2,1)} %constant.6.clone.order_ref, bf16[64,64]{1,0:T(8,128)(2,1)} %constant.7.clone.own_order_ref, bf16[2,2,40,128]{3,2,1,0:T(8,128)(2,1)} %q_ref.1, bf16[2,2,8,128]{3,2,1,0:T(8,128)(2,1)} %k_ref.1, bf16[2,2,8,128]{3,2,1,0:T(8,128)(2,1)} %v_ref.1), custom_call_target="tpu_custom_call" | custom-call | tf_op jit(solution)/shard_map/message/pallas_call | solution.py:287
  1.9 11.1 %all-to-all-start = ((bf16[32,48,128]{2,1,0:T(8,128)(2,1)}), bf16[32,48,128]{2,1,0:T(8,128)(2,1)S(1)}, u32[]{:S(2)}, u32[]{:S(2)}) async-start(bf16[32,48,128]{2,1,0:T(8,128)(2,1)} %bitcast.13), calls=%async_computation | async-start | bytes 786432 | tf_op jit(solution)/shard_map/all_to_all | solution.py:303
  13.0 1.8 %pack.1.refs_0_ = bf16[1040,128]{1,0:T(8,128)(2,1)} custom-call(s32[2,128]{1,0:T(2,128)} %bitcast.16, bf16[512,128]{1,0:T(8,128)(2,1)} %bitcast.14, bf16[512,128]{1,0:T(8,128)(2,1)} %bitcast.15), custom_call_target="tpu_custom_call" | custom-call | tf_op jit(solution)/shard_map/pack/pallas_call | solution.py:271
  14.7 2.5 %collective-permute-start.3 = (bf16[1040,128]{1,0:T(8,128)(2,1)}, bf16[1040,128]{1,0:T(8,128)(2,1)S(1)}, u32[]{:S(2)}, u32[]{:S(2)}) collective-permute-start(bf16[1040,128]{1,0:T(8,128)(2,1)} %pack.1.refs_0_), channel_id=1, source_target_pairs={{0,4},{4,0},{1,5},{5,1},{2,6},{6,2},{3,7},{7,3},{8,12},{12,8},{9,1... | collective-permute-start | bytes 798728 | tf_op jit(solution)/shard_map/ppermute | solution.py:253
  17.2 2.9 %collective-permute-start.2 = (bf16[1040,128]{1,0:T(8,128)(2,1)}, bf16[1040,128]{1,0:T(8,128)(2,1)S(1)}, u32[]{:S(2)}, u32[]{:S(2)}) collective-permute-start(bf16[1040,128]{1,0:T(8,128)(2,1)} %pack.1.refs_0_), channel_id=1, source_target_pairs={{0,16},{8,24},{16,0},{24,8},{1,17},{9,25},{17,1},{25,9},{2,18},{10... | collective-permute-start | bytes 798728 | tf_op jit(solution)/shard_map/ppermute | solution.py:253
  20.1 0.4 collective-permute-start
  20.5 2.3 %collective-permute-start.1 = (bf16[1040,128]{1,0:T(8,128)(2,1)}, bf16[1040,128]{1,0:T(8,128)(2,1)S(1)}, u32[]{:S(2)}, u32[]{:S(2)}) collective-permute-start(bf16[1040,128]{1,0:T(8,128)(2,1)} %pack.1.refs_0_), channel_id=1, source_target_pairs={{0,24},{8,0},{16,8},{24,16},{1,25},{9,1},{17,9},{25,17},{2,26},{10... | collective-permute-start | bytes 798728 | tf_op jit(solution)/shard_map/ppermute | solution.py:253
  22.8 5.1 %collective-permute-done.3.refs_4_ = bf16[1040,128]{1,0:T(8,128)(2,1)S(1)} collective-permute-done((bf16[1040,128]{1,0:T(8,128)(2,1)}, bf16[1040,128]{1,0:T(8,128)(2,1)S(1)}, u32[]{:S(2)}, u32[]{:S(2)}) %collective-permute-start.3) | collective-permute-done | bytes 266272 | tf_op jit(solution)/shard_map/ppermute | solution.py:253
  27.9 1.3 %collective-permute-start.4 = (bf16[1040,128]{1,0:T(8,128)(2,1)S(1)}, bf16[1040,128]{1,0:T(8,128)(2,1)S(1)}, u32[]{:S(2)}, u32[]{:S(2)}) collective-permute-start(bf16[1040,128]{1,0:T(8,128)(2,1)S(1)} %collective-permute-done.3.refs_4_), channel_id=1, source_target_pairs={{0,8},{8,16},{16,24},{24,0},{1,9},{9,17},{17,25},{25,1},{2,10},{10... | collective-permute-start | bytes 798728 | tf_op jit(solution)/shard_map/ppermute | solution.py:253
  29.2 1.4 %collective-permute-start.5 = (bf16[1040,128]{1,0:T(8,128)(2,1)S(1)}, bf16[1040,128]{1,0:T(8,128)(2,1)S(1)}, u32[]{:S(2)}, u32[]{:S(2)}) collective-permute-start(bf16[1040,128]{1,0:T(8,128)(2,1)S(1)} %collective-permute-done.3.refs_4_), channel_id=1, source_target_pairs={{0,24},{8,0},{16,8},{24,16},{1,25},{9,1},{17,9},{25,17},{2,26},{10... | collective-permute-start | bytes 798728 | tf_op jit(solution)/shard_map/ppermute | solution.py:253
  30.7 0.0 collective-permute-done.2.refs_3_
  30.7 1.5 %collective-permute-start.6 = (bf16[1040,128]{1,0:T(8,128)(2,1)S(1)}, bf16[1040,128]{1,0:T(8,128)(2,1)S(1)}, u32[]{:S(2)}, u32[]{:S(2)}) collective-permute-start(bf16[1040,128]{1,0:T(8,128)(2,1)S(1)} %collective-permute-done.2.refs_3_), channel_id=1, source_target_pairs={{0,4},{4,0},{1,5},{5,1},{2,6},{6,2},{3,7},{7,3},{8,12},{12,8},{9,1... | collective-permute-start | bytes 798728 | tf_op jit(solution)/shard_map/ppermute | solution.py:253
  32.2 0.0 all-to-all-done
  32.2 6.8 %all-to-all-start.1 = ((bf16[32,16,128]{2,1,0:T(8,128)(2,1)}), bf16[32,16,128]{2,1,0:T(8,128)(2,1)S(1)}, u32[]{:S(2)}, u32[]{:S(2)}) async-start(bf16[32,16,128]{2,1,0:T(8,128)(2,1)} %bitcast.2), calls=%async_computation.1 | async-start | bytes 262144 | tf_op jit(solution)/shard_map/all_to_all | solution.py:305
  39.0 0.0 collective-permute-done.refs_1_
  39.0 0.0 collective-permute-done.1.refs_2_
  39.0 0.0 collective-permute-done.4.refs_5_
  39.0 0.0 collective-permute-done.5.refs_6_
  39.0 0.0 collective-permute-done.6.refs_7_
  39.1 7.6 %all-to-all-done.1 = bf16[32,16,128]{2,1,0:T(8,128)(2,1)S(1)} async-done(((bf16[32,16,128]{2,1,0:T(8,128)(2,1)}), bf16[32,16,128]{2,1,0:T(8,128)(2,1)S(1)}, u32[]{:S(2)}, u32[]{:S(2)}) %all-to-all-start.1) | async-done | bytes 131104 | tf_op jit(solution)/shard_map/all_to_all | solution.py:305
  46.6 0.7 copy-done.1
  47.3 6.3 %attend.1 = bf16[32,2,24,128]{3,2,1,0:T(8,128)(2,1)S(1)} custom-call(s32[2]{0:T(128)S(1)} %copy-done.1, bf16[32,2,24,128]{3,2,1,0:T(8,128)(2,1)S(1)} %bitcast.9, bf16[512,128]{1,0:T(8,128)(2,1)S(1)} %bitcast.11, bf16[1040,128]{1,0:T(8,128)(2,1)S(1)} %copy-done, bf16[1040,128]{1,0:T(8,128)(2,1)S(1)} %collective-permute-done.refs_1_, ...), custom_call_target="tpu_custom_call" | custom-call | flops 1811939328 | bytes 4194304 | tf_op jit(solution)/shard_map/attend/pallas_call | solution.py:311
  53.6 19.9 %all_to_all.15 = bf16[32,48,128]{2,1,0:T(8,128)(2,1)} all-to-all(bf16[32,48,128]{2,1,0:T(8,128)(2,1)S(1)} %bitcast.10), channel_id=1, replica_groups=mesh['z'=8,'y'=4,'xh'=2,'xl'=2,'c'=2] {'z','xl','c'}, dimensions={0} | all-to-all | bytes 786432 | tf_op jit(solution)/shard_map/all_to_all | solution.py:326
  73.5 2.1 %combine.1 = bf16[2,2,40,128]{3,2,1,0:T(8,128)(2,1)} custom-call(s32[2]{0:T(128)} %lengths_ref.1, bf16[160,192]{1,0:T(8,128)(2,1)} %constant.8.clone.order_ref, bf16[8,4,2,24,128]{4,3,2,1,0:T(8,128)(2,1)} %bitcast.12), custom_call_target="tpu_custom_call" | custom-call | tf_op jit(solution)/shard_map/combine/pallas_call | solution.py:327
  (3 shorter events, 0.0 us)
Async XLA Ops:
  1.9 30.3 %all-to-all-start = ((bf16[32,48,128]{2,1,0:T(8,128)(2,1)}), bf16[32,48,128]{2,1,0:T(8,128)(2,1)S(1)}, u32[]{:S(2)}, u32[]{:S(2)}) async-start(bf16[32,48,128]{2,1,0:T(8,128)(2,1)} %bitcast.13), calls=%async_computation | async-start | bytes 786432 | tf_op jit(solution)/shard_map/all_to_all | solution.py:303
  14.7 31.9 %copy-start = (bf16[1040,128]{1,0:T(8,128)(2,1)S(1)}, bf16[1040,128]{1,0:T(8,128)(2,1)}, u32[]{:S(2)}) copy-start(bf16[1040,128]{1,0:T(8,128)(2,1)} %pack.1.refs_0_) | copy-start | bytes 798724
  14.7 13.2 %collective-permute-start.3 = (bf16[1040,128]{1,0:T(8,128)(2,1)}, bf16[1040,128]{1,0:T(8,128)(2,1)S(1)}, u32[]{:S(2)}, u32[]{:S(2)}) collective-permute-start(bf16[1040,128]{1,0:T(8,128)(2,1)} %pack.1.refs_0_), channel_id=1, source_target_pairs={{0,4},{4,0},{1,5},{5,1},{2,6},{6,2},{3,7},{7,3},{8,12},{12,8},{9,1... | collective-permute-start | bytes 798728 | tf_op jit(solution)/shard_map/ppermute | solution.py:253
  17.2 13.5 %collective-permute-start.2 = (bf16[1040,128]{1,0:T(8,128)(2,1)}, bf16[1040,128]{1,0:T(8,128)(2,1)S(1)}, u32[]{:S(2)}, u32[]{:S(2)}) collective-permute-start(bf16[1040,128]{1,0:T(8,128)(2,1)} %pack.1.refs_0_), channel_id=1, source_target_pairs={{0,16},{8,24},{16,0},{24,8},{1,17},{9,25},{17,1},{25,9},{2,18},{10... | collective-permute-start | bytes 798728 | tf_op jit(solution)/shard_map/ppermute | solution.py:253
  20.1 18.9 %collective-permute-start = (bf16[1040,128]{1,0:T(8,128)(2,1)}, bf16[1040,128]{1,0:T(8,128)(2,1)S(1)}, u32[]{:S(2)}, u32[]{:S(2)}) collective-permute-start(bf16[1040,128]{1,0:T(8,128)(2,1)} %pack.1.refs_0_), channel_id=1, source_target_pairs={{0,8},{8,16},{16,24},{24,0},{1,9},{9,17},{17,25},{25,1},{2,10},{10... | collective-permute-start | bytes 798728 | tf_op jit(solution)/shard_map/ppermute | solution.py:253
  20.5 18.5 %collective-permute-start.1 = (bf16[1040,128]{1,0:T(8,128)(2,1)}, bf16[1040,128]{1,0:T(8,128)(2,1)S(1)}, u32[]{:S(2)}, u32[]{:S(2)}) collective-permute-start(bf16[1040,128]{1,0:T(8,128)(2,1)} %pack.1.refs_0_), channel_id=1, source_target_pairs={{0,24},{8,0},{16,8},{24,16},{1,25},{9,1},{17,9},{25,17},{2,26},{10... | collective-permute-start | bytes 798728 | tf_op jit(solution)/shard_map/ppermute | solution.py:253
  27.9 11.1 %collective-permute-start.4 = (bf16[1040,128]{1,0:T(8,128)(2,1)S(1)}, bf16[1040,128]{1,0:T(8,128)(2,1)S(1)}, u32[]{:S(2)}, u32[]{:S(2)}) collective-permute-start(bf16[1040,128]{1,0:T(8,128)(2,1)S(1)} %collective-permute-done.3.refs_4_), channel_id=1, source_target_pairs={{0,8},{8,16},{16,24},{24,0},{1,9},{9,17},{17,25},{25,1},{2,10},{10... | collective-permute-start | bytes 798728 | tf_op jit(solution)/shard_map/ppermute | solution.py:253
  29.2 9.8 %collective-permute-start.5 = (bf16[1040,128]{1,0:T(8,128)(2,1)S(1)}, bf16[1040,128]{1,0:T(8,128)(2,1)S(1)}, u32[]{:S(2)}, u32[]{:S(2)}) collective-permute-start(bf16[1040,128]{1,0:T(8,128)(2,1)S(1)} %collective-permute-done.3.refs_4_), channel_id=1, source_target_pairs={{0,24},{8,0},{16,8},{24,16},{1,25},{9,1},{17,9},{25,17},{2,26},{10... | collective-permute-start | bytes 798728 | tf_op jit(solution)/shard_map/ppermute | solution.py:253
  30.7 8.4 %collective-permute-start.6 = (bf16[1040,128]{1,0:T(8,128)(2,1)S(1)}, bf16[1040,128]{1,0:T(8,128)(2,1)S(1)}, u32[]{:S(2)}, u32[]{:S(2)}) collective-permute-start(bf16[1040,128]{1,0:T(8,128)(2,1)S(1)} %collective-permute-done.2.refs_3_), channel_id=1, source_target_pairs={{0,4},{4,0},{1,5},{5,1},{2,6},{6,2},{3,7},{7,3},{8,12},{12,8},{9,1... | collective-permute-start | bytes 798728 | tf_op jit(solution)/shard_map/ppermute | solution.py:253
  32.2 14.4 %all-to-all-start.1 = ((bf16[32,16,128]{2,1,0:T(8,128)(2,1)}), bf16[32,16,128]{2,1,0:T(8,128)(2,1)S(1)}, u32[]{:S(2)}, u32[]{:S(2)}) async-start(bf16[32,16,128]{2,1,0:T(8,128)(2,1)} %bitcast.2), calls=%async_computation.1 | async-start | bytes 262144 | tf_op jit(solution)/shard_map/all_to_all | solution.py:305
  46.6 0.7 copy-start.1

commit v5 on v4

--- a/solution.py
+++ b/solution.py
@@ -9,9 +9,10 @@
 from jax.experimental.pallas import tpu as pltpu
 from jax.sharding import Mesh, PartitionSpec as P
 
-Z, Y, XH, XL, C = 8, 4, 2, 2, 2
+ZZ, ZC, Y, XH, XL, C = 4, 2, 4, 2, 2, 2
 HEADS = XL * C
-PLANE = Z * HEADS
+SPREAD = ZZ * ZC
+PLANE = SPREAD * HEADS
 HOLD = Y * XH
 T, R, G, J, D = 2, 2, 2, 5, 128
 LIVE = R * T * J
@@ -20,14 +21,16 @@
 QUERIES = T * R * HEADS * G * J
 MESSAGE = HEADS * G * ROWS
 MASK = 4 * BLOCK
-PACK = MASK + 16
+OWN = MASK + 16
+OWN_ROWS = HEADS * R * T
+PACK = OWN + 2 * G * OWN_ROWS
 OWN_PART = 2 * G * R * T
-NEAR = HOLD * HEADS
 BLOCKS = ((0, 0), (3, 0), (1, 0), (2, 0), (0, 1), (3, 1), (1, 1), (2, 1))
 SOURCES = 16
 TILE = SOURCES * ROWS
 TILES = PLANE // SOURCES
 LOWEST = -1e30
+HIDE_FLOPS = int(3 * (1 << 30))
 LOG2E = math.log2(math.e)
 F32 = jnp.float32
 BF16 = jnp.bfloat16
@@ -41,11 +44,15 @@
     return hi, mid, lo
 
 
-def ctx_of(offset):
-    dy, dx = offset
+def device_of(zz, zc, y, xh, head):
+    return (((zz * ZC + zc) * Y + y) * XH + xh) * HEADS + head
+
+
+def place_of(offset):
+    dy, dxh = offset
     y = lax.rem(lax.axis_index("y") + dy, Y)
-    xh = lax.rem(lax.axis_index("xh") + dx, XH)
-    return (lax.axis_index("z") * Y + y) * XH + xh
+    xh = lax.rem(lax.axis_index("xh") + dxh, XH)
+    return device_of(lax.axis_index("zz"), lax.axis_index("zc"), y, xh, 0) // HEADS * BLOCK
 
 
 def row_parts():
@@ -54,23 +61,27 @@
     return source, lane - source * ROWS
 
 
-def fill_bias(reach_ref, kv_refs, bias_ref):
+def hide_kernel(reach_ref, *refs):
+    kv_refs, hide_ref = refs[:HOLD], refs[HOLD]
     lane = lax.broadcasted_iota(jnp.int32, (1, D), 1)
     sub = lax.broadcasted_iota(jnp.int32, (8, D), 0)
+    reach = jnp.where(sub == 0, reach_ref[0], reach_ref[1])
+    for b, (kv_ref, offset) in enumerate(zip(kv_refs, BLOCKS)):
+        first = place_of(offset)
+        mask = kv_ref[...].astype(F32)
+        for i in range(BLOCK // D):
+            seen = (mask[i : i + 1, :] > 0.5) & (first + i * D + lane < reach)
+            hide_ref[b, :, i * D : (i + 1) * D] = jnp.where(seen, 0.0, LOWEST)
+
+
+def fill_bias(hide_ref, bias_ref):
     _, within = row_parts()
     row_r = jnp.where(within >= T * J, 1, 0)
     pick = (lax.broadcasted_iota(jnp.int32, (8, TILE), 0) == row_r).astype(F32).astype(BF16)
-    for b, (kv_ref, offset) in enumerate(zip(kv_refs, BLOCKS)):
-        ctx = ctx_of(offset)
-        mask = kv_ref[MASK:PACK, :].astype(F32)
-        for i in range(BLOCK // D):
-            place = ctx * BLOCK + i * D + lane
-            reach = jnp.where(sub == 0, reach_ref[0], reach_ref[1])
-            seen = (mask[i : i + 1, :] > 0.5) & (place < reach)
-            hide = jnp.where(seen, 0.0, LOWEST).astype(BF16)
-            bias_ref[b, i * D : (i + 1) * D, :] = lax.dot_general(
-                hide, pick, (((0,), (0,)), ((), ())), preferred_element_type=F32
-            )
+    for b in range(HOLD):
+        bias_ref[b] = lax.dot_general(
+            hide_ref[b].astype(BF16), pick, (((0,), (0,)), ((), ())), preferred_element_type=F32
+        )
 
 
 def tile_queries(q_ref, tile, g):
@@ -134,28 +145,29 @@
     in_r = jnp.where(is_r1, within - T * J, within)
     row_r = jnp.where(is_r1, 1, 0)
     row_t = jnp.where(in_r >= J, 1, 0)
-    k = lax.broadcasted_iota(jnp.int32, (R * T * NEAR, 1), 0)
-    own_place = T * (lax.axis_index("z") * NEAR + (k & (NEAR - 1))) + ((k >> 5) & 1)
-    own_r = k >> 6
-    here = lax.axis_index("y") * XH + lax.axis_index("xh")
+    k = lax.broadcasted_iota(jnp.int32, (HOLD * OWN_ROWS, 1), 0)
+    own_place = T * ((k >> 2) & 3) + (k & 1)
+    for b, offset in enumerate(BLOCKS):
+        first = place_of(offset) // BLOCK * HEADS * T
+        own_place = own_place + jnp.where((k >> 4) == b, first, 0)
+    own_r = (k >> 1) & 1
+    zz, zc, y, xh = (lax.axis_index(name) for name in ("zz", "zc", "y", "xh"))
     from_source = tile * SOURCES + source
-    row_device = ((from_source >> 2) * HOLD + here) * HEADS + (from_source & 3)
+    row_device = device_of(from_source >> 3, (from_source >> 2) & 1, y, xh, from_source & 3)
     row_place = T * row_device + row_t
     return (own_r == row_r) & (own_place <= row_place)
 
 
-def own_part(own_rows, kind):
-    at = kind * R * T
-    parts = [own_rows[pl.ds(at + e, NEAR, stride=OWN_PART), :] for e in range(R * T)]
-    return jnp.concatenate(parts, axis=0).astype(BF16)
-
-
-def attend_kernel(reach_ref, q_ref, own_ref, *refs):
-    kv_refs, (out_ref, bias_ref, own_rows) = refs[:HOLD], refs[HOLD:]
-    fill_bias(reach_ref, kv_refs, bias_ref)
-    own_rows[...] = own_ref[...].astype(F32)
-    own_keys = [own_part(own_rows, g) for g in range(G)]
-    own_values = [own_part(own_rows, G + g) for g in range(G)]
+def own_part(kv_refs, kind):
+    at = OWN + kind * OWN_ROWS
+    return jnp.concatenate([ref[at : at + OWN_ROWS, :] for ref in kv_refs], axis=0)
+
+
+def attend_kernel(hide_ref, q_ref, *refs):
+    kv_refs, (out_ref, bias_ref) = refs[:HOLD], refs[HOLD:]
+    fill_bias(hide_ref, bias_ref)
+    own_keys = [own_part(kv_refs, g) for g in range(G)]
+    own_values = [own_part(kv_refs, G + g) for g in range(G)]
     scale = LOG2E / math.sqrt(D)
     for tile in range(TILES):
         seen = own_seen(tile)
@@ -193,7 +205,9 @@
             rows_ref[at : at + ROWS, :] = jnp.where(row[0] < LIVE, o, 0.0)
     rows = jnp.dot(order_ref[...], rows_ref[...].astype(BF16), preferred_element_type=F32)
     heads = HEADS * G * J
-    first = T * (ctx_of((0, 0)) * HEADS + lax.axis_index("xl") * C + lax.axis_index("c"))
+    names = ("zz", "zc", "y", "xh")
+    head = lax.axis_index("xl") * C + lax.axis_index("c")
+    first = T * device_of(*(lax.axis_index(name) for name in names), head)
     for t in range(T):
         for r in range(R):
             at = (t * R + r) * heads
@@ -226,27 +240,43 @@
     return order
 
 
-def message_kernel(order_ref, own_order_ref, q_ref, k_ref, v_ref, message_ref, own_ref):
+def own_kernel(own_order_ref, k_ref, v_ref, *refs):
+    own_refs, own_rows = refs[:HEADS], refs[HEADS]
+    own = [ref[...].astype(F32).reshape(T * R * HEADS * G, D) for ref in (k_ref, v_ref)]
+    own = jnp.concatenate(own, axis=0).astype(BF16)
+    own = jnp.dot(own_order_ref[...], own, preferred_element_type=F32)
+    own_rows[...] = own.reshape(HEADS, OWN_PART, D)
+    head = lax.axis_index("xl") * C + lax.axis_index("c")
+    for step, own_ref in enumerate(own_refs):
+        own_ref[...] = own_rows[lax.rem(head + step, HEADS)].astype(BF16)
+
+
+def message_kernel(order_ref, q_ref, message_ref):
     q = q_ref[...].astype(F32).reshape(QUERIES, D).astype(BF16)
     rows = jnp.dot(order_ref[...], q, preferred_element_type=F32).astype(BF16)
-    for z in range(Z):
-        message_ref[z] = rows
-    own = [ref[...].astype(F32).reshape(T * R * HEADS * G, D) for ref in (k_ref, v_ref)]
-    own = jnp.concatenate(own, axis=0).astype(BF16)
-    own = jnp.dot(own_order_ref[...], own, preferred_element_type=F32).astype(BF16)
-    for hold in range(HOLD):
-        own_ref[hold] = own
-
-
-def pack_kernel(mask_ref, k_ref, v_ref, pack_ref, wide, mask_rows):
+    for to in range(SPREAD):
+        message_ref[to] = rows
+
+
+def pack_kernel(mask_ref, k_ref, v_ref, *refs):
+    own_refs, (pack_ref, wide, by_head, sorted_rows) = refs[:HEADS], refs[HEADS:]
     for kv, ref in enumerate((k_ref, v_ref)):
         wide[kv] = ref[...].astype(F32)
         for g in range(G):
             at = (g * 2 + kv) * BLOCK
             pack_ref[at : at + BLOCK, :] = wide[kv, pl.ds(g, BLOCK, stride=G), :].astype(BF16)
-    mask_rows[...] = jnp.zeros_like(mask_rows)
-    mask_rows[0 : BLOCK // D, :] = mask_ref[...].astype(F32)
-    pack_ref[MASK:PACK, :] = mask_rows[...].astype(BF16)
+    head = lax.axis_index("xl") * C + lax.axis_index("c")
+    for step, own_ref in enumerate(own_refs):
+        by_head[lax.rem(head + HEADS - step, HEADS)] = own_ref[...].astype(F32)
+    part = T * R
+    for h in range(HEADS):
+        for kind in range(2 * G):
+            at = kind * OWN_ROWS + h * part
+            sorted_rows[at : at + part, :] = by_head[h, kind * part : (kind + 1) * part, :]
+    pack_ref[OWN:PACK, :] = sorted_rows[...].astype(BF16)
+    by_head[0] = jnp.zeros((OWN_PART, D), F32)
+    by_head[0, 0 : BLOCK // D, :] = mask_ref[...].astype(F32)
+    pack_ref[MASK:OWN, :] = by_head[0].astype(BF16)
 
 
 def permute(x, axis, size, shift):
@@ -263,66 +293,76 @@
     resp_lengths,
     prompt_reach,
 ):
-    plane = ("z", "xl", "c")
-    near = ("y", "xh", "xl", "c")
+    plane = ("zz", "zc", "xl", "c")
     smem = pl.BlockSpec(memory_space=pltpu.SMEM)
     vmem = pl.BlockSpec(memory_space=pltpu.VMEM)
     order = message_order()
+    own = pl.pallas_call(
+        own_kernel,
+        out_shape=[jax.ShapeDtypeStruct((OWN_PART, D), BF16)] * HEADS,
+        in_specs=[vmem] * 3,
+        out_specs=[vmem] * HEADS,
+        scratch_shapes=[pltpu.VMEM((HEADS, OWN_PART, D), F32)],
+        name="own",
+    )(jnp.asarray(own_order(), BF16), response_keys, response_values)
+    own = [own[0]] + [permute(own[step], ("xl", "c"), HEADS, step) for step in range(1, HEADS)]
+    message = pl.pallas_call(
+        message_kernel,
+        out_shape=jax.ShapeDtypeStruct((SPREAD, MESSAGE, D), BF16),
+        in_specs=[vmem] * 2,
+        out_specs=vmem,
+        name="message",
+    )(jnp.asarray(order, BF16), response_queries)
     kv = pl.pallas_call(
         pack_kernel,
         out_shape=jax.ShapeDtypeStruct((PACK, D), BF16),
-        in_specs=[vmem] * 3,
+        in_specs=[vmem] * (3 + HEADS),
         out_specs=vmem,
-        scratch_shapes=[pltpu.VMEM((2, G * BLOCK, D), F32), pltpu.VMEM((16, D), F32)],
+        scratch_shapes=[
+            pltpu.VMEM((2, G * BLOCK, D), F32),
+            pltpu.VMEM((HEADS, OWN_PART, D), F32),
+            pltpu.VMEM((HEADS * OWN_PART, D), F32),
+        ],
         name="pack",
     )(
         prompt_mask.reshape(BLOCK // D, D),
         prompt_keys.reshape(BLOCK * G, D),
         prompt_values.reshape(BLOCK * G, D),
+        *own,
     )
+    message, kv = lax.optimization_barrier((message, kv))
     across = permute(kv, "xh", XH, 1)
     far = permute(kv, "y", Y, 2)
     before = permute(kv, "y", Y, 1)
     after = permute(kv, "y", Y, 3)
-    message, own = pl.pallas_call(
-        message_kernel,
-        out_shape=[
-            jax.ShapeDtypeStruct((Z, MESSAGE, D), BF16),
-            jax.ShapeDtypeStruct((HOLD, HEADS * OWN_PART, D), BF16),
-        ],
-        in_specs=[vmem] * 5,
-        out_specs=[vmem] * 2,
-        name="message",
-    )(
-        jnp.asarray(order, BF16),
-        jnp.asarray(own_order(), BF16),
-        response_queries,
-        response_keys,
-        response_values,
-    )
     rows = lax.all_to_all(message.reshape(PLANE, G * ROWS, D), plane, 0, 0, tiled=True)
-    rows, own = lax.optimization_barrier((rows, own))
-    own = lax.all_to_all(own.reshape(NEAR, OWN_PART, D), near, 0, 0, tiled=True)
     across_before = permute(across, "y", Y, 1)
     across_after = permute(across, "y", Y, 3)
     across_far = permute(far, "xh", XH, 1)
     blocks = (kv, before, after, far, across, across_before, across_after, across_far)
+    hide = pl.pallas_call(
+        hide_kernel,
+        out_shape=jax.ShapeDtypeStruct((HOLD, 8, BLOCK), F32),
+        grid=(1,),
+        in_specs=[smem] + [pl.BlockSpec((OWN - MASK, D), lambda i: (MASK // 16, 0))] * HOLD,
+        out_specs=pl.BlockSpec((HOLD, 8, BLOCK), lambda i: (0, 0, 0)),
+        compiler_params=pltpu.CompilerParams(vmem_limit_bytes=4 << 20),
+        cost_estimate=pl.CostEstimate(flops=HIDE_FLOPS, bytes_accessed=1 << 20, transcendentals=0),
+        name="hide",
+    )(prompt_reach, *blocks)
     pair_flops = 4 * PLANE * G * ROWS * BLOCK * D
     partial = pl.pallas_call(
         attend_kernel,
         out_shape=jax.ShapeDtypeStruct((PLANE, G, ROWS, D), BF16),
-        in_specs=[smem] + [vmem] * (2 + HOLD),
+        in_specs=[vmem] * (2 + HOLD),
         out_specs=vmem,
-        scratch_shapes=[
-            pltpu.VMEM((HOLD, BLOCK, TILE), F32),
-            pltpu.VMEM((NEAR * OWN_PART, D), F32),
-        ],
+        scratch_shapes=[pltpu.VMEM((HOLD, BLOCK, TILE), F32)],
         compiler_params=pltpu.CompilerParams(vmem_limit_bytes=32 << 20),
         cost_estimate=pl.CostEstimate(
             flops=9 * pair_flops, bytes_accessed=4 << 20, transcendentals=9 * pair_flops // 512
         ),
         name="attend",
-    )(prompt_reach, rows.reshape(PLANE, G, ROWS, D), own.reshape(NEAR * OWN_PART, D), *blocks)
+    )(hide, rows.reshape(PLANE, G, ROWS, D), *blocks)
     partial = lax.all_to_all(partial.reshape(PLANE, G * ROWS, D), plane, 0, 0, tiled=True)
     return pl.pallas_call(
         combine_kernel,
@@ -331,12 +371,13 @@
         out_specs=vmem,
         scratch_shapes=[pltpu.VMEM((MESSAGE, D), F32)],
         name="combine",
-    )(resp_lengths, jnp.asarray(order.T, BF16), partial.reshape(Z, HEADS, G, ROWS, D))
+    )(resp_lengths, jnp.asarray(order.T, BF16), partial.reshape(SPREAD, HEADS, G, ROWS, D))
 
 
 def solution(mesh):
-    fine = Mesh(mesh.devices.reshape(Z, Y, XH, XL, C), ("z", "y", "xh", "xl", "c"))
-    ctx, head = ("z", "y", "xh"), ("xl", "c")
+    names = ("zz", "zc", "y", "xh", "xl", "c")
+    fine = Mesh(mesh.devices.reshape(ZZ, ZC, Y, XH, XL, C), names)
+    ctx, head = names[:4], names[4:]
     return jax.shard_map(
         per_device,
         mesh=fine,

time: 76.1 us -> 72.8 us (0.957)
  starting transfers between devices: 30.2 us -> 22.7 us
  blocking collectives: 19.9 us -> 22.9 us
  Pallas kernels: 12.1 us -> 13.6 us
    all_to_all x1 -> x0, waiting for transfers between devices: 7.57 us -> none  [per_device(): own = lax.all_to_all(own.reshape(NEAR, OWN_PART, D), near, 0, 0, tiled=True)]
    ppermute x7 -> x10, waiting for transfers between devices: 5.14 us -> 12.4 us  [permute(): return lax.ppermute(x, axis, [(i, (i + shift) % size) for i in range(size)])]
    all_to_all x1 -> x0, starting transfers between devices: 6.81 us -> none  [per_device(): own = lax.all_to_all(own.reshape(NEAR, OWN_PART, D), near, 0, 0, tiled=True)]
    all_to_all x1, blocking collectives: 19.9 us -> 22.9 us  [per_device(): lax.all_to_all(partial.reshape(PLANE, G * ROWS, D), plane, 0, 0, tiled=True)]
    pallas_call x1 -> x3, Pallas kernels: 1.92 us -> 3.91 us  [the longest x1 1.82 us: per_device(): pl.pallas_call(message_kernel, out_shape=jax.ShapeDtypeStruct((SPREAD, ME...]
    all_to_all x1, starting transfers between devices: 11.1 us -> 9.46 us  [per_device(): lax.all_to_all(message.reshape(PLANE, G * ROWS, D), plane, 0, 0, tiled=True)]
    ppermute x7 -> x10, starting transfers between devices: 12.3 us -> 13.2 us  [permute(): return lax.ppermute(x, axis, [(i, (i + shift) % size) for i in range(size)])]
  transfers between devices with their start and end apart: 9 -> 11, of which waited for: 2 -> 5; matrix products, arithmetic and copies ran while one was open for 0% -> 0% of each run, Pallas kernels for 2% -> 3%
where the time goes in v5:
time: 72.8 us; the launch traced here: 72.3 us
  blocking collectives  22.9 us (31%)
  starting transfers between devices  22.7 us (31%)
  Pallas kernels  13.6 us (19%)
  waiting for transfers between devices  12.4 us (17%)
    all_to_all x1, blocking collectives, per_device(): lax.all_to_all(partial.reshape(PLANE, G * ROWS, D), plane, 0, 0, tiled=True)  22.9 us
    ppermute x10, starting transfers between devices, permute(): return lax.ppermute(x, axis, [(i, (i + shift) % size) for i in range(size)])  13.2 us
    ppermute x10, waiting for transfers between devices, permute(): return lax.ppermute(x, axis, [(i, (i + shift) % size) for i in range(size)])  12.4 us
    all_to_all x1, starting transfers between devices, per_device(): lax.all_to_all(message.reshape(PLANE, G * ROWS, D), plane, 0, 0, tiled=True)  9.46 us
    pallas_call x1, Pallas kernels, per_device(): pl.pallas_call(attend_kernel, out_shape=jax.ShapeDtypeStruct((PLANE, G, R...  5.72 us
    pallas_call x1, Pallas kernels, per_device(): pl.pallas_call(combine_kernel, out_shape=jax.ShapeDtypeStruct((T, R, HEAD...  2.13 us
    pallas_call x1, Pallas kernels, per_device(): pl.pallas_call(message_kernel, out_shape=jax.ShapeDtypeStruct((SPREAD, ME...  1.82 us
    pallas_call x1, Pallas kernels, per_device(): pl.pallas_call(pack_kernel, out_shape=jax.ShapeDtypeStruct((PACK, D), BF1...  1.8 us
  transfers between devices with their start and end apart: 11, of which 5 were waited for; matrix products, arithmetic and copies ran while one was open for 0% of the time, Pallas kernels for 3%

profile of v5, /device:TPU:1, one launch (start us, length us, event | category | flops | bytes accessed | tf_op | source)
XLA Modules:
  0.0 72.3 jit_solution(1602947681760034697)
XLA Ops:
  0.0 1.5 %own.1 = (bf16[16,128]{1,0:T(8,128)(2,1)}, bf16[16,128]{1,0:T(8,128)(2,1)}, bf16[16,128]{1,0:T(8,128)(2,1)}, bf16[16,128]{1,0:T(8,128)(2,1)}) custom-call(bf16[64,64]{1,0:T(8,128)(2,1)} %constant.6.clone.own_order_ref, bf16[2,2,8,128]{3,2,1,0:T(8,128)(2,1)} %k_ref.1, bf16[2,2,8,128]{3,2,1,0:T(8,128)(2,1)} %v_ref.1), custom_call_target="tpu_custom_call" | custom-call | tf_op jit(solution)/shard_map/own/pallas_call | solution.py:300
  1.5 2.6 %collective-permute-start = (bf16[16,128]{1,0:T(8,128)(2,1)}, bf16[16,128]{1,0:T(8,128)(2,1)S(1)}, u32[]{:S(2)}, u32[]{:S(2)}) collective-permute-start(bf16[16,128]{1,0:T(8,128)(2,1)} %get-tuple-element.12), channel_id=1, source_target_pairs={{0,1},{1,2},{2,3},{3,0},{4,5},{5,6},{6,7},{7,4},{8,9},{9,10},{10,1... | collective-permute-start | bytes 12296 | tf_op jit(solution)/shard_map/ppermute | solution.py:283
  4.1 2.0 %collective-permute-start.1 = (bf16[16,128]{1,0:T(8,128)(2,1)}, bf16[16,128]{1,0:T(8,128)(2,1)S(1)}, u32[]{:S(2)}, u32[]{:S(2)}) collective-permute-start(bf16[16,128]{1,0:T(8,128)(2,1)} %get-tuple-element.13), channel_id=1, source_target_pairs={{0,2},{1,3},{2,0},{3,1},{4,6},{5,7},{6,4},{7,5},{8,10},{9,11},{10,... | collective-permute-start | bytes 12296 | tf_op jit(solution)/shard_map/ppermute | solution.py:283
  6.1 1.8 %message.1 = bf16[8,192,128]{2,1,0:T(8,128)(2,1)} custom-call(bf16[192,160]{1,0:T(8,128)(2,1)} %constant.7.clone.order_ref, bf16[2,2,40,128]{3,2,1,0:T(8,128)(2,1)} %q_ref.1), custom_call_target="tpu_custom_call" | custom-call | tf_op jit(solution)/shard_map/message/pallas_call | solution.py:309
  7.9 0.0 collective-permute-done.refs_1_
  7.9 0.0 collective-permute-done.1.refs_2_
  7.9 1.2 %collective-permute-done.2.refs_3_ = bf16[16,128]{1,0:T(8,128)(2,1)S(1)} collective-permute-done((bf16[16,128]{1,0:T(8,128)(2,1)S(1)}, bf16[16,128]{1,0:T(8,128)(2,1)S(1)}, u32[]{:S(2)}, u32[]{:S(2)}) %collective-permute-start.2) | collective-permute-done | bytes 4128 | tf_op jit(solution)/shard_map/ppermute | solution.py:283
  9.1 0.6 copy-done.4
  9.7 1.8 %pack.1.refs_0_ = bf16[1104,128]{1,0:T(8,128)(2,1)} custom-call(s32[2,128]{1,0:T(2,128)} %bitcast.12, bf16[512,128]{1,0:T(8,128)(2,1)} %bitcast.10, bf16[512,128]{1,0:T(8,128)(2,1)} %bitcast.11, bf16[16,128]{1,0:T(8,128)(2,1)} %get-tuple-element.11.refs_0_, bf16[16,128]{1,0:T(8,128)(2,1)} %copy-done.2, bf16[16,128]{1,0:T(8,128)(2,1)} %copy-done.3, ...), custom_call_target="tpu_custom_call" | custom-call | tf_op jit(solution)/shard_map/pack/pallas_call | solution.py:316
  11.5 1.0 %collective-permute-start.6 = (bf16[1104,128]{1,0:T(8,128)(2,1)}, bf16[1104,128]{1,0:T(8,128)(2,1)S(1)}, u32[]{:S(2)}, u32[]{:S(2)}) collective-permute-start(bf16[1104,128]{1,0:T(8,128)(2,1)} %pack.1.refs_0_), channel_id=1, source_target_pairs={{0,4},{4,0},{1,5},{5,1},{2,6},{6,2},{3,7},{7,3},{8,12},{12,8},{9,1... | collective-permute-start | bytes 847880 | tf_op jit(solution)/shard_map/ppermute | solution.py:283
  12.5 2.9 %collective-permute-start.5 = (bf16[1104,128]{1,0:T(8,128)(2,1)}, bf16[1104,128]{1,0:T(8,128)(2,1)S(1)}, u32[]{:S(2)}, u32[]{:S(2)}) collective-permute-start(bf16[1104,128]{1,0:T(8,128)(2,1)} %pack.1.refs_0_), channel_id=1, source_target_pairs={{0,16},{8,24},{16,0},{24,8},{1,17},{9,25},{17,1},{25,9},{2,18},{10... | collective-permute-start | bytes 847880 | tf_op jit(solution)/shard_map/ppermute | solution.py:283
  15.4 9.5 %all-to-all-start = ((bf16[32,48,128]{2,1,0:T(8,128)(2,1)}), bf16[32,48,128]{2,1,0:T(8,128)(2,1)S(1)}, u32[]{:S(2)}, u32[]{:S(2)}) async-start(bf16[32,48,128]{2,1,0:T(8,128)(2,1)} %bitcast.3), calls=%async_computation | async-start | bytes 786432 | tf_op jit(solution)/shard_map/all_to_all | solution.py:338
  24.9 0.9 %collective-permute-start.4 = (bf16[1104,128]{1,0:T(8,128)(2,1)S(1)}, bf16[1104,128]{1,0:T(8,128)(2,1)S(1)}, u32[]{:S(2)}, u32[]{:S(2)}) collective-permute-start(bf16[1104,128]{1,0:T(8,128)(2,1)S(1)} %copy-done), channel_id=1, source_target_pairs={{0,24},{8,0},{16,8},{24,16},{1,25},{9,1},{17,9},{25,17},{2,26},{10... | collective-permute-start | bytes 847880 | tf_op jit(solution)/shard_map/ppermute | solution.py:283
  25.8 0.7 collective-permute-start.3
  26.4 2.0 %collective-permute-start.8 = (bf16[1104,128]{1,0:T(8,128)(2,1)S(1)}, bf16[1104,128]{1,0:T(8,128)(2,1)S(1)}, u32[]{:S(2)}, u32[]{:S(2)}) collective-permute-start(bf16[1104,128]{1,0:T(8,128)(2,1)S(1)} %collective-permute-done.6.refs_4_), channel_id=1, source_target_pairs={{0,24},{8,0},{16,8},{24,16},{1,25},{9,1},{17,9},{25,17},{2,26},{10... | collective-permute-start | bytes 847880 | tf_op jit(solution)/shard_map/ppermute | solution.py:283
  28.4 1.2 %collective-permute-start.9 = (bf16[1104,128]{1,0:T(8,128)(2,1)S(1)}, bf16[1104,128]{1,0:T(8,128)(2,1)S(1)}, u32[]{:S(2)}, u32[]{:S(2)}) collective-permute-start(bf16[1104,128]{1,0:T(8,128)(2,1)S(1)} %collective-permute-done.5.refs_3_), channel_id=1, source_target_pairs={{0,4},{4,0},{1,5},{5,1},{2,6},{6,2},{3,7},{7,3},{8,12},{12,8},{9,1... | collective-permute-start | bytes 847880 | tf_op jit(solution)/shard_map/ppermute | solution.py:283
  29.6 3.5 %collective-permute-done.4.refs_2_ = bf16[1104,128]{1,0:T(8,128)(2,1)S(1)} collective-permute-done((bf16[1104,128]{1,0:T(8,128)(2,1)S(1)}, bf16[1104,128]{1,0:T(8,128)(2,1)S(1)}, u32[]{:S(2)}, u32[]{:S(2)}) %collective-permute-start.4) | collective-permute-done | bytes 282656 | tf_op jit(solution)/shard_map/ppermute | solution.py:283
  33.1 1.7 %collective-permute-done.3.refs_1_ = bf16[1104,128]{1,0:T(8,128)(2,1)S(1)} collective-permute-done((bf16[1104,128]{1,0:T(8,128)(2,1)S(1)}, bf16[1104,128]{1,0:T(8,128)(2,1)S(1)}, u32[]{:S(2)}, u32[]{:S(2)}) %collective-permute-start.3) | collective-permute-done | bytes 282656 | tf_op jit(solution)/shard_map/ppermute | solution.py:283
  34.8 4.4 %collective-permute-done.8.refs_6_ = bf16[1104,128]{1,0:T(8,128)(2,1)S(1)} collective-permute-done((bf16[1104,128]{1,0:T(8,128)(2,1)S(1)}, bf16[1104,128]{1,0:T(8,128)(2,1)S(1)}, u32[]{:S(2)}, u32[]{:S(2)}) %collective-permute-start.8) | collective-permute-done | bytes 282656 | tf_op jit(solution)/shard_map/ppermute | solution.py:283
  39.1 1.7 %collective-permute-done.7.refs_5_ = bf16[1104,128]{1,0:T(8,128)(2,1)S(1)} collective-permute-done((bf16[1104,128]{1,0:T(8,128)(2,1)S(1)}, bf16[1104,128]{1,0:T(8,128)(2,1)S(1)}, u32[]{:S(2)}, u32[]{:S(2)}) %collective-permute-start.7) | collective-permute-done | bytes 282656 | tf_op jit(solution)/shard_map/ppermute | solution.py:283
  40.8 0.6 hide.1.hide_ref
  41.5 5.7 %attend.1 = bf16[32,2,24,128]{3,2,1,0:T(8,128)(2,1)S(1)} custom-call(f32[8,8,256]{2,1,0:T(8,128)S(1)} %hide.1.hide_ref, bf16[32,2,24,128]{3,2,1,0:T(8,128)(2,1)S(1)} %bitcast.7, bf16[1104,128]{1,0:T(8,128)(2,1)S(1)} %copy-done, bf16[1104,128]{1,0:T(8,128)(2,1)S(1)} %collective-permute-done.3.refs_1_, bf16[1104,128]{1,0:T(8,128)(2,1)S(1)} %collective-permute-done.4.refs_2_, ...), custom_call_target="tpu_custom_call" | custom-call | flops 1811939328 | bytes 4194304 | tf_op jit(solution)/shard_map/attend/pallas_call | solution.py:354
  47.2 22.9 %all_to_all.10 = bf16[32,48,128]{2,1,0:T(8,128)(2,1)} all-to-all(bf16[32,48,128]{2,1,0:T(8,128)(2,1)S(1)} %bitcast.8), channel_id=1, replica_groups=mesh['zz'=4,'zc'=2,'y'=4,'xh'=2,'xl'=2,'c'=2] {'zz','zc','xl','c'}, dimensions={0} | all-to-all | bytes 786432 | tf_op jit(solution)/shard_map/all_to_all | solution.py:366
  70.1 2.1 %combine.1 = bf16[2,2,40,128]{3,2,1,0:T(8,128)(2,1)} custom-call(s32[2]{0:T(128)} %lengths_ref.1, bf16[160,192]{1,0:T(8,128)(2,1)} %constant.8.clone.order_ref, bf16[8,4,2,24,128]{4,3,2,1,0:T(8,128)(2,1)} %bitcast.9), custom_call_target="tpu_custom_call" | custom-call | tf_op jit(solution)/shard_map/combine/pallas_call | solution.py:367
  (17 shorter events, 0.0 us)
Async XLA Ops:
  1.5 4.6 %copy-start.5 = (bf16[16,128]{1,0:T(8,128)(2,1)S(1)}, bf16[16,128]{1,0:T(8,128)(2,1)}, u32[]{:S(2)}) copy-start(bf16[16,128]{1,0:T(8,128)(2,1)} %get-tuple-element.14) | copy-start | bytes 12292
  1.5 6.4 %collective-permute-start = (bf16[16,128]{1,0:T(8,128)(2,1)}, bf16[16,128]{1,0:T(8,128)(2,1)S(1)}, u32[]{:S(2)}, u32[]{:S(2)}) collective-permute-start(bf16[16,128]{1,0:T(8,128)(2,1)} %get-tuple-element.12), channel_id=1, source_target_pairs={{0,1},{1,2},{2,3},{3,0},{4,5},{5,6},{6,7},{7,4},{8,9},{9,10},{10,1... | collective-permute-start | bytes 12296 | tf_op jit(solution)/shard_map/ppermute | solution.py:283
  4.1 3.8 %collective-permute-start.1 = (bf16[16,128]{1,0:T(8,128)(2,1)}, bf16[16,128]{1,0:T(8,128)(2,1)S(1)}, u32[]{:S(2)}, u32[]{:S(2)}) collective-permute-start(bf16[16,128]{1,0:T(8,128)(2,1)} %get-tuple-element.13), channel_id=1, source_target_pairs={{0,2},{1,3},{2,0},{3,1},{4,6},{5,7},{6,4},{7,5},{8,10},{9,11},{10,... | collective-permute-start | bytes 12296 | tf_op jit(solution)/shard_map/ppermute | solution.py:283
  6.1 3.0 %collective-permute-start.2 = (bf16[16,128]{1,0:T(8,128)(2,1)S(1)}, bf16[16,128]{1,0:T(8,128)(2,1)S(1)}, u32[]{:S(2)}, u32[]{:S(2)}) collective-permute-start(bf16[16,128]{1,0:T(8,128)(2,1)S(1)} %copy-done.5), channel_id=1, source_target_pairs={{0,3},{1,0},{2,1},{3,2},{4,7},{5,4},{6,5},{7,6},{8,11},{9,8},{10,9... | collective-permute-start | bytes 12296 | tf_op jit(solution)/shard_map/ppermute | solution.py:283
  7.9 1.2 %copy-start.2 = (bf16[16,128]{1,0:T(8,128)(2,1)}, bf16[16,128]{1,0:T(8,128)(2,1)S(1)}, u32[]{:S(2)}) copy-start(bf16[16,128]{1,0:T(8,128)(2,1)S(1)} %collective-permute-done.refs_1_) | copy-start | bytes 12292
  7.9 1.2 %copy-start.3 = (bf16[16,128]{1,0:T(8,128)(2,1)}, bf16[16,128]{1,0:T(8,128)(2,1)S(1)}, u32[]{:S(2)}) copy-start(bf16[16,128]{1,0:T(8,128)(2,1)S(1)} %collective-permute-done.1.refs_2_) | copy-start | bytes 12292
  9.1 0.6 copy-start.4
  11.5 15.0 %collective-permute-start.6 = (bf16[1104,128]{1,0:T(8,128)(2,1)}, bf16[1104,128]{1,0:T(8,128)(2,1)S(1)}, u32[]{:S(2)}, u32[]{:S(2)}) collective-permute-start(bf16[1104,128]{1,0:T(8,128)(2,1)} %pack.1.refs_0_), channel_id=1, source_target_pairs={{0,4},{4,0},{1,5},{5,1},{2,6},{6,2},{3,7},{7,3},{8,12},{12,8},{9,1... | collective-permute-start | bytes 847880 | tf_op jit(solution)/shard_map/ppermute | solution.py:283
  12.5 15.9 %collective-permute-start.5 = (bf16[1104,128]{1,0:T(8,128)(2,1)}, bf16[1104,128]{1,0:T(8,128)(2,1)S(1)}, u32[]{:S(2)}, u32[]{:S(2)}) collective-permute-start(bf16[1104,128]{1,0:T(8,128)(2,1)} %pack.1.refs_0_), channel_id=1, source_target_pairs={{0,16},{8,24},{16,0},{24,8},{1,17},{9,25},{17,1},{25,9},{2,18},{10... | collective-permute-start | bytes 847880 | tf_op jit(solution)/shard_map/ppermute | solution.py:283
  15.4 9.5 %copy-start = (bf16[1104,128]{1,0:T(8,128)(2,1)S(1)}, bf16[1104,128]{1,0:T(8,128)(2,1)}, u32[]{:S(2)}) copy-start(bf16[1104,128]{1,0:T(8,128)(2,1)} %pack.1.refs_0_) | copy-start | bytes 847876
  15.4 25.4 %copy-start.1 = (s32[2]{0:T(128)S(1)}, s32[2]{0:T(128)}, u32[]{:S(2)}) copy-start(s32[2]{0:T(128)} %reach_ref.1) | copy-start | bytes 28
  15.4 26.0 %all-to-all-start = ((bf16[32,48,128]{2,1,0:T(8,128)(2,1)}), bf16[32,48,128]{2,1,0:T(8,128)(2,1)S(1)}, u32[]{:S(2)}, u32[]{:S(2)}) async-start(bf16[32,48,128]{2,1,0:T(8,128)(2,1)} %bitcast.3), calls=%async_computation | async-start | bytes 786432 | tf_op jit(solution)/shard_map/all_to_all | solution.py:338
  24.9 8.2 %collective-permute-start.4 = (bf16[1104,128]{1,0:T(8,128)(2,1)S(1)}, bf16[1104,128]{1,0:T(8,128)(2,1)S(1)}, u32[]{:S(2)}, u32[]{:S(2)}) collective-permute-start(bf16[1104,128]{1,0:T(8,128)(2,1)S(1)} %copy-done), channel_id=1, source_target_pairs={{0,24},{8,0},{16,8},{24,16},{1,25},{9,1},{17,9},{25,17},{2,26},{10... | collective-permute-start | bytes 847880 | tf_op jit(solution)/shard_map/ppermute | solution.py:283
  25.8 9.0 %collective-permute-start.3 = (bf16[1104,128]{1,0:T(8,128)(2,1)S(1)}, bf16[1104,128]{1,0:T(8,128)(2,1)S(1)}, u32[]{:S(2)}, u32[]{:S(2)}) collective-permute-start(bf16[1104,128]{1,0:T(8,128)(2,1)S(1)} %copy-done), channel_id=1, source_target_pairs={{0,8},{8,16},{16,24},{24,0},{1,9},{9,17},{17,25},{25,1},{2,10},{10... | collective-permute-start | bytes 847880 | tf_op jit(solution)/shard_map/ppermute | solution.py:283
  26.4 12.7 %collective-permute-start.8 = (bf16[1104,128]{1,0:T(8,128)(2,1)S(1)}, bf16[1104,128]{1,0:T(8,128)(2,1)S(1)}, u32[]{:S(2)}, u32[]{:S(2)}) collective-permute-start(bf16[1104,128]{1,0:T(8,128)(2,1)S(1)} %collective-permute-done.6.refs_4_), channel_id=1, source_target_pairs={{0,24},{8,0},{16,8},{24,16},{1,25},{9,1},{17,9},{25,17},{2,26},{10... | collective-permute-start | bytes 847880 | tf_op jit(solution)/shard_map/ppermute | solution.py:283
  28.4 12.4 %collective-permute-start.7 = (bf16[1104,128]{1,0:T(8,128)(2,1)S(1)}, bf16[1104,128]{1,0:T(8,128)(2,1)S(1)}, u32[]{:S(2)}, u32[]{:S(2)}) collective-permute-start(bf16[1104,128]{1,0:T(8,128)(2,1)S(1)} %collective-permute-done.6.refs_4_), channel_id=1, source_target_pairs={{0,8},{8,16},{16,24},{24,0},{1,9},{9,17},{17,25},{25,1},{2,10},{10... | collective-permute-start | bytes 847880 | tf_op jit(solution)/shard_map/ppermute | solution.py:283
  28.4 12.4 %collective-permute-start.9 = (bf16[1104,128]{1,0:T(8,128)(2,1)S(1)}, bf16[1104,128]{1,0:T(8,128)(2,1)S(1)}, u32[]{:S(2)}, u32[]{:S(2)}) collective-permute-start(bf16[1104,128]{1,0:T(8,128)(2,1)S(1)} %collective-permute-done.5.refs_3_), channel_id=1, source_target_pairs={{0,4},{4,0},{1,5},{5,1},{2,6},{6,2},{3,7},{7,3},{8,12},{12,8},{9,1... | collective-permute-start | bytes 847880 | tf_op jit(solution)/shard_map/ppermute | solution.py:283

commit v6 on v5

--- a/solution.py
+++ b/solution.py
@@ -30,7 +30,9 @@
 TILE = SOURCES * ROWS
 TILES = PLANE // SOURCES
 LOWEST = -1e30
-HIDE_FLOPS = int(3 * (1 << 30))
+HIDE_FLOPS = int(6 * (1 << 30))
+FIRST_FLOPS = int(1 * (1 << 30))
+EARLY = 5
 LOG2E = math.log2(math.e)
 F32 = jnp.float32
 BF16 = jnp.bfloat16
@@ -61,27 +63,31 @@
     return source, lane - source * ROWS
 
 
-def hide_kernel(reach_ref, *refs):
-    kv_refs, hide_ref = refs[:HOLD], refs[HOLD]
+def hide_rows(reach_ref, mask, offset):
     lane = lax.broadcasted_iota(jnp.int32, (1, D), 1)
     sub = lax.broadcasted_iota(jnp.int32, (8, D), 0)
     reach = jnp.where(sub == 0, reach_ref[0], reach_ref[1])
-    for b, (kv_ref, offset) in enumerate(zip(kv_refs, BLOCKS)):
-        first = place_of(offset)
-        mask = kv_ref[...].astype(F32)
-        for i in range(BLOCK // D):
-            seen = (mask[i : i + 1, :] > 0.5) & (first + i * D + lane < reach)
-            hide_ref[b, :, i * D : (i + 1) * D] = jnp.where(seen, 0.0, LOWEST)
-
-
-def fill_bias(hide_ref, bias_ref):
+    first = place_of(offset)
+    parts = []
+    for i in range(BLOCK // D):
+        seen = (mask[i : i + 1, :] > 0.5) & (first + i * D + lane < reach)
+        parts.append(jnp.where(seen, 0.0, LOWEST))
+    return jnp.concatenate(parts, axis=1)
+
+
+def hide_kernel(reach_ref, *refs):
+    mask_refs, hide_ref = refs[:-1], refs[-1]
+    for b, mask_ref in enumerate(mask_refs):
+        hide_ref[b] = hide_rows(reach_ref, mask_ref[...].astype(F32), BLOCKS[b])
+
+
+def bias_of(hide):
     _, within = row_parts()
     row_r = jnp.where(within >= T * J, 1, 0)
     pick = (lax.broadcasted_iota(jnp.int32, (8, TILE), 0) == row_r).astype(F32).astype(BF16)
-    for b in range(HOLD):
-        bias_ref[b] = lax.dot_general(
-            hide_ref[b].astype(BF16), pick, (((0,), (0,)), ((), ())), preferred_element_type=F32
-        )
+    return lax.dot_general(
+        hide.astype(BF16), pick, (((0,), (0,)), ((), ())), preferred_element_type=F32
+    )
 
 
 def tile_queries(q_ref, tile, g):
@@ -163,11 +169,29 @@
     return jnp.concatenate([ref[at : at + OWN_ROWS, :] for ref in kv_refs], axis=0)
 
 
-def attend_kernel(hide_ref, q_ref, *refs):
-    kv_refs, (out_ref, bias_ref) = refs[:HOLD], refs[HOLD:]
-    fill_bias(hide_ref, bias_ref)
-    own_keys = [own_part(kv_refs, g) for g in range(G)]
-    own_values = [own_part(kv_refs, G + g) for g in range(G)]
+def first_kernel(hide_ref, q_ref, *refs):
+    kv_refs, (acc_ref, stat_ref, bias_ref) = refs[:EARLY], refs[EARLY:]
+    for b in range(EARLY):
+        bias_ref[b] = bias_of(hide_ref[b])
+    for g in range(G):
+        for tile in range(TILES):
+            q = tile_queries(q_ref, tile, g)
+            scores = block_scores(q, kv_refs, g, bias_ref)
+            top = top_of(scores)
+            total, summed = weigh(scores, block_values(kv_refs, g), top)
+            acc_ref[tile, g] = summed
+            stat_ref[tile, g, 0:1, :] = top
+            stat_ref[tile, g, 1:2, :] = total
+
+
+def second_kernel(reach_ref, q_ref, *refs):
+    all_refs, (acc_ref, stat_ref, out_ref, bias_ref) = refs[:HOLD], refs[HOLD:]
+    kv_refs = all_refs[EARLY:]
+    for b, kv_ref in enumerate(kv_refs):
+        mask = kv_ref[MASK:OWN, :].astype(F32)
+        bias_ref[b] = bias_of(hide_rows(reach_ref, mask, BLOCKS[EARLY + b]))
+    own_keys = [own_part(all_refs, g) for g in range(G)]
+    own_values = [own_part(all_refs, G + g) for g in range(G)]
     scale = LOG2E / math.sqrt(D)
     for tile in range(TILES):
         seen = own_seen(tile)
@@ -177,10 +201,15 @@
             scores = block_scores(q, kv_refs, g, bias_ref)
             so = lax.dot_general(own_keys[g], q, CONTRACT_LAST, preferred_element_type=F32)
             so = jnp.where(seen, so, LOWEST)
+            before = stat_ref[tile, g]
+            top_before, total_before = before[0:1, :], before[1:2, :]
             top = jnp.maximum(top_of(scores), jnp.max(so, axis=0, keepdims=True))
+            top = jnp.maximum(top, top_before)
             values = block_values(kv_refs, g) + [own_values[g]]
             total, summed = weigh(scores + [so], values, top)
-            summed = summed * (1.0 / total)
+            shrink = jnp.exp2((top_before - top) * scale)
+            total = total + total_before * shrink
+            summed = (summed + acc_ref[tile, g] * shrink) * (1.0 / total)
             outs.append(jnp.transpose(summed).reshape(SOURCES, ROWS, D))
             lse.append(top * scale + jnp.log2(total))
         finish(outs, lse, tile, out_ref)
@@ -342,27 +371,39 @@
     blocks = (kv, before, after, far, across, across_before, across_after, across_far)
     hide = pl.pallas_call(
         hide_kernel,
-        out_shape=jax.ShapeDtypeStruct((HOLD, 8, BLOCK), F32),
+        out_shape=jax.ShapeDtypeStruct((EARLY, 8, BLOCK), F32),
         grid=(1,),
-        in_specs=[smem] + [pl.BlockSpec((OWN - MASK, D), lambda i: (MASK // 16, 0))] * HOLD,
-        out_specs=pl.BlockSpec((HOLD, 8, BLOCK), lambda i: (0, 0, 0)),
+        in_specs=[smem]
+        + [pl.BlockSpec((OWN - MASK, D), lambda i: (MASK // 16, 0))] * (EARLY),
+        out_specs=pl.BlockSpec((EARLY, 8, BLOCK), lambda i: (0, 0, 0)),
         compiler_params=pltpu.CompilerParams(vmem_limit_bytes=4 << 20),
         cost_estimate=pl.CostEstimate(flops=HIDE_FLOPS, bytes_accessed=1 << 20, transcendentals=0),
         name="hide",
-    )(prompt_reach, *blocks)
-    pair_flops = 4 * PLANE * G * ROWS * BLOCK * D
+    )(prompt_reach, *blocks[:EARLY])
+    rows = rows.reshape(PLANE, G, ROWS, D)
+    acc, stat = pl.pallas_call(
+        first_kernel,
+        out_shape=[
+            jax.ShapeDtypeStruct((TILES, G, D, TILE), F32),
+            jax.ShapeDtypeStruct((TILES, G, 8, TILE), F32),
+        ],
+        in_specs=[vmem] * (2 + EARLY),
+        out_specs=[vmem] * 2,
+        scratch_shapes=[pltpu.VMEM((EARLY, BLOCK, TILE), F32)],
+        compiler_params=pltpu.CompilerParams(vmem_limit_bytes=24 << 20),
+        cost_estimate=pl.CostEstimate(flops=FIRST_FLOPS, bytes_accessed=2 << 20, transcendentals=0),
+        name="attend_first",
+    )(hide, rows, *blocks[:EARLY])
     partial = pl.pallas_call(
-        attend_kernel,
+        second_kernel,
         out_shape=jax.ShapeDtypeStruct((PLANE, G, ROWS, D), BF16),
-        in_specs=[vmem] * (2 + HOLD),
+        in_specs=[smem] + [vmem] * (3 + HOLD),
         out_specs=vmem,
-        scratch_shapes=[pltpu.VMEM((HOLD, BLOCK, TILE), F32)],
-        compiler_params=pltpu.CompilerParams(vmem_limit_bytes=32 << 20),
-        cost_estimate=pl.CostEstimate(
-            flops=9 * pair_flops, bytes_accessed=4 << 20, transcendentals=9 * pair_flops // 512
-        ),
-        name="attend",
-    )(hide, rows.reshape(PLANE, G, ROWS, D), *blocks)
+        scratch_shapes=[pltpu.VMEM((HOLD - EARLY, BLOCK, TILE), F32)],
+        compiler_params=pltpu.CompilerParams(vmem_limit_bytes=24 << 20),
+        cost_estimate=pl.CostEstimate(flops=2 << 30, bytes_accessed=3 << 20, transcendentals=0),
+        name="attend_second",
+    )(prompt_reach, rows, *blocks, acc, stat)
     partial = lax.all_to_all(partial.reshape(PLANE, G * ROWS, D), plane, 0, 0, tiled=True)
     return pl.pallas_call(
         combine_kernel,

time: 72.8 us -> 70.2 us (0.964)
  blocking collectives: 22.9 us -> 18.9 us
  Pallas kernels: 13.6 us -> 15.8 us
  waiting for transfers between devices: 12.4 us -> 11.1 us
    ppermute x10, waiting for transfers between devices: 12.4 us -> 1.22 us  [permute(): return lax.ppermute(x, axis, [(i, (i + shift) % size) for i in range(size)])]
    all_to_all x1, waiting for transfers between devices: 0.01 us -> 9.91 us  [per_device(): lax.all_to_all(message.reshape(PLANE, G * ROWS, D), plane, 0, 0, tiled=True)]
    all_to_all x1, blocking collectives: 22.9 us -> 18.9 us  [per_device(): lax.all_to_all(partial.reshape(PLANE, G * ROWS, D), plane, 0, 0, tiled=True)]
    pallas_call x2 -> x3, Pallas kernels: 6.34 us -> 8.58 us  [the longest x1 4.07 us: per_device(): pl.pallas_call(first_kernel, out_shape=[jax.ShapeDtypeStruct((TILES, G, D...]
  transfers between devices with their start and end apart: 11 -> 11, of which waited for: 5 -> 2; matrix products, arithmetic and copies ran while one was open for 0% -> 0% of each run, Pallas kernels for 3% -> 9%
where the time goes in v6:
time: 70.2 us; the launch traced here: 69.7 us
  starting transfers between devices  23.2 us (33%)
  blocking collectives  18.9 us (27%)
  Pallas kernels  15.8 us (23%)
  waiting for transfers between devices  11.1 us (16%)
    all_to_all x1, blocking collectives, per_device(): lax.all_to_all(partial.reshape(PLANE, G * ROWS, D), plane, 0, 0, tiled=True)  18.9 us
    ppermute x10, starting transfers between devices, permute(): return lax.ppermute(x, axis, [(i, (i + shift) % size) for i in range(size)])  13.2 us
    all_to_all x1, starting transfers between devices, per_device(): lax.all_to_all(message.reshape(PLANE, G * ROWS, D), plane, 0, 0, tiled=True)  10 us
    all_to_all x1, waiting for transfers between devices, per_device(): lax.all_to_all(message.reshape(PLANE, G * ROWS, D), plane, 0, 0, tiled=True)  9.91 us
    pallas_call x1, Pallas kernels, per_device(): pl.pallas_call(first_kernel, out_shape=[jax.ShapeDtypeStruct((TILES, G, D...  4.07 us
    pallas_call x1, Pallas kernels, per_device(): pl.pallas_call(second_kernel, out_shape=jax.ShapeDtypeStruct((PLANE, G, R...  3.91 us
    pallas_call x1, Pallas kernels, per_device(): pl.pallas_call(combine_kernel, out_shape=jax.ShapeDtypeStruct((T, R, HEAD...  2.13 us
    pallas_call x1, Pallas kernels, per_device(): pl.pallas_call(message_kernel, out_shape=jax.ShapeDtypeStruct((SPREAD, ME...  1.81 us
  transfers between devices with their start and end apart: 11, of which 2 were waited for; matrix products, arithmetic and copies ran while one was open for 0% of the time, Pallas kernels for 9%

profile of v6, /device:TPU:1, one launch (start us, length us, event | category | flops | bytes accessed | tf_op | source)
XLA Modules:
  0.0 69.7 jit_solution(11508662189123308434)
XLA Ops:
  0.0 1.5 %own.1 = (bf16[16,128]{1,0:T(8,128)(2,1)}, bf16[16,128]{1,0:T(8,128)(2,1)}, bf16[16,128]{1,0:T(8,128)(2,1)}, bf16[16,128]{1,0:T(8,128)(2,1)}) custom-call(bf16[64,64]{1,0:T(8,128)(2,1)} %constant.6.clone.own_order_ref, bf16[2,2,8,128]{3,2,1,0:T(8,128)(2,1)} %k_ref.1, bf16[2,2,8,128]{3,2,1,0:T(8,128)(2,1)} %v_ref.1), custom_call_target="tpu_custom_call" | custom-call | tf_op jit(solution)/shard_map/own/pallas_call | solution.py:329
  1.5 2.6 %collective-permute-start = (bf16[16,128]{1,0:T(8,128)(2,1)}, bf16[16,128]{1,0:T(8,128)(2,1)S(1)}, u32[]{:S(2)}, u32[]{:S(2)}) collective-permute-start(bf16[16,128]{1,0:T(8,128)(2,1)} %get-tuple-element.14), channel_id=1, source_target_pairs={{0,1},{1,2},{2,3},{3,0},{4,5},{5,6},{6,7},{7,4},{8,9},{9,10},{10,1... | collective-permute-start | bytes 12296 | tf_op jit(solution)/shard_map/ppermute | solution.py:312
  4.1 2.0 %collective-permute-start.1 = (bf16[16,128]{1,0:T(8,128)(2,1)}, bf16[16,128]{1,0:T(8,128)(2,1)S(1)}, u32[]{:S(2)}, u32[]{:S(2)}) collective-permute-start(bf16[16,128]{1,0:T(8,128)(2,1)} %get-tuple-element.15), channel_id=1, source_target_pairs={{0,2},{1,3},{2,0},{3,1},{4,6},{5,7},{6,4},{7,5},{8,10},{9,11},{10,... | collective-permute-start | bytes 12296 | tf_op jit(solution)/shard_map/ppermute | solution.py:312
  6.1 0.0 collective-permute-start.2
  6.1 1.8 %message.1 = bf16[8,192,128]{2,1,0:T(8,128)(2,1)} custom-call(bf16[192,160]{1,0:T(8,128)(2,1)} %constant.7.clone.order_ref, bf16[2,2,40,128]{3,2,1,0:T(8,128)(2,1)} %q_ref.1), custom_call_target="tpu_custom_call" | custom-call | tf_op jit(solution)/shard_map/message/pallas_call | solution.py:338
  7.9 0.0 collective-permute-done.1.refs_2_
  7.9 1.2 %collective-permute-done.2.refs_3_ = bf16[16,128]{1,0:T(8,128)(2,1)S(1)} collective-permute-done((bf16[16,128]{1,0:T(8,128)(2,1)S(1)}, bf16[16,128]{1,0:T(8,128)(2,1)S(1)}, u32[]{:S(2)}, u32[]{:S(2)}) %collective-permute-start.2) | collective-permute-done | bytes 4128 | tf_op jit(solution)/shard_map/ppermute | solution.py:312
  9.1 0.6 copy-done.4
  9.7 1.8 %pack.1.refs_0_ = bf16[1104,128]{1,0:T(8,128)(2,1)} custom-call(s32[2,128]{1,0:T(2,128)} %bitcast.13, bf16[512,128]{1,0:T(8,128)(2,1)} %bitcast.11, bf16[512,128]{1,0:T(8,128)(2,1)} %bitcast.12, bf16[16,128]{1,0:T(8,128)(2,1)} %get-tuple-element.13.refs_0_, bf16[16,128]{1,0:T(8,128)(2,1)} %copy-done.2, bf16[16,128]{1,0:T(8,128)(2,1)} %copy-done.3, ...), custom_call_target="tpu_custom_call" | custom-call | tf_op jit(solution)/shard_map/pack/pallas_call | solution.py:345
  11.5 1.0 %collective-permute-start.6 = (bf16[1104,128]{1,0:T(8,128)(2,1)}, bf16[1104,128]{1,0:T(8,128)(2,1)S(1)}, u32[]{:S(2)}, u32[]{:S(2)}) collective-permute-start(bf16[1104,128]{1,0:T(8,128)(2,1)} %pack.1.refs_0_), channel_id=1, source_target_pairs={{0,4},{4,0},{1,5},{5,1},{2,6},{6,2},{3,7},{7,3},{8,12},{12,8},{9,1... | collective-permute-start | bytes 847880 | tf_op jit(solution)/shard_map/ppermute | solution.py:312
  12.5 2.9 %collective-permute-start.5 = (bf16[1104,128]{1,0:T(8,128)(2,1)}, bf16[1104,128]{1,0:T(8,128)(2,1)S(1)}, u32[]{:S(2)}, u32[]{:S(2)}) collective-permute-start(bf16[1104,128]{1,0:T(8,128)(2,1)} %pack.1.refs_0_), channel_id=1, source_target_pairs={{0,16},{8,24},{16,0},{24,8},{1,17},{9,25},{17,1},{25,9},{2,18},{10... | collective-permute-start | bytes 847880 | tf_op jit(solution)/shard_map/ppermute | solution.py:312
  15.4 0.8 %collective-permute-start.4 = (bf16[1104,128]{1,0:T(8,128)(2,1)}, bf16[1104,128]{1,0:T(8,128)(2,1)S(1)}, u32[]{:S(2)}, u32[]{:S(2)}) collective-permute-start(bf16[1104,128]{1,0:T(8,128)(2,1)} %pack.1.refs_0_), channel_id=1, source_target_pairs={{0,24},{8,0},{16,8},{24,16},{1,25},{9,1},{17,9},{25,17},{2,26},{10... | collective-permute-start | bytes 847880 | tf_op jit(solution)/shard_map/ppermute | solution.py:312
  16.2 0.7 collective-permute-start.3
  16.9 10.0 %all-to-all-start = ((bf16[32,48,128]{2,1,0:T(8,128)(2,1)}), bf16[32,48,128]{2,1,0:T(8,128)(2,1)S(1)}, u32[]{:S(2)}, u32[]{:S(2)}) async-start(bf16[32,48,128]{2,1,0:T(8,128)(2,1)} %bitcast.3), calls=%async_computation | async-start | bytes 786432 | tf_op jit(solution)/shard_map/all_to_all | solution.py:367
  26.9 0.0 collective-permute-done.6.refs_4_
  26.9 2.1 %collective-permute-start.8 = (bf16[1104,128]{1,0:T(8,128)(2,1)S(1)}, bf16[1104,128]{1,0:T(8,128)(2,1)S(1)}, u32[]{:S(2)}, u32[]{:S(2)}) collective-permute-start(bf16[1104,128]{1,0:T(8,128)(2,1)S(1)} %collective-permute-done.6.refs_4_), channel_id=1, source_target_pairs={{0,24},{8,0},{16,8},{24,16},{1,25},{9,1},{17,9},{25,17},{2,26},{10... | collective-permute-start | bytes 847880 | tf_op jit(solution)/shard_map/ppermute | solution.py:312
  29.0 0.0 collective-permute-start.7
  29.0 1.1 %collective-permute-start.9 = (bf16[1104,128]{1,0:T(8,128)(2,1)S(1)}, bf16[1104,128]{1,0:T(8,128)(2,1)S(1)}, u32[]{:S(2)}, u32[]{:S(2)}) collective-permute-start(bf16[1104,128]{1,0:T(8,128)(2,1)S(1)} %collective-permute-done.5.refs_3_), channel_id=1, source_target_pairs={{0,4},{4,0},{1,5},{5,1},{2,6},{6,2},{3,7},{7,3},{8,12},{12,8},{9,1... | collective-permute-start | bytes 847880 | tf_op jit(solution)/shard_map/ppermute | solution.py:312
  30.2 0.6 hide.1.hide_ref
  30.8 9.9 %all-to-all-done = bf16[32,48,128]{2,1,0:T(8,128)(2,1)S(1)} async-done(((bf16[32,48,128]{2,1,0:T(8,128)(2,1)}), bf16[32,48,128]{2,1,0:T(8,128)(2,1)S(1)}, u32[]{:S(2)}, u32[]{:S(2)}) %all-to-all-start) | async-done | bytes 393248 | tf_op jit(solution)/shard_map/all_to_all | solution.py:367
  40.7 4.1 %attend_first.1 = (f32[2,2,128,384]{3,2,1,0:T(8,128)S(1)}, f32[2,2,8,384]{3,2,1,0:T(8,128)S(1)}) custom-call(f32[5,8,256]{2,1,0:T(8,128)S(1)} %hide.1.hide_ref, bf16[32,2,24,128]{3,2,1,0:T(8,128)(2,1)S(1)} %bitcast.7, bf16[1104,128]{1,0:T(8,128)(2,1)S(1)} %copy-done, bf16[1104,128]{1,0:T(8,128)(2,1)S(1)} %collective-permute-done.3.refs_1_, ...), custom_call_target="tpu_custom_call" | custom-call | flops 1073741824 | bytes 2097152 | tf_op jit(solution)/shard_map/attend_first/pallas_call | solution.py:384
  44.8 3.9 %attend_second.1 = bf16[32,2,24,128]{3,2,1,0:T(8,128)(2,1)S(1)} custom-call(s32[2]{0:T(128)S(1)} %copy-done.1, bf16[32,2,24,128]{3,2,1,0:T(8,128)(2,1)S(1)} %bitcast.8, bf16[1104,128]{1,0:T(8,128)(2,1)S(1)} %copy-done, bf16[1104,128]{1,0:T(8,128)(2,1)S(1)} %collective-permute-done.3.refs_1_, bf16[1104,128]{1,0:T(8,128)(2,1)S(1)} %collective-permute-done.4.refs_2_, ...), custom_call_target="tpu_custom_call" | custom-call | flops 2147483648 | bytes 3145728 | tf_op jit(solution)/shard_map/attend_second/pallas_call | solution.py:397
  48.7 18.9 %all_to_all.10 = bf16[32,48,128]{2,1,0:T(8,128)(2,1)} all-to-all(bf16[32,48,128]{2,1,0:T(8,128)(2,1)S(1)} %bitcast.9), channel_id=1, replica_groups=mesh['zz'=4,'zc'=2,'y'=4,'xh'=2,'xl'=2,'c'=2] {'zz','zc','xl','c'}, dimensions={0} | all-to-all | bytes 786432 | tf_op jit(solution)/shard_map/all_to_all | solution.py:407
  67.6 2.1 %combine.1 = bf16[2,2,40,128]{3,2,1,0:T(8,128)(2,1)} custom-call(s32[2]{0:T(128)} %lengths_ref.1, bf16[160,192]{1,0:T(8,128)(2,1)} %constant.8.clone.order_ref, bf16[8,4,2,24,128]{4,3,2,1,0:T(8,128)(2,1)} %bitcast.10), custom_call_target="tpu_custom_call" | custom-call | tf_op jit(solution)/shard_map/combine/pallas_call | solution.py:408
  (18 shorter events, 0.0 us)
Async XLA Ops:
  1.5 4.6 %copy-start.5 = (bf16[16,128]{1,0:T(8,128)(2,1)S(1)}, bf16[16,128]{1,0:T(8,128)(2,1)}, u32[]{:S(2)}) copy-start(bf16[16,128]{1,0:T(8,128)(2,1)} %get-tuple-element.16) | copy-start | bytes 12292
  1.5 6.4 %collective-permute-start = (bf16[16,128]{1,0:T(8,128)(2,1)}, bf16[16,128]{1,0:T(8,128)(2,1)S(1)}, u32[]{:S(2)}, u32[]{:S(2)}) collective-permute-start(bf16[16,128]{1,0:T(8,128)(2,1)} %get-tuple-element.14), channel_id=1, source_target_pairs={{0,1},{1,2},{2,3},{3,0},{4,5},{5,6},{6,7},{7,4},{8,9},{9,10},{10,1... | collective-permute-start | bytes 12296 | tf_op jit(solution)/shard_map/ppermute | solution.py:312
  4.1 3.8 %collective-permute-start.1 = (bf16[16,128]{1,0:T(8,128)(2,1)}, bf16[16,128]{1,0:T(8,128)(2,1)S(1)}, u32[]{:S(2)}, u32[]{:S(2)}) collective-permute-start(bf16[16,128]{1,0:T(8,128)(2,1)} %get-tuple-element.15), channel_id=1, source_target_pairs={{0,2},{1,3},{2,0},{3,1},{4,6},{5,7},{6,4},{7,5},{8,10},{9,11},{10,... | collective-permute-start | bytes 12296 | tf_op jit(solution)/shard_map/ppermute | solution.py:312
  6.1 3.0 %collective-permute-start.2 = (bf16[16,128]{1,0:T(8,128)(2,1)S(1)}, bf16[16,128]{1,0:T(8,128)(2,1)S(1)}, u32[]{:S(2)}, u32[]{:S(2)}) collective-permute-start(bf16[16,128]{1,0:T(8,128)(2,1)S(1)} %copy-done.5), channel_id=1, source_target_pairs={{0,3},{1,0},{2,1},{3,2},{4,7},{5,4},{6,5},{7,6},{8,11},{9,8},{10,9... | collective-permute-start | bytes 12296 | tf_op jit(solution)/shard_map/ppermute | solution.py:312
  7.9 1.2 %copy-start.2 = (bf16[16,128]{1,0:T(8,128)(2,1)}, bf16[16,128]{1,0:T(8,128)(2,1)S(1)}, u32[]{:S(2)}) copy-start(bf16[16,128]{1,0:T(8,128)(2,1)S(1)} %collective-permute-done.refs_1_) | copy-start | bytes 12292
  7.9 1.2 %copy-start.3 = (bf16[16,128]{1,0:T(8,128)(2,1)}, bf16[16,128]{1,0:T(8,128)(2,1)S(1)}, u32[]{:S(2)}) copy-start(bf16[16,128]{1,0:T(8,128)(2,1)S(1)} %collective-permute-done.1.refs_2_) | copy-start | bytes 12292
  9.1 0.6 copy-start.4
  11.5 15.4 %collective-permute-start.6 = (bf16[1104,128]{1,0:T(8,128)(2,1)}, bf16[1104,128]{1,0:T(8,128)(2,1)S(1)}, u32[]{:S(2)}, u32[]{:S(2)}) collective-permute-start(bf16[1104,128]{1,0:T(8,128)(2,1)} %pack.1.refs_0_), channel_id=1, source_target_pairs={{0,4},{4,0},{1,5},{5,1},{2,6},{6,2},{3,7},{7,3},{8,12},{12,8},{9,1... | collective-permute-start | bytes 847880 | tf_op jit(solution)/shard_map/ppermute | solution.py:312
  12.5 16.5 %collective-permute-start.5 = (bf16[1104,128]{1,0:T(8,128)(2,1)}, bf16[1104,128]{1,0:T(8,128)(2,1)S(1)}, u32[]{:S(2)}, u32[]{:S(2)}) collective-permute-start(bf16[1104,128]{1,0:T(8,128)(2,1)} %pack.1.refs_0_), channel_id=1, source_target_pairs={{0,16},{8,24},{16,0},{24,8},{1,17},{9,25},{17,1},{25,9},{2,18},{10... | collective-permute-start | bytes 847880 | tf_op jit(solution)/shard_map/ppermute | solution.py:312
  15.4 14.7 %collective-permute-start.4 = (bf16[1104,128]{1,0:T(8,128)(2,1)}, bf16[1104,128]{1,0:T(8,128)(2,1)S(1)}, u32[]{:S(2)}, u32[]{:S(2)}) collective-permute-start(bf16[1104,128]{1,0:T(8,128)(2,1)} %pack.1.refs_0_), channel_id=1, source_target_pairs={{0,24},{8,0},{16,8},{24,16},{1,25},{9,1},{17,9},{25,17},{2,26},{10... | collective-permute-start | bytes 847880 | tf_op jit(solution)/shard_map/ppermute | solution.py:312
  16.2 14.0 %collective-permute-start.3 = (bf16[1104,128]{1,0:T(8,128)(2,1)}, bf16[1104,128]{1,0:T(8,128)(2,1)S(1)}, u32[]{:S(2)}, u32[]{:S(2)}) collective-permute-start(bf16[1104,128]{1,0:T(8,128)(2,1)} %pack.1.refs_0_), channel_id=1, source_target_pairs={{0,8},{8,16},{16,24},{24,0},{1,9},{9,17},{17,25},{25,1},{2,10},{10... | collective-permute-start | bytes 847880 | tf_op jit(solution)/shard_map/ppermute | solution.py:312
  16.9 13.3 %copy-start = (bf16[1104,128]{1,0:T(8,128)(2,1)S(1)}, bf16[1104,128]{1,0:T(8,128)(2,1)}, u32[]{:S(2)}) copy-start(bf16[1104,128]{1,0:T(8,128)(2,1)} %pack.1.refs_0_) | copy-start | bytes 847876
  16.9 13.3 %copy-start.1 = (s32[2]{0:T(128)S(1)}, s32[2]{0:T(128)}, u32[]{:S(2)}) copy-start(s32[2]{0:T(128)} %reach_ref.3) | copy-start | bytes 28
  16.9 23.8 %all-to-all-start = ((bf16[32,48,128]{2,1,0:T(8,128)(2,1)}), bf16[32,48,128]{2,1,0:T(8,128)(2,1)S(1)}, u32[]{:S(2)}, u32[]{:S(2)}) async-start(bf16[32,48,128]{2,1,0:T(8,128)(2,1)} %bitcast.3), calls=%async_computation | async-start | bytes 786432 | tf_op jit(solution)/shard_map/all_to_all | solution.py:367
  26.9 17.8 %collective-permute-start.8 = (bf16[1104,128]{1,0:T(8,128)(2,1)S(1)}, bf16[1104,128]{1,0:T(8,128)(2,1)S(1)}, u32[]{:S(2)}, u32[]{:S(2)}) collective-permute-start(bf16[1104,128]{1,0:T(8,128)(2,1)S(1)} %collective-permute-done.6.refs_4_), channel_id=1, source_target_pairs={{0,24},{8,0},{16,8},{24,16},{1,25},{9,1},{17,9},{25,17},{2,26},{10... | collective-permute-start | bytes 847880 | tf_op jit(solution)/shard_map/ppermute | solution.py:312
  29.0 15.8 %collective-permute-start.7 = (bf16[1104,128]{1,0:T(8,128)(2,1)S(1)}, bf16[1104,128]{1,0:T(8,128)(2,1)S(1)}, u32[]{:S(2)}, u32[]{:S(2)}) collective-permute-start(bf16[1104,128]{1,0:T(8,128)(2,1)S(1)} %collective-permute-done.6.refs_4_), channel_id=1, source_target_pairs={{0,8},{8,16},{16,24},{24,0},{1,9},{9,17},{17,25},{25,1},{2,10},{10... | collective-permute-start | bytes 847880 | tf_op jit(solution)/shard_map/ppermute | solution.py:312
  29.0 15.8 %collective-permute-start.9 = (bf16[1104,128]{1,0:T(8,128)(2,1)S(1)}, bf16[1104,128]{1,0:T(8,128)(2,1)S(1)}, u32[]{:S(2)}, u32[]{:S(2)}) collective-permute-start(bf16[1104,128]{1,0:T(8,128)(2,1)S(1)} %collective-permute-done.5.refs_3_), channel_id=1, source_target_pairs={{0,4},{4,0},{1,5},{5,1},{2,6},{6,2},{3,7},{7,3},{8,12},{12,8},{9,1... | collective-permute-start | bytes 847880 | tf_op jit(solution)/shard_map/ppermute | solution.py:312

commit v7 on v6

--- a/solution.py
+++ b/solution.py
@@ -352,6 +352,7 @@
             pltpu.VMEM((HEADS, OWN_PART, D), F32),
             pltpu.VMEM((HEADS * OWN_PART, D), F32),
         ],
+        compiler_params=pltpu.CompilerParams(vmem_limit_bytes=6 << 20),
         name="pack",
     )(
         prompt_mask.reshape(BLOCK // D, D),
@@ -411,6 +412,7 @@
         in_specs=[smem, vmem, vmem],
         out_specs=vmem,
         scratch_shapes=[pltpu.VMEM((MESSAGE, D), F32)],
+        compiler_params=pltpu.CompilerParams(vmem_limit_bytes=6 << 20),
         name="combine",
     )(resp_lengths, jnp.asarray(order.T, BF16), partial.reshape(SPREAD, HEADS, G, ROWS, D))
 

time: 70.2 us -> 68.3 us (0.973)
  Pallas kernels: 15.8 us -> 13.6 us
  local copies, waits for them, and re-layouts: 0.6 us -> 1.35 us
    pallas_call x1, Pallas kernels: 1.8 us -> 0.09 us  [per_device(): pl.pallas_call(pack_kernel, out_shape=jax.ShapeDtypeStruct((PACK, D), BF1...]
    unnamed x12 -> x16, local copies, waits for them, and re-layouts: 0.6 us -> 1.35 us
  transfers between devices with their start and end apart: 11 -> 11, of which waited for: 2 -> 2; matrix products, arithmetic and copies ran while one was open for 0% -> 0% of each run, Pallas kernels for 9% -> 10%
where the time goes in v7:
time: 68.3 us; the launch traced here: 67.8 us
  starting transfers between devices  23.3 us (34%)
  blocking collectives  18.3 us (27%)
  Pallas kernels  13.6 us (20%)
  waiting for transfers between devices  11.1 us (16%)
  local copies, waits for them, and re-layouts  1.35 us (2%)
    all_to_all x1, blocking collectives, per_device(): lax.all_to_all(partial.reshape(PLANE, G * ROWS, D), plane, 0, 0, tiled=True)  18.3 us
    ppermute x10, starting transfers between devices, permute(): return lax.ppermute(x, axis, [(i, (i + shift) % size) for i in range(size)])  13.3 us
    all_to_all x1, starting transfers between devices, per_device(): lax.all_to_all(message.reshape(PLANE, G * ROWS, D), plane, 0, 0, tiled=True)  10 us
    all_to_all x1, waiting for transfers between devices, per_device(): lax.all_to_all(message.reshape(PLANE, G * ROWS, D), plane, 0, 0, tiled=True)  9.92 us
    pallas_call x1, Pallas kernels, per_device(): pl.pallas_call(first_kernel, out_shape=[jax.ShapeDtypeStruct((TILES, G, D...  4.07 us
    pallas_call x1, Pallas kernels, per_device(): pl.pallas_call(second_kernel, out_shape=jax.ShapeDtypeStruct((PLANE, G, R...  3.91 us
    pallas_call x1, Pallas kernels, per_device(): pl.pallas_call(message_kernel, out_shape=jax.ShapeDtypeStruct((SPREAD, ME...  1.86 us
    pallas_call x1, Pallas kernels, per_device(): pl.pallas_call(combine_kernel, out_shape=jax.ShapeDtypeStruct((T, R, HEAD...  1.62 us
  transfers between devices with their start and end apart: 11, of which 2 were waited for; matrix products, arithmetic and copies ran while one was open for 0% of the time, Pallas kernels for 10%

profile of v7, /device:TPU:1, one launch (start us, length us, event | category | flops | bytes accessed | tf_op | source)
XLA Modules:
  0.0 67.8 jit_solution(2651184694982513035)
XLA Ops:
  0.0 1.5 %own.1 = (bf16[16,128]{1,0:T(8,128)(2,1)}, bf16[16,128]{1,0:T(8,128)(2,1)}, bf16[16,128]{1,0:T(8,128)(2,1)}, bf16[16,128]{1,0:T(8,128)(2,1)}) custom-call(bf16[64,64]{1,0:T(8,128)(2,1)} %constant.6.clone.own_order_ref, bf16[2,2,8,128]{3,2,1,0:T(8,128)(2,1)} %k_ref.1, bf16[2,2,8,128]{3,2,1,0:T(8,128)(2,1)} %v_ref.1), custom_call_target="tpu_custom_call" | custom-call | tf_op jit(solution)/shard_map/own/pallas_call | solution.py:329
  1.5 2.6 %collective-permute-start = (bf16[16,128]{1,0:T(8,128)(2,1)}, bf16[16,128]{1,0:T(8,128)(2,1)S(1)}, u32[]{:S(2)}, u32[]{:S(2)}) collective-permute-start(bf16[16,128]{1,0:T(8,128)(2,1)} %get-tuple-element.14), channel_id=1, source_target_pairs={{0,1},{1,2},{2,3},{3,0},{4,5},{5,6},{6,7},{7,4},{8,9},{9,10},{10,1... | collective-permute-start | bytes 12296 | tf_op jit(solution)/shard_map/ppermute | solution.py:312
  4.1 2.0 %collective-permute-start.1 = (bf16[16,128]{1,0:T(8,128)(2,1)}, bf16[16,128]{1,0:T(8,128)(2,1)S(1)}, u32[]{:S(2)}, u32[]{:S(2)}) collective-permute-start(bf16[16,128]{1,0:T(8,128)(2,1)} %get-tuple-element.15), channel_id=1, source_target_pairs={{0,2},{1,3},{2,0},{3,1},{4,6},{5,7},{6,4},{7,5},{8,10},{9,11},{10,... | collective-permute-start | bytes 12296 | tf_op jit(solution)/shard_map/ppermute | solution.py:312
  6.1 0.0 collective-permute-start.2
  6.1 1.9 %message.1 = bf16[8,192,128]{2,1,0:T(8,128)(2,1)} custom-call(bf16[192,160]{1,0:T(8,128)(2,1)} %constant.7.clone.order_ref, bf16[2,2,40,128]{3,2,1,0:T(8,128)(2,1)} %q_ref.1), custom_call_target="tpu_custom_call" | custom-call | tf_op jit(solution)/shard_map/message/pallas_call | solution.py:338
  7.9 0.0 collective-permute-done.1.refs_2_
  8.0 1.1 %collective-permute-done.2.refs_3_ = bf16[16,128]{1,0:T(8,128)(2,1)S(1)} collective-permute-done((bf16[16,128]{1,0:T(8,128)(2,1)S(1)}, bf16[16,128]{1,0:T(8,128)(2,1)S(1)}, u32[]{:S(2)}, u32[]{:S(2)}) %collective-permute-start.2) | collective-permute-done | bytes 4128 | tf_op jit(solution)/shard_map/ppermute | solution.py:312
  9.1 0.7 copy-done.4
  9.8 0.1 pack.1.refs_0_
  9.9 1.1 %collective-permute-start.6 = (bf16[1104,128]{1,0:T(8,128)(2,1)S(1)}, bf16[1104,128]{1,0:T(8,128)(2,1)S(1)}, u32[]{:S(2)}, u32[]{:S(2)}) collective-permute-start(bf16[1104,128]{1,0:T(8,128)(2,1)S(1)} %pack.1.refs_0_), channel_id=1, source_target_pairs={{0,4},{4,0},{1,5},{5,1},{2,6},{6,2},{3,7},{7,3},{8,12},{12,8},{9,1... | collective-permute-start | bytes 847880 | tf_op jit(solution)/shard_map/ppermute | solution.py:312
  11.0 2.9 %collective-permute-start.5 = (bf16[1104,128]{1,0:T(8,128)(2,1)S(1)}, bf16[1104,128]{1,0:T(8,128)(2,1)S(1)}, u32[]{:S(2)}, u32[]{:S(2)}) collective-permute-start(bf16[1104,128]{1,0:T(8,128)(2,1)S(1)} %pack.1.refs_0_), channel_id=1, source_target_pairs={{0,16},{8,24},{16,0},{24,8},{1,17},{9,25},{17,1},{25,9},{2,18},{10... | collective-permute-start | bytes 847880 | tf_op jit(solution)/shard_map/ppermute | solution.py:312
  13.9 0.8 %collective-permute-start.4 = (bf16[1104,128]{1,0:T(8,128)(2,1)S(1)}, bf16[1104,128]{1,0:T(8,128)(2,1)S(1)}, u32[]{:S(2)}, u32[]{:S(2)}) collective-permute-start(bf16[1104,128]{1,0:T(8,128)(2,1)S(1)} %pack.1.refs_0_), channel_id=1, source_target_pairs={{0,24},{8,0},{16,8},{24,16},{1,25},{9,1},{17,9},{25,17},{2,26},{10... | collective-permute-start | bytes 847880 | tf_op jit(solution)/shard_map/ppermute | solution.py:312
  14.7 0.7 %collective-permute-start.3 = (bf16[1104,128]{1,0:T(8,128)(2,1)S(1)}, bf16[1104,128]{1,0:T(8,128)(2,1)S(1)}, u32[]{:S(2)}, u32[]{:S(2)}) collective-permute-start(bf16[1104,128]{1,0:T(8,128)(2,1)S(1)} %pack.1.refs_0_), channel_id=1, source_target_pairs={{0,8},{8,16},{16,24},{24,0},{1,9},{9,17},{17,25},{25,1},{2,10},{10... | collective-permute-start | bytes 847880 | tf_op jit(solution)/shard_map/ppermute | solution.py:312
  15.3 10.0 %all-to-all-start = ((bf16[32,48,128]{2,1,0:T(8,128)(2,1)}), bf16[32,48,128]{2,1,0:T(8,128)(2,1)S(1)}, u32[]{:S(2)}, u32[]{:S(2)}) async-start(bf16[32,48,128]{2,1,0:T(8,128)(2,1)} %bitcast.3), calls=%async_computation | async-start | bytes 786432 | tf_op jit(solution)/shard_map/all_to_all | solution.py:368
  25.4 2.1 %collective-permute-start.8 = (bf16[1104,128]{1,0:T(8,128)(2,1)S(1)}, bf16[1104,128]{1,0:T(8,128)(2,1)S(1)}, u32[]{:S(2)}, u32[]{:S(2)}) collective-permute-start(bf16[1104,128]{1,0:T(8,128)(2,1)S(1)} %collective-permute-done.6.refs_4_), channel_id=1, source_target_pairs={{0,24},{8,0},{16,8},{24,16},{1,25},{9,1},{17,9},{25,17},{2,26},{10... | collective-permute-start | bytes 847880 | tf_op jit(solution)/shard_map/ppermute | solution.py:312
  27.5 1.1 %collective-permute-start.9 = (bf16[1104,128]{1,0:T(8,128)(2,1)S(1)}, bf16[1104,128]{1,0:T(8,128)(2,1)S(1)}, u32[]{:S(2)}, u32[]{:S(2)}) collective-permute-start(bf16[1104,128]{1,0:T(8,128)(2,1)S(1)} %collective-permute-done.5.refs_3_), channel_id=1, source_target_pairs={{0,4},{4,0},{1,5},{5,1},{2,6},{6,2},{3,7},{7,3},{8,12},{12,8},{9,1... | collective-permute-start | bytes 847880 | tf_op jit(solution)/shard_map/ppermute | solution.py:312
  28.6 0.6 hide.1.hide_ref
  29.2 9.9 %all-to-all-done = bf16[32,48,128]{2,1,0:T(8,128)(2,1)S(1)} async-done(((bf16[32,48,128]{2,1,0:T(8,128)(2,1)}), bf16[32,48,128]{2,1,0:T(8,128)(2,1)S(1)}, u32[]{:S(2)}, u32[]{:S(2)}) %all-to-all-start) | async-done | bytes 393248 | tf_op jit(solution)/shard_map/all_to_all | solution.py:368
  39.1 4.1 %attend_first.1 = (f32[2,2,128,384]{3,2,1,0:T(8,128)S(1)}, f32[2,2,8,384]{3,2,1,0:T(8,128)S(1)}) custom-call(f32[5,8,256]{2,1,0:T(8,128)S(1)} %hide.1.hide_ref, bf16[32,2,24,128]{3,2,1,0:T(8,128)(2,1)S(1)} %bitcast.8, bf16[1104,128]{1,0:T(8,128)(2,1)S(1)} %pack.1.refs_0_, bf16[1104,128]{1,0:T(8,128)(2,1)S(1)} %collective-permute-done.3.refs_1_, ...), custom_call_target="tpu_custom_call" | custom-call | flops 1073741824 | bytes 2097152 | tf_op jit(solution)/shard_map/attend_first/pallas_call | solution.py:385
  43.2 3.9 %attend_second.1 = bf16[32,2,24,128]{3,2,1,0:T(8,128)(2,1)S(1)} custom-call(s32[2]{0:T(128)S(1)} %copy-done.6, bf16[32,2,24,128]{3,2,1,0:T(8,128)(2,1)S(1)} %bitcast.9, bf16[1104,128]{1,0:T(8,128)(2,1)S(1)} %pack.1.refs_0_, bf16[1104,128]{1,0:T(8,128)(2,1)S(1)} %collective-permute-done.3.refs_1_, bf16[1104,128]{1,0:T(8,128)(2,1)S(1)} %collective-permute-done.4.refs_2_, ...), custom_call_target="tpu_custom_call" | custom-call | flops 2147483648 | bytes 3145728 | tf_op jit(solution)/shard_map/attend_second/pallas_call | solution.py:398
  47.2 0.0 copy-start.2
  47.2 18.3 %all_to_all.10 = bf16[32,48,128]{2,1,0:T(8,128)(2,1)S(1)} all-to-all(bf16[32,48,128]{2,1,0:T(8,128)(2,1)S(1)} %bitcast.10), channel_id=1, replica_groups=mesh['zz'=4,'zc'=2,'y'=4,'xh'=2,'xl'=2,'c'=2] {'zz','zc','xl','c'}, dimensions={0} | all-to-all | bytes 786432 | tf_op jit(solution)/shard_map/all_to_all | solution.py:408
  65.5 0.7 copy-done.5
  66.2 1.6 %combine.1 = bf16[2,2,40,128]{3,2,1,0:T(8,128)(2,1)} custom-call(s32[2]{0:T(128)S(1)} %copy-done.5, bf16[160,192]{1,0:T(8,128)(2,1)S(1)} %copy-done.2, bf16[8,4,2,24,128]{4,3,2,1,0:T(8,128)(2,1)S(1)} %bitcast.7), custom_call_target="tpu_custom_call" | custom-call | tf_op jit(solution)/shard_map/combine/pallas_call | solution.py:409
  (22 shorter events, 0.0 us)
Async XLA Ops:
  1.5 4.6 %copy-start.7 = (bf16[16,128]{1,0:T(8,128)(2,1)S(1)}, bf16[16,128]{1,0:T(8,128)(2,1)}, u32[]{:S(2)}) copy-start(bf16[16,128]{1,0:T(8,128)(2,1)} %get-tuple-element.16) | copy-start | bytes 12292
  1.5 6.5 %collective-permute-start = (bf16[16,128]{1,0:T(8,128)(2,1)}, bf16[16,128]{1,0:T(8,128)(2,1)S(1)}, u32[]{:S(2)}, u32[]{:S(2)}) collective-permute-start(bf16[16,128]{1,0:T(8,128)(2,1)} %get-tuple-element.14), channel_id=1, source_target_pairs={{0,1},{1,2},{2,3},{3,0},{4,5},{5,6},{6,7},{7,4},{8,9},{9,10},{10,1... | collective-permute-start | bytes 12296 | tf_op jit(solution)/shard_map/ppermute | solution.py:312
  4.1 3.9 %collective-permute-start.1 = (bf16[16,128]{1,0:T(8,128)(2,1)}, bf16[16,128]{1,0:T(8,128)(2,1)S(1)}, u32[]{:S(2)}, u32[]{:S(2)}) collective-permute-start(bf16[16,128]{1,0:T(8,128)(2,1)} %get-tuple-element.15), channel_id=1, source_target_pairs={{0,2},{1,3},{2,0},{3,1},{4,6},{5,7},{6,4},{7,5},{8,10},{9,11},{10,... | collective-permute-start | bytes 12296 | tf_op jit(solution)/shard_map/ppermute | solution.py:312
  6.1 3.0 %copy-start = (bf16[256,2,128]{2,1,0:T(2,128)(2,1)S(1)}, bf16[256,2,128]{2,1,0:T(2,128)(2,1)}, u32[]{:S(2)}) copy-start(bf16[256,2,128]{2,1,0:T(2,128)(2,1)} %param.11) | copy-start | bytes 393220
  6.1 3.0 %copy-start.1 = (bf16[256,2,128]{2,1,0:T(2,128)(2,1)S(1)}, bf16[256,2,128]{2,1,0:T(2,128)(2,1)}, u32[]{:S(2)}) copy-start(bf16[256,2,128]{2,1,0:T(2,128)(2,1)} %param.12) | copy-start | bytes 393220
  6.1 3.0 %collective-permute-start.2 = (bf16[16,128]{1,0:T(8,128)(2,1)S(1)}, bf16[16,128]{1,0:T(8,128)(2,1)S(1)}, u32[]{:S(2)}, u32[]{:S(2)}) collective-permute-start(bf16[16,128]{1,0:T(8,128)(2,1)S(1)} %copy-done.7), channel_id=1, source_target_pairs={{0,3},{1,0},{2,1},{3,2},{4,7},{5,4},{6,5},{7,6},{8,11},{9,8},{10,9... | collective-permute-start | bytes 12296 | tf_op jit(solution)/shard_map/ppermute | solution.py:312
  7.9 1.2 %copy-start.3 = (bf16[16,128]{1,0:T(8,128)(2,1)S(1)}, bf16[16,128]{1,0:T(8,128)(2,1)}, u32[]{:S(2)}) copy-start(bf16[16,128]{1,0:T(8,128)(2,1)} %get-tuple-element.13.refs_0_) | copy-start | bytes 12292
  9.1 0.7 %copy-start.4 = (s32[256]{0:T(256)S(1)}, s32[256]{0:T(256)}, u32[]{:S(2)}) copy-start(s32[256]{0:T(256)} %param.13) | copy-start | bytes 3076
  9.9 15.5 %collective-permute-start.6 = (bf16[1104,128]{1,0:T(8,128)(2,1)S(1)}, bf16[1104,128]{1,0:T(8,128)(2,1)S(1)}, u32[]{:S(2)}, u32[]{:S(2)}) collective-permute-start(bf16[1104,128]{1,0:T(8,128)(2,1)S(1)} %pack.1.refs_0_), channel_id=1, source_target_pairs={{0,4},{4,0},{1,5},{5,1},{2,6},{6,2},{3,7},{7,3},{8,12},{12,8},{9,1... | collective-permute-start | bytes 847880 | tf_op jit(solution)/shard_map/ppermute | solution.py:312
  11.0 16.5 %collective-permute-start.5 = (bf16[1104,128]{1,0:T(8,128)(2,1)S(1)}, bf16[1104,128]{1,0:T(8,128)(2,1)S(1)}, u32[]{:S(2)}, u32[]{:S(2)}) collective-permute-start(bf16[1104,128]{1,0:T(8,128)(2,1)S(1)} %pack.1.refs_0_), channel_id=1, source_target_pairs={{0,16},{8,24},{16,0},{24,8},{1,17},{9,25},{17,1},{25,9},{2,18},{10... | collective-permute-start | bytes 847880 | tf_op jit(solution)/shard_map/ppermute | solution.py:312
  13.9 14.7 %collective-permute-start.4 = (bf16[1104,128]{1,0:T(8,128)(2,1)S(1)}, bf16[1104,128]{1,0:T(8,128)(2,1)S(1)}, u32[]{:S(2)}, u32[]{:S(2)}) collective-permute-start(bf16[1104,128]{1,0:T(8,128)(2,1)S(1)} %pack.1.refs_0_), channel_id=1, source_target_pairs={{0,24},{8,0},{16,8},{24,16},{1,25},{9,1},{17,9},{25,17},{2,26},{10... | collective-permute-start | bytes 847880 | tf_op jit(solution)/shard_map/ppermute | solution.py:312
  14.7 13.9 %collective-permute-start.3 = (bf16[1104,128]{1,0:T(8,128)(2,1)S(1)}, bf16[1104,128]{1,0:T(8,128)(2,1)S(1)}, u32[]{:S(2)}, u32[]{:S(2)}) collective-permute-start(bf16[1104,128]{1,0:T(8,128)(2,1)S(1)} %pack.1.refs_0_), channel_id=1, source_target_pairs={{0,8},{8,16},{16,24},{24,0},{1,9},{9,17},{17,25},{25,1},{2,10},{10... | collective-permute-start | bytes 847880 | tf_op jit(solution)/shard_map/ppermute | solution.py:312
  15.3 13.3 %copy-start.6 = (s32[2]{0:T(128)S(1)}, s32[2]{0:T(128)}, u32[]{:S(2)}) copy-start(s32[2]{0:T(128)} %reach_ref.3) | copy-start | bytes 28
  15.3 23.8 %all-to-all-start = ((bf16[32,48,128]{2,1,0:T(8,128)(2,1)}), bf16[32,48,128]{2,1,0:T(8,128)(2,1)S(1)}, u32[]{:S(2)}, u32[]{:S(2)}) async-start(bf16[32,48,128]{2,1,0:T(8,128)(2,1)} %bitcast.3), calls=%async_computation | async-start | bytes 786432 | tf_op jit(solution)/shard_map/all_to_all | solution.py:368
  25.4 17.8 %collective-permute-start.8 = (bf16[1104,128]{1,0:T(8,128)(2,1)S(1)}, bf16[1104,128]{1,0:T(8,128)(2,1)S(1)}, u32[]{:S(2)}, u32[]{:S(2)}) collective-permute-start(bf16[1104,128]{1,0:T(8,128)(2,1)S(1)} %collective-permute-done.6.refs_4_), channel_id=1, source_target_pairs={{0,24},{8,0},{16,8},{24,16},{1,25},{9,1},{17,9},{25,17},{2,26},{10... | collective-permute-start | bytes 847880 | tf_op jit(solution)/shard_map/ppermute | solution.py:312
  27.4 15.8 %collective-permute-start.7 = (bf16[1104,128]{1,0:T(8,128)(2,1)S(1)}, bf16[1104,128]{1,0:T(8,128)(2,1)S(1)}, u32[]{:S(2)}, u32[]{:S(2)}) collective-permute-start(bf16[1104,128]{1,0:T(8,128)(2,1)S(1)} %collective-permute-done.6.refs_4_), channel_id=1, source_target_pairs={{0,8},{8,16},{16,24},{24,0},{1,9},{9,17},{17,25},{25,1},{2,10},{10... | collective-permute-start | bytes 847880 | tf_op jit(solution)/shard_map/ppermute | solution.py:312
  27.5 15.8 %collective-permute-start.9 = (bf16[1104,128]{1,0:T(8,128)(2,1)S(1)}, bf16[1104,128]{1,0:T(8,128)(2,1)S(1)}, u32[]{:S(2)}, u32[]{:S(2)}) collective-permute-start(bf16[1104,128]{1,0:T(8,128)(2,1)S(1)} %collective-permute-done.5.refs_3_), channel_id=1, source_target_pairs={{0,4},{4,0},{1,5},{5,1},{2,6},{6,2},{3,7},{7,3},{8,12},{12,8},{9,1... | collective-permute-start | bytes 847880 | tf_op jit(solution)/shard_map/ppermute | solution.py:312
  47.2 18.3 %copy-start.2 = (bf16[160,192]{1,0:T(8,128)(2,1)S(1)}, bf16[160,192]{1,0:T(8,128)(2,1)}, u32[]{:S(2)}) copy-start(bf16[160,192]{1,0:T(8,128)(2,1)} %constant.8.clone.order_ref) | copy-start | bytes 184324
  65.5 0.7 copy-start.5

commit v8 on v7

--- a/solution.py
+++ b/solution.py
@@ -75,8 +75,16 @@
     return jnp.concatenate(parts, axis=1)
 
 
-def hide_kernel(reach_ref, *refs):
-    mask_refs, hide_ref = refs[:-1], refs[-1]
+def hide_kernel(reach_ref, lengths_ref, *refs):
+    mask_refs, (hide_ref, live_ref) = refs[:-2], refs[-2:]
+    names = ("zz", "zc", "y", "xh")
+    head = lax.axis_index("xl") * C + lax.axis_index("c")
+    first = T * device_of(*(lax.axis_index(name) for name in names), head)
+    for t in range(T):
+        for r in range(R):
+            at = (t * R + r) * HEADS * G * J
+            live = jnp.where(first + t < lengths_ref[r], 1.0, 0.0)
+            live_ref[at : at + HEADS * G * J, :] = jnp.full((HEADS * G * J, D), live, F32)
     for b, mask_ref in enumerate(mask_refs):
         hide_ref[b] = hide_rows(reach_ref, mask_ref[...].astype(F32), BLOCKS[b])
 
@@ -215,7 +223,7 @@
         finish(outs, lse, tile, out_ref)
 
 
-def combine_kernel(lengths_ref, order_ref, in_ref, out_ref, rows_ref):
+def combine_kernel(live_ref, order_ref, in_ref, out_ref, rows_ref):
     lane = lax.broadcasted_iota(jnp.int32, (1, ROWS, D), 2)
     row = lax.broadcasted_iota(jnp.int32, (1, ROWS, D), 1)
     for h in range(HEADS):
@@ -234,13 +242,10 @@
             rows_ref[at : at + ROWS, :] = jnp.where(row[0] < LIVE, o, 0.0)
     rows = jnp.dot(order_ref[...], rows_ref[...].astype(BF16), preferred_element_type=F32)
     heads = HEADS * G * J
-    names = ("zz", "zc", "y", "xh")
-    head = lax.axis_index("xl") * C + lax.axis_index("c")
-    first = T * device_of(*(lax.axis_index(name) for name in names), head)
     for t in range(T):
         for r in range(R):
             at = (t * R + r) * heads
-            live = first + t < lengths_ref[r]
+            live = live_ref[at : at + heads, :] > 0.5
             out_ref[t, r] = jnp.where(live, rows[at : at + heads, :], 0.0).astype(BF16)
 
 
@@ -370,17 +375,23 @@
     across_after = permute(across, "y", Y, 3)
     across_far = permute(far, "xh", XH, 1)
     blocks = (kv, before, after, far, across, across_before, across_after, across_far)
-    hide = pl.pallas_call(
+    hide, live = pl.pallas_call(
         hide_kernel,
-        out_shape=jax.ShapeDtypeStruct((EARLY, 8, BLOCK), F32),
+        out_shape=[
+            jax.ShapeDtypeStruct((EARLY, 8, BLOCK), F32),
+            jax.ShapeDtypeStruct((QUERIES, D), F32),
+        ],
         grid=(1,),
-        in_specs=[smem]
+        in_specs=[smem] * 2
         + [pl.BlockSpec((OWN - MASK, D), lambda i: (MASK // 16, 0))] * (EARLY),
-        out_specs=pl.BlockSpec((EARLY, 8, BLOCK), lambda i: (0, 0, 0)),
+        out_specs=[
+            pl.BlockSpec((EARLY, 8, BLOCK), lambda i: (0, 0, 0)),
+            pl.BlockSpec((QUERIES, D), lambda i: (0, 0)),
+        ],
         compiler_params=pltpu.CompilerParams(vmem_limit_bytes=4 << 20),
         cost_estimate=pl.CostEstimate(flops=HIDE_FLOPS, bytes_accessed=1 << 20, transcendentals=0),
         name="hide",
-    )(prompt_reach, *blocks[:EARLY])
+    )(prompt_reach, resp_lengths, *blocks[:EARLY])
     rows = rows.reshape(PLANE, G, ROWS, D)
     acc, stat = pl.pallas_call(
         first_kernel,
@@ -409,12 +420,12 @@
     return pl.pallas_call(
         combine_kernel,
         out_shape=jax.ShapeDtypeStruct((T, R, HEADS * G * J, D), BF16),
-        in_specs=[smem, vmem, vmem],
+        in_specs=[vmem] * 3,
         out_specs=vmem,
         scratch_shapes=[pltpu.VMEM((MESSAGE, D), F32)],
         compiler_params=pltpu.CompilerParams(vmem_limit_bytes=6 << 20),
         name="combine",
-    )(resp_lengths, jnp.asarray(order.T, BF16), partial.reshape(SPREAD, HEADS, G, ROWS, D))
+    )(live, jnp.asarray(order.T, BF16), partial.reshape(SPREAD, HEADS, G, ROWS, D))
 
 
 def solution(mesh):

time: 68.3 us -> 67.1 us (0.982)
  no operation moved by 1% of the time
where the time goes in v8:
time: 67.1 us; the launch traced here: 66.6 us
  starting transfers between devices  23.3 us (35%)
  blocking collectives  18.3 us (27%)
  Pallas kernels  13.1 us (20%)
  waiting for transfers between devices  11.1 us (17%)
  local copies, waits for them, and re-layouts  0.7 us (1%)
    all_to_all x1, blocking collectives, per_device(): lax.all_to_all(partial.reshape(PLANE, G * ROWS, D), plane, 0, 0, tiled=True)  18.3 us
    ppermute x10, starting transfers between devices, permute(): return lax.ppermute(x, axis, [(i, (i + shift) % size) for i in range(size)])  13.3 us
    all_to_all x1, starting transfers between devices, per_device(): lax.all_to_all(message.reshape(PLANE, G * ROWS, D), plane, 0, 0, tiled=True)  10 us
    all_to_all x1, waiting for transfers between devices, per_device(): lax.all_to_all(message.reshape(PLANE, G * ROWS, D), plane, 0, 0, tiled=True)  9.91 us
    pallas_call x1, Pallas kernels, per_device(): pl.pallas_call(first_kernel, out_shape=[jax.ShapeDtypeStruct((TILES, G, D...  4.08 us
    pallas_call x1, Pallas kernels, per_device(): pl.pallas_call(second_kernel, out_shape=jax.ShapeDtypeStruct((PLANE, G, R...  3.9 us
    pallas_call x1, Pallas kernels, per_device(): pl.pallas_call(message_kernel, out_shape=jax.ShapeDtypeStruct((SPREAD, ME...  1.86 us
    pallas_call x1, Pallas kernels, per_device(): pl.pallas_call(own_kernel, out_shape=[jax.ShapeDtypeStruct((OWN_PART, D),...  1.47 us
  transfers between devices with their start and end apart: 11, of which 2 were waited for; matrix products, arithmetic and copies ran while one was open for 0% of the time, Pallas kernels for 10%

profile of v8, /device:TPU:1, one launch (start us, length us, event | category | flops | bytes accessed | tf_op | source)
XLA Modules:
  0.0 66.6 jit_solution(6115169665008818050)
XLA Ops:
  0.0 1.5 %own.1 = (bf16[16,128]{1,0:T(8,128)(2,1)}, bf16[16,128]{1,0:T(8,128)(2,1)}, bf16[16,128]{1,0:T(8,128)(2,1)}, bf16[16,128]{1,0:T(8,128)(2,1)}) custom-call(bf16[64,64]{1,0:T(8,128)(2,1)} %constant.6.clone.own_order_ref, bf16[2,2,8,128]{3,2,1,0:T(8,128)(2,1)} %k_ref.1, bf16[2,2,8,128]{3,2,1,0:T(8,128)(2,1)} %v_ref.1), custom_call_target="tpu_custom_call" | custom-call | tf_op jit(solution)/shard_map/own/pallas_call | solution.py:334
  1.5 2.6 %collective-permute-start = (bf16[16,128]{1,0:T(8,128)(2,1)}, bf16[16,128]{1,0:T(8,128)(2,1)S(1)}, u32[]{:S(2)}, u32[]{:S(2)}) collective-permute-start(bf16[16,128]{1,0:T(8,128)(2,1)} %get-tuple-element.16), channel_id=1, source_target_pairs={{0,1},{1,2},{2,3},{3,0},{4,5},{5,6},{6,7},{7,4},{8,9},{9,10},{10,1... | collective-permute-start | bytes 12296 | tf_op jit(solution)/shard_map/ppermute | solution.py:317
  4.1 2.0 %collective-permute-start.1 = (bf16[16,128]{1,0:T(8,128)(2,1)}, bf16[16,128]{1,0:T(8,128)(2,1)S(1)}, u32[]{:S(2)}, u32[]{:S(2)}) collective-permute-start(bf16[16,128]{1,0:T(8,128)(2,1)} %get-tuple-element.17), channel_id=1, source_target_pairs={{0,2},{1,3},{2,0},{3,1},{4,6},{5,7},{6,4},{7,5},{8,10},{9,11},{10,... | collective-permute-start | bytes 12296 | tf_op jit(solution)/shard_map/ppermute | solution.py:317
  6.1 1.9 %message.1 = bf16[8,192,128]{2,1,0:T(8,128)(2,1)} custom-call(bf16[192,160]{1,0:T(8,128)(2,1)} %constant.7.clone.order_ref, bf16[2,2,40,128]{3,2,1,0:T(8,128)(2,1)} %q_ref.1), custom_call_target="tpu_custom_call" | custom-call | tf_op jit(solution)/shard_map/message/pallas_call | solution.py:343
  8.0 1.1 %collective-permute-done.2.refs_3_ = bf16[16,128]{1,0:T(8,128)(2,1)S(1)} collective-permute-done((bf16[16,128]{1,0:T(8,128)(2,1)S(1)}, bf16[16,128]{1,0:T(8,128)(2,1)S(1)}, u32[]{:S(2)}, u32[]{:S(2)}) %collective-permute-start.2) | collective-permute-done | bytes 4128 | tf_op jit(solution)/shard_map/ppermute | solution.py:317
  9.1 0.7 %copy-done.4 = s32[256]{0:T(256)S(1)} copy-done((s32[256]{0:T(256)S(1)}, s32[256]{0:T(256)}, u32[]{:S(2)}) %copy-start.4) | copy-done | bytes 1048
  9.8 0.1 pack.1.refs_0_
  9.9 1.1 %collective-permute-start.6 = (bf16[1104,128]{1,0:T(8,128)(2,1)S(1)}, bf16[1104,128]{1,0:T(8,128)(2,1)S(1)}, u32[]{:S(2)}, u32[]{:S(2)}) collective-permute-start(bf16[1104,128]{1,0:T(8,128)(2,1)S(1)} %pack.1.refs_0_), channel_id=1, source_target_pairs={{0,4},{4,0},{1,5},{5,1},{2,6},{6,2},{3,7},{7,3},{8,12},{12,8},{9,1... | collective-permute-start | bytes 847880 | tf_op jit(solution)/shard_map/ppermute | solution.py:317
  11.0 2.9 %collective-permute-start.5 = (bf16[1104,128]{1,0:T(8,128)(2,1)S(1)}, bf16[1104,128]{1,0:T(8,128)(2,1)S(1)}, u32[]{:S(2)}, u32[]{:S(2)}) collective-permute-start(bf16[1104,128]{1,0:T(8,128)(2,1)S(1)} %pack.1.refs_0_), channel_id=1, source_target_pairs={{0,16},{8,24},{16,0},{24,8},{1,17},{9,25},{17,1},{25,9},{2,18},{10... | collective-permute-start | bytes 847880 | tf_op jit(solution)/shard_map/ppermute | solution.py:317
  13.9 0.8 %collective-permute-start.4 = (bf16[1104,128]{1,0:T(8,128)(2,1)S(1)}, bf16[1104,128]{1,0:T(8,128)(2,1)S(1)}, u32[]{:S(2)}, u32[]{:S(2)}) collective-permute-start(bf16[1104,128]{1,0:T(8,128)(2,1)S(1)} %pack.1.refs_0_), channel_id=1, source_target_pairs={{0,24},{8,0},{16,8},{24,16},{1,25},{9,1},{17,9},{25,17},{2,26},{10... | collective-permute-start | bytes 847880 | tf_op jit(solution)/shard_map/ppermute | solution.py:317
  14.7 0.7 %collective-permute-start.3 = (bf16[1104,128]{1,0:T(8,128)(2,1)S(1)}, bf16[1104,128]{1,0:T(8,128)(2,1)S(1)}, u32[]{:S(2)}, u32[]{:S(2)}) collective-permute-start(bf16[1104,128]{1,0:T(8,128)(2,1)S(1)} %pack.1.refs_0_), channel_id=1, source_target_pairs={{0,8},{8,16},{16,24},{24,0},{1,9},{9,17},{17,25},{25,1},{2,10},{10... | collective-permute-start | bytes 847880 | tf_op jit(solution)/shard_map/ppermute | solution.py:317
  15.4 10.0 %all-to-all-start = ((bf16[32,48,128]{2,1,0:T(8,128)(2,1)}), bf16[32,48,128]{2,1,0:T(8,128)(2,1)S(1)}, u32[]{:S(2)}, u32[]{:S(2)}) async-start(bf16[32,48,128]{2,1,0:T(8,128)(2,1)} %bitcast.3), calls=%async_computation | async-start | bytes 786432 | tf_op jit(solution)/shard_map/all_to_all | solution.py:373
  25.4 0.0 collective-permute-done.6.refs_4_
  25.4 2.1 %collective-permute-start.8 = (bf16[1104,128]{1,0:T(8,128)(2,1)S(1)}, bf16[1104,128]{1,0:T(8,128)(2,1)S(1)}, u32[]{:S(2)}, u32[]{:S(2)}) collective-permute-start(bf16[1104,128]{1,0:T(8,128)(2,1)S(1)} %collective-permute-done.6.refs_4_), channel_id=1, source_target_pairs={{0,24},{8,0},{16,8},{24,16},{1,25},{9,1},{17,9},{25,17},{2,26},{10... | collective-permute-start | bytes 847880 | tf_op jit(solution)/shard_map/ppermute | solution.py:317
  27.5 0.0 collective-permute-done.5.refs_3_
  27.5 1.1 %collective-permute-start.9 = (bf16[1104,128]{1,0:T(8,128)(2,1)S(1)}, bf16[1104,128]{1,0:T(8,128)(2,1)S(1)}, u32[]{:S(2)}, u32[]{:S(2)}) collective-permute-start(bf16[1104,128]{1,0:T(8,128)(2,1)S(1)} %collective-permute-done.5.refs_3_), channel_id=1, source_target_pairs={{0,4},{4,0},{1,5},{5,1},{2,6},{6,2},{3,7},{7,3},{8,12},{12,8},{9,1... | collective-permute-start | bytes 847880 | tf_op jit(solution)/shard_map/ppermute | solution.py:317
  28.6 0.0 collective-permute-done.4.refs_2_
  28.6 0.6 hide.1
  29.2 9.9 %all-to-all-done = bf16[32,48,128]{2,1,0:T(8,128)(2,1)S(1)} async-done(((bf16[32,48,128]{2,1,0:T(8,128)(2,1)}), bf16[32,48,128]{2,1,0:T(8,128)(2,1)S(1)}, u32[]{:S(2)}, u32[]{:S(2)}) %all-to-all-start) | async-done | bytes 393248 | tf_op jit(solution)/shard_map/all_to_all | solution.py:373
  39.1 4.1 %attend_first.1 = (f32[2,2,128,384]{3,2,1,0:T(8,128)S(1)}, f32[2,2,8,384]{3,2,1,0:T(8,128)S(1)}) custom-call(f32[5,8,256]{2,1,0:T(8,128)S(1)} %get-tuple-element.22.hide_ref, bf16[32,2,24,128]{3,2,1,0:T(8,128)(2,1)S(1)} %bitcast.8, bf16[1104,128]{1,0:T(8,128)(2,1)S(1)} %pack.1.refs_0_, bf16[1104,128]{1,0:T(8,128)(2,1)S(1)} %collective-permute-done.3.refs_1_, ...), custom_call_target="tpu_custom_call" | custom-call | flops 1073741824 | bytes 2097152 | tf_op jit(solution)/shard_map/attend_first/pallas_call | solution.py:396
  43.3 3.9 %attend_second.1 = bf16[32,2,24,128]{3,2,1,0:T(8,128)(2,1)S(1)} custom-call(s32[2]{0:T(128)S(1)} %copy-done.6, bf16[32,2,24,128]{3,2,1,0:T(8,128)(2,1)S(1)} %bitcast.9, bf16[1104,128]{1,0:T(8,128)(2,1)S(1)} %pack.1.refs_0_, bf16[1104,128]{1,0:T(8,128)(2,1)S(1)} %collective-permute-done.3.refs_1_, bf16[1104,128]{1,0:T(8,128)(2,1)S(1)} %collective-permute-done.4.refs_2_, ...), custom_call_target="tpu_custom_call" | custom-call | flops 2147483648 | bytes 3145728 | tf_op jit(solution)/shard_map/attend_second/pallas_call | solution.py:409
  47.2 0.0 copy-start.2
  47.2 18.3 %all_to_all.10 = bf16[32,48,128]{2,1,0:T(8,128)(2,1)S(1)} all-to-all(bf16[32,48,128]{2,1,0:T(8,128)(2,1)S(1)} %bitcast.10), channel_id=1, replica_groups=mesh['zz'=4,'zc'=2,'y'=4,'xh'=2,'xl'=2,'c'=2] {'zz','zc','xl','c'}, dimensions={0} | all-to-all | bytes 786432 | tf_op jit(solution)/shard_map/all_to_all | solution.py:419
  65.5 1.1 %combine.1 = bf16[2,2,40,128]{3,2,1,0:T(8,128)(2,1)} custom-call(f32[160,128]{1,0:T(8,128)S(1)} %get-tuple-element.20.live_ref, bf16[160,192]{1,0:T(8,128)(2,1)S(1)} %copy-done.2, bf16[8,4,2,24,128]{4,3,2,1,0:T(8,128)(2,1)S(1)} %bitcast.7), custom_call_target="tpu_custom_call" | custom-call | tf_op jit(solution)/shard_map/combine/pallas_call | solution.py:420
  (22 shorter events, 0.0 us)
Async XLA Ops:
  1.5 4.6 %copy-start.7 = (bf16[16,128]{1,0:T(8,128)(2,1)S(1)}, bf16[16,128]{1,0:T(8,128)(2,1)}, u32[]{:S(2)}) copy-start(bf16[16,128]{1,0:T(8,128)(2,1)} %get-tuple-element.18) | copy-start | bytes 12292
  1.5 6.5 %collective-permute-start = (bf16[16,128]{1,0:T(8,128)(2,1)}, bf16[16,128]{1,0:T(8,128)(2,1)S(1)}, u32[]{:S(2)}, u32[]{:S(2)}) collective-permute-start(bf16[16,128]{1,0:T(8,128)(2,1)} %get-tuple-element.16), channel_id=1, source_target_pairs={{0,1},{1,2},{2,3},{3,0},{4,5},{5,6},{6,7},{7,4},{8,9},{9,10},{10,1... | collective-permute-start | bytes 12296 | tf_op jit(solution)/shard_map/ppermute | solution.py:317
  4.1 3.9 %collective-permute-start.1 = (bf16[16,128]{1,0:T(8,128)(2,1)}, bf16[16,128]{1,0:T(8,128)(2,1)S(1)}, u32[]{:S(2)}, u32[]{:S(2)}) collective-permute-start(bf16[16,128]{1,0:T(8,128)(2,1)} %get-tuple-element.17), channel_id=1, source_target_pairs={{0,2},{1,3},{2,0},{3,1},{4,6},{5,7},{6,4},{7,5},{8,10},{9,11},{10,... | collective-permute-start | bytes 12296 | tf_op jit(solution)/shard_map/ppermute | solution.py:317
  6.1 3.0 %copy-start = (bf16[256,2,128]{2,1,0:T(2,128)(2,1)S(1)}, bf16[256,2,128]{2,1,0:T(2,128)(2,1)}, u32[]{:S(2)}) copy-start(bf16[256,2,128]{2,1,0:T(2,128)(2,1)} %param.11) | copy-start | bytes 393220
  6.1 3.0 %copy-start.1 = (bf16[256,2,128]{2,1,0:T(2,128)(2,1)S(1)}, bf16[256,2,128]{2,1,0:T(2,128)(2,1)}, u32[]{:S(2)}) copy-start(bf16[256,2,128]{2,1,0:T(2,128)(2,1)} %param.12) | copy-start | bytes 393220
  6.1 3.0 %collective-permute-start.2 = (bf16[16,128]{1,0:T(8,128)(2,1)S(1)}, bf16[16,128]{1,0:T(8,128)(2,1)S(1)}, u32[]{:S(2)}, u32[]{:S(2)}) collective-permute-start(bf16[16,128]{1,0:T(8,128)(2,1)S(1)} %copy-done.7), channel_id=1, source_target_pairs={{0,3},{1,0},{2,1},{3,2},{4,7},{5,4},{6,5},{7,6},{8,11},{9,8},{10,9... | collective-permute-start | bytes 12296 | tf_op jit(solution)/shard_map/ppermute | solution.py:317
  7.9 1.2 %copy-start.3 = (bf16[16,128]{1,0:T(8,128)(2,1)S(1)}, bf16[16,128]{1,0:T(8,128)(2,1)}, u32[]{:S(2)}) copy-start(bf16[16,128]{1,0:T(8,128)(2,1)} %get-tuple-element.15.refs_0_) | copy-start | bytes 12292
  9.1 0.7 %copy-start.4 = (s32[256]{0:T(256)S(1)}, s32[256]{0:T(256)}, u32[]{:S(2)}) copy-start(s32[256]{0:T(256)} %param.13) | copy-start | bytes 3076
  9.9 15.5 %collective-permute-start.6 = (bf16[1104,128]{1,0:T(8,128)(2,1)S(1)}, bf16[1104,128]{1,0:T(8,128)(2,1)S(1)}, u32[]{:S(2)}, u32[]{:S(2)}) collective-permute-start(bf16[1104,128]{1,0:T(8,128)(2,1)S(1)} %pack.1.refs_0_), channel_id=1, source_target_pairs={{0,4},{4,0},{1,5},{5,1},{2,6},{6,2},{3,7},{7,3},{8,12},{12,8},{9,1... | collective-permute-start | bytes 847880 | tf_op jit(solution)/shard_map/ppermute | solution.py:317
  11.0 16.5 %collective-permute-start.5 = (bf16[1104,128]{1,0:T(8,128)(2,1)S(1)}, bf16[1104,128]{1,0:T(8,128)(2,1)S(1)}, u32[]{:S(2)}, u32[]{:S(2)}) collective-permute-start(bf16[1104,128]{1,0:T(8,128)(2,1)S(1)} %pack.1.refs_0_), channel_id=1, source_target_pairs={{0,16},{8,24},{16,0},{24,8},{1,17},{9,25},{17,1},{25,9},{2,18},{10... | collective-permute-start | bytes 847880 | tf_op jit(solution)/shard_map/ppermute | solution.py:317
  13.9 14.7 %collective-permute-start.4 = (bf16[1104,128]{1,0:T(8,128)(2,1)S(1)}, bf16[1104,128]{1,0:T(8,128)(2,1)S(1)}, u32[]{:S(2)}, u32[]{:S(2)}) collective-permute-start(bf16[1104,128]{1,0:T(8,128)(2,1)S(1)} %pack.1.refs_0_), channel_id=1, source_target_pairs={{0,24},{8,0},{16,8},{24,16},{1,25},{9,1},{17,9},{25,17},{2,26},{10... | collective-permute-start | bytes 847880 | tf_op jit(solution)/shard_map/ppermute | solution.py:317
  14.7 13.9 %collective-permute-start.3 = (bf16[1104,128]{1,0:T(8,128)(2,1)S(1)}, bf16[1104,128]{1,0:T(8,128)(2,1)S(1)}, u32[]{:S(2)}, u32[]{:S(2)}) collective-permute-start(bf16[1104,128]{1,0:T(8,128)(2,1)S(1)} %pack.1.refs_0_), channel_id=1, source_target_pairs={{0,8},{8,16},{16,24},{24,0},{1,9},{9,17},{17,25},{25,1},{2,10},{10... | collective-permute-start | bytes 847880 | tf_op jit(solution)/shard_map/ppermute | solution.py:317
  15.3 13.3 %copy-start.5 = (s32[2]{0:T(128)S(1)}, s32[2]{0:T(128)}, u32[]{:S(2)}) copy-start(s32[2]{0:T(128)} %lengths_ref.1) | copy-start | bytes 28
  15.4 13.3 %copy-start.6 = (s32[2]{0:T(128)S(1)}, s32[2]{0:T(128)}, u32[]{:S(2)}) copy-start(s32[2]{0:T(128)} %reach_ref.3) | copy-start | bytes 28
  15.4 23.8 %all-to-all-start = ((bf16[32,48,128]{2,1,0:T(8,128)(2,1)}), bf16[32,48,128]{2,1,0:T(8,128)(2,1)S(1)}, u32[]{:S(2)}, u32[]{:S(2)}) async-start(bf16[32,48,128]{2,1,0:T(8,128)(2,1)} %bitcast.3), calls=%async_computation | async-start | bytes 786432 | tf_op jit(solution)/shard_map/all_to_all | solution.py:373
  25.4 17.8 %collective-permute-start.8 = (bf16[1104,128]{1,0:T(8,128)(2,1)S(1)}, bf16[1104,128]{1,0:T(8,128)(2,1)S(1)}, u32[]{:S(2)}, u32[]{:S(2)}) collective-permute-start(bf16[1104,128]{1,0:T(8,128)(2,1)S(1)} %collective-permute-done.6.refs_4_), channel_id=1, source_target_pairs={{0,24},{8,0},{16,8},{24,16},{1,25},{9,1},{17,9},{25,17},{2,26},{10... | collective-permute-start | bytes 847880 | tf_op jit(solution)/shard_map/ppermute | solution.py:317
  27.5 15.8 %collective-permute-start.7 = (bf16[1104,128]{1,0:T(8,128)(2,1)S(1)}, bf16[1104,128]{1,0:T(8,128)(2,1)S(1)}, u32[]{:S(2)}, u32[]{:S(2)}) collective-permute-start(bf16[1104,128]{1,0:T(8,128)(2,1)S(1)} %collective-permute-done.6.refs_4_), channel_id=1, source_target_pairs={{0,8},{8,16},{16,24},{24,0},{1,9},{9,17},{17,25},{25,1},{2,10},{10... | collective-permute-start | bytes 847880 | tf_op jit(solution)/shard_map/ppermute | solution.py:317
  27.5 15.8 %collective-permute-start.9 = (bf16[1104,128]{1,0:T(8,128)(2,1)S(1)}, bf16[1104,128]{1,0:T(8,128)(2,1)S(1)}, u32[]{:S(2)}, u32[]{:S(2)}) collective-permute-start(bf16[1104,128]{1,0:T(8,128)(2,1)S(1)} %collective-permute-done.5.refs_3_), channel_id=1, source_target_pairs={{0,4},{4,0},{1,5},{5,1},{2,6},{6,2},{3,7},{7,3},{8,12},{12,8},{9,1... | collective-permute-start | bytes 847880 | tf_op jit(solution)/shard_map/ppermute | solution.py:317
  47.2 18.4 %copy-start.2 = (bf16[160,192]{1,0:T(8,128)(2,1)S(1)}, bf16[160,192]{1,0:T(8,128)(2,1)}, u32[]{:S(2)}) copy-start(bf16[160,192]{1,0:T(8,128)(2,1)} %constant.8.clone.order_ref) | copy-start | bytes 184324
